TPU v7x, 256 devices: a whole 4x4x8 slice. The times are simulated.
256 devices in a mesh: blk: 64 (over y, x, z_lo), head: 4 (over z_hi, core).
Axes of the slice: x: 4, y: 4, z: 8 (z_hi: 2, z_lo: 4; z = z_hi * 4 + z_lo), core: 2. Of those that a mesh axis runs over, the one named last changes fastest.
Arguments:
- hidden_in: bfloat16 [32768, 2048], P('blk'), may hold values from -6 to 6
- layer_input: bfloat16 [32768, 256], P(('blk', 'head')), may hold values from -6 to 6
- in_gain: float32 [2048], replicated, may hold values from 0.5 to 1.5
- w_query: bfloat16 [2048, 2048], P(None, 'head'), may hold values from -0.125 to 0.125
- w_keyval: bfloat16 [2048, 1024], P(None, 'head'), may hold values from -0.125 to 0.125
- q_gain: float32 [256], replicated, may hold values from 0.2 to 0.45
- k_gain: float32 [256], replicated, may hold values from 0.2 to 0.45
- w_out: bfloat16 [2048, 2048], P('head'), may hold values from -0.125 to 0.125
- post_gain: float32 [2048], replicated, may hold values from 0.5 to 1.5
- laurel_left: bfloat16 [2048, 64], replicated, may hold values from -0.125 to 0.125
- laurel_right: bfloat16 [64, 2048], replicated, may hold values from -0.75 to 0.75
- laurel_gain: float32 [2048], replicated, may hold values from 0.5 to 1.5
- w_plgate: bfloat16 [2048, 256], replicated, may hold values from -0.125 to 0.125
- w_plproj: bfloat16 [256, 2048], replicated, may hold values from -0.375 to 0.375
- pl_gain: float32 [2048], replicated, may hold values from 0.5 to 1.5
- kv_pool: bfloat16 [768, 4, 128, 256], P('blk'), may hold values from -44 to 44, as said below
- page_table: int32 [64, 12], P('blk'), may hold values from 0 to 11, each once within a row
- prefix_len: int32 [64], P('blk'), may hold values from 1 to 1536, as said below
- decode_owner: int32 [64], replicated, may hold values from 0 to 63, each once
Outputs:
- mixed: bfloat16 [32768, 2048], P(('blk', 'head'))
- decode_kv: bfloat16 [4, 64, 2048, 256], P('head', 'blk')
Inputs may be any that keep to these rules, and one draw needn't show every extreme that they name: `kv_pool`: cached keys and values; one request's prefix fills its 12 pages in every draw. `page_table`: each row names each of its 12 pool pages once. `prefix_len`: some request has exactly 1536 cached tokens. `decode_owner`: each request has its own slot.
All inputs are finite; a program needn't handle non-finite values.
Results may differ from a plain program's by a relative error of at most 0.009.
Values may be sent and summed in bfloat16 or wider, within the bound.
No kernel may reach another device: no remote copies, remote signals or barrier semaphores. Data moves between devices by JAX's collectives and lax.ppermute only.
A program may use at most 128 MiB of HBM per device.

v0:
```python
import jax
import jax.numpy as jnp
from jax import lax
from jax.sharding import PartitionSpec as P

QH = 8
KVH = 2


eps = 1e-06
rope_base = 1000000.0


def rms_scale(values):
    return values * lax.rsqrt(jnp.mean(values * values, axis=-1, keepdims=True) + eps)


def rotate(values, positions):
    half_dim = values.shape[-1] // 2
    frequency = rope_base ** (-jnp.arange(half_dim, dtype=jnp.float32) / half_dim)
    angles = positions.astype(jnp.float32)[:, None] * frequency[None, :]
    cosine = jnp.cos(angles)
    sine_part = jnp.sin(angles)
    lower_half = values[..., :half_dim]
    upper_half = values[..., half_dim:]
    return jnp.concatenate(
        [
            lower_half * cosine - upper_half * sine_part,
            upper_half * cosine + lower_half * sine_part,
        ],
        axis=-1,
    )


def scores_of(rows, keys):
    return lax.dot_general(rows, keys, (((1,), (1,)), ((), ())), preferred_element_type=jnp.float32)


def on_device(
    hidden_in,
    layer_input,
    in_gain,
    w_query,
    w_keyval,
    q_gain,
    k_gain,
    w_out,
    post_gain,
    laurel_left,
    laurel_right,
    laurel_gain,
    w_plgate,
    w_plproj,
    pl_gain,
    kv_pool,
    page_table,
    prefix_len,
    decode_owner,
):
    new_rows = hidden_in.shape[0]
    head_dim = kv_pool.shape[3]
    page_len = kv_pool.shape[2]
    n_pages = page_table.shape[1]
    kv_heads = kv_pool.shape[1] // 2
    local_heads = w_query.shape[1] // head_dim
    prefix_max = n_pages * page_len
    total_len = prefix_max + new_rows
    blocks = lax.axis_size("blk")
    block_span = total_len // blocks
    head_idx = lax.axis_index("head")
    kv_of = head_idx * local_heads // (QH // KVH)
    length = prefix_len[0]
    positions = length + jnp.arange(new_rows, dtype=jnp.int32)
    my_pages = jnp.take(kv_pool, page_table[0], axis=0)
    live_mask = jnp.arange(prefix_max, dtype=jnp.int32) < length
    own_old = lax.dynamic_index_in_dim(my_pages, head_idx, 1, keepdims=False).reshape(
        prefix_max, head_dim
    )
    own_old = jnp.where(live_mask[:, None], own_old, jnp.zeros_like(own_old))
    old_part = jnp.concatenate([own_old, jnp.zeros((new_rows, head_dim), jnp.bfloat16)], axis=0)
    normed = (rms_scale(hidden_in.astype(jnp.float32)) * in_gain).astype(jnp.bfloat16)
    queries = jnp.dot(normed, w_query, preferred_element_type=jnp.float32).reshape(
        new_rows, local_heads, head_dim
    )
    queries = rotate(jnp.transpose(rms_scale(queries) * q_gain, (1, 0, 2)), positions).astype(
        jnp.bfloat16
    )
    own_proj = rms_scale(jnp.dot(normed, w_keyval, preferred_element_type=jnp.float32))
    fresh_slot = jnp.where(
        head_idx < kv_heads, rotate(own_proj * k_gain, positions), own_proj
    ).astype(jnp.bfloat16)
    gathered = lax.all_gather(fresh_slot[None], "head", axis=0, tiled=True)
    new_key = lax.dynamic_index_in_dim(gathered, kv_of, 0, keepdims=False)
    new_val = lax.dynamic_index_in_dim(gathered, kv_of + kv_heads, 0, keepdims=False)
    pre_key = lax.dynamic_index_in_dim(my_pages, kv_of, 1, keepdims=False).reshape(
        prefix_max, head_dim
    )
    pre_val = lax.dynamic_index_in_dim(my_pages, kv_of + kv_heads, 1, keepdims=False).reshape(
        prefix_max, head_dim
    )
    flat_q = queries.reshape(local_heads * new_rows, head_dim)
    row_pos = jnp.tile(jnp.arange(new_rows, dtype=jnp.int32), local_heads)
    causal = jnp.arange(new_rows, dtype=jnp.int32)[None, :] <= row_pos[:, None]
    new_scores = jnp.where(causal, scores_of(flat_q, new_key), -jnp.inf)
    old_scores = jnp.where(live_mask[None, :], scores_of(flat_q, pre_key), -jnp.inf)
    row_top = jnp.maximum(jnp.max(old_scores, axis=1), jnp.max(new_scores, axis=1))
    old_exp = jnp.exp(old_scores - row_top[:, None])
    new_exp = jnp.exp(new_scores - row_top[:, None])
    row_total = jnp.sum(old_exp, axis=1) + jnp.sum(new_exp, axis=1)
    weighted = jnp.dot(old_exp.astype(jnp.bfloat16), pre_val, preferred_element_type=jnp.float32)
    weighted = weighted + jnp.dot(
        new_exp.astype(jnp.bfloat16), new_val, preferred_element_type=jnp.float32
    )
    attn = (
        (weighted / row_total[:, None])
        .astype(jnp.bfloat16)
        .reshape(local_heads, new_rows, head_dim)
    )
    attn = jnp.transpose(attn, (1, 0, 2)).reshape(new_rows, local_heads * head_dim)
    quarter = new_rows // lax.axis_size("head")
    row_start = head_idx * quarter
    proj_rows = lax.psum_scatter(
        jnp.dot(attn, w_out, preferred_element_type=jnp.float32).astype(jnp.bfloat16),
        "head",
        scatter_dimension=0,
        tiled=True,
    ).astype(jnp.float32)
    tokens_rows = lax.dynamic_slice_in_dim(hidden_in, row_start, quarter, 0).astype(jnp.float32)
    normed_rows = lax.dynamic_slice_in_dim(normed, row_start, quarter, 0)
    branch_low = jnp.dot(normed_rows, laurel_left, preferred_element_type=jnp.float32).astype(
        jnp.bfloat16
    )
    laurel = (
        normed_rows.astype(jnp.float32)
        + rms_scale(jnp.dot(branch_low, laurel_right, preferred_element_type=jnp.float32))
        * laurel_gain
    )
    state = (tokens_rows + rms_scale(proj_rows) * post_gain + laurel) * 2.0 ** (-0.5)
    state_b = state.astype(jnp.bfloat16)
    gated = (
        jax.nn.gelu(
            jnp.dot(state_b, w_plgate, preferred_element_type=jnp.float32), approximate=True
        )
        * layer_input.astype(jnp.float32)
    ).astype(jnp.bfloat16)
    mixed = (
        state + rms_scale(jnp.dot(gated, w_plproj, preferred_element_type=jnp.float32)) * pl_gain
    ).astype(jnp.bfloat16)
    full_seq = lax.dynamic_update_slice(old_part, fresh_slot, (length, jnp.int32(0)))
    spread = lax.all_to_all(
        full_seq.reshape(blocks, block_span, head_dim),
        "blk",
        split_axis=0,
        concat_axis=0,
        tiled=True,
    )
    inverse = (
        jnp.zeros((blocks,), jnp.int32).at[decode_owner].set(jnp.arange(blocks, dtype=jnp.int32))
    )
    arranged = jnp.take(spread, inverse, axis=0)
    owned = lax.all_to_all(arranged, "blk", split_axis=0, concat_axis=0, tiled=True)
    return (mixed, owned.reshape(1, 1, total_len, head_dim))


def solution(mesh):
    in_specs = (
        P("blk", None),
        P(("blk", "head"), None),
        P(),
        P(None, "head"),
        P(None, "head"),
        P(),
        P(),
        P("head", None),
        P(),
        P(),
        P(),
        P(),
        P(),
        P(),
        P(),
        P("blk", None, None, None),
        P("blk", None),
        P("blk"),
        P(),
    )
    out_specs = (P(("blk", "head"), None), P("head", "blk", None, None))
    return jax.shard_map(
        on_device, mesh=mesh, in_specs=in_specs, out_specs=out_specs, check_vma=False
    )
```

profile of v0, /device:TPU:1, one launch (start us, length us, event | category | flops | bytes accessed | tf_op | source)
XLA Modules:
  0.0 160.5 jit_solution(11719426284139527065)
XLA Ops:
  7.2 0.0 copy-start
  7.2 0.0 copy-start.13
  7.2 0.0 all-gather.3.cloned.1.call-start
  7.3 0.0 copy-start.2
  8.1 2.2 %fusion.2 = f32[512]{0:T(512)S(1)} fusion(bf16[512,2048]{1,0:T(8,128)(2,1)} %param.19), kind=kLoop, calls=%fused_computation.9 | loop fusion | flops 3145216 | bytes 2099200 | tf_op jit(solution)/shard_map/reduce_sum | solution.py:15
  10.3 0.0 copy-done.13
  10.3 0.0 copy-done.2
  10.3 0.0 copy-start.17
  10.3 0.5 fusion.4
  10.9 0.0 copy-start.3
  10.9 1.3 copy-done.3
  12.2 0.0 copy-done.17
  12.3 1.5 multiply_reduce_fusion.3
  13.8 0.0 copy-done.15
  13.8 1.2 multiply_multiply_fusion
  15.0 1.2 multiply_subtract_fusion
  16.2 0.0 copy-done.6
  16.2 0.8 fusion.26
  17.1 0.0 all-gather.3.cloned.1.call-update
  17.1 0.0 copy-done.18
  17.2 0.0 copy-done
  17.2 2.5 %gather_fusion = bf16[12,4,128,256]{3,2,1,0:T(8,128)(2,1)} fusion(bf16[12,4,128,256]{3,2,1,0:T(8,128)(2,1)S(1)} %copy-done, s32[1024]{0:T(1024)S(1)} %pad_clamp_fusion.1), kind=kCustom, calls=%fused_computation | custom fusion | bytes 6291504 | tf_op jit(solution)/shard_map/jit(_take)/gather | solution.py:74
  19.7 3.9 %broadcast_select_fusion = bf16[12,4,128,256]{3,2,1,0:T(8,128)(2,1)} fusion(bf16[12,4,128,256]{3,2,1,0:T(8,128)(2,1)} %gather_fusion, pred[12]{0:T(512)(128)(4,1)S(1)} %compare_and_fusion.1), kind=kLoop, calls=%fused_computation.15 | loop fusion | flops 1572864 | bytes 6291468 | tf_op jit(solution)/shard_map/jit(_take)/select_n | solution.py:74
  23.6 2.9 %constant_dynamic-slice_fusion = (bf16[12,1,128,256]{3,2,1,0:T(8,128)(2,1)S(1)}, bf16[12,1,128,256]{3,2,1,0:T(8,128)(2,1)}, bf16[12,1,128,256]{3,2,1,0:T(8,128)(2,1)}) fusion(bf16[12,4,128,256]{3,2,1,0:T(8,128)(2,1)} %broadcast_select_fusion, s32[]{:T(128)S(6)} %select_n.90, s32[]{:T(128)S(6)} %select_n.87, s32[]{:T(128)S(6)} %select_n.82), kind=kLoop, calls=%fused_computation.96 | loop fusion | bytes 4718604 | tf_op jit(solution)/shard_map/jit(dynamic_index_in_dim)/dynamic_slice | solution.py:76
  26.5 0.3 bitcast_select_fusion
  26.8 1.0 concatenate.19
  27.9 0.0 copy-done.5
  27.9 2.8 %dynamic_update_slice.3 = bf16[2048,256]{1,0:T(8,128)(2,1)} dynamic-update-slice(bf16[2048,256]{1,0:T(8,128)(2,1)} %concatenate.19, bf16[512,256]{1,0:T(8,128)(2,1)S(1)} %copy-done.5, s32[]{:T(128)S(6)} %select_n.92, s32[]{:T(128)} %constant.53.clone.1) | dynamic-update-slice | bytes 524292 | tf_op jit(solution)/shard_map/dynamic_update_slice | solution.py:149
  30.7 12.8 %all-to-all-start = ((bf16[64,32,256]{2,1,0:T(8,128)(2,1)}), bf16[64,32,256]{2,1,0:T(8,128)(2,1)}, u32[]{:S(2)}, u32[]{:S(2)}) async-start(bf16[64,32,256]{2,1,0:T(8,128)(2,1)} %bitcast.52), calls=%async_computation.1 | async-start | bytes 2097152 | tf_op jit(solution)/shard_map/all_to_all | solution.py:150
  43.5 0.2 reduce-scatter.2.cloned.1.call-start
  43.7 4.5 %multiply_reduce_fusion.2 = (f32[512,2]{0,1:T(2,128)S(1)}, f32[512,512]{0,1:T(8,128)}) fusion(bf16[512,2048]{1,0:T(8,128)(2,1)} %copy-done.3, bf16[2048,512]{1,0:T(8,128)(2,1)} %param.22), kind=kOutput, calls=%fused_computation.43 | convolution fusion | flops 1074265088 | bytes 5246976 | tf_op jit(solution)/shard_map/dot_general | solution.py:82
  48.2 2.5 %copy.23 = f32[512,2,256]{2,0,1:T(8,128)} copy(f32[512,2,256]{0,2,1:T(8,128)} %bitcast.54) | data formatting | bytes 2097152 | tf_op jit(solution)/shard_map/reshape | solution.py:82
  50.8 1.0 multiply_cosine_fusion
  51.8 0.0 copy-done.16
  51.8 0.0 copy-start.4
  51.8 1.5 multiply_bitcast_fusion
  53.3 0.1 subtract_convert_fusion
  53.4 0.0 copy-start.7
  53.5 0.7 copy-done.7
  54.1 0.0 copy-done.4
  54.1 3.7 %select_reduce_fusion = (f32[1024]{0:T(1024)S(1)}, f32[1024,1536]{1,0:T(8,128)}) fusion(pred[1536]{0:T(1024)(128)(4,1)S(1)} %iota_compare_fusion.1, bf16[1536,256]{1,0:T(8,128)(2,1)S(1)} %bitcast.53, bf16[1024,128]{1,0:T(8,128)(2,1)S(1)} %bitcast.57, bf16[1024,128]{1,0:T(8,128)(2,1)S(1)} %bitcast.55), kind=kOutput, calls=%fused_computation.4 | convolution fusion | flops 809499648 | bytes 7607808 | tf_op jit(solution)/shard_map/dot_general | solution.py:36
  57.8 1.6 fusion.11
  59.4 0.0 copy-start.1
  59.4 4.1 %fusion = f32[1024]{0:T(1024)S(1)} fusion(f32[1024,1536]{1,0:T(8,128)} %get-tuple-element.14, f32[1024]{0:T(1024)S(1)} %max.7, pred[1536]{0:T(1024)(128)(4,1)S(1)} %iota_compare_fusion.1), kind=kLoop, calls=%fused_computation.7 | loop fusion | flops 4717568 | bytes 6301184 | tf_op jit(solution)/shard_map/reduce_sum | solution.py:109
  63.5 0.5 copy-done.1
  64.0 1.2 fusion.5
  65.2 0.5 fusion.12
  65.7 2.5 %fusion.15 = bf16[1024,256]{1,0:T(8,128)(2,1)} fusion(f32[1024,256]{1,0:T(8,128)S(1)} %fusion.5, f32[1024,512]{0,1:T(8,128)S(1)} %get-tuple-element.18, f32[1024]{0:T(1024)S(1)} %max.7, s32[1024]{0:T(1024)S(1)} %bitcast.64, f32[1024]{0:T(1024)S(1)} %add.171, bf16[4,512,256]{2,1,0:T(8,128)(2,1)} %bitcast.66, s32[]{:T(128)S(6)} %select_n.87), kind=kOutput, calls=%fused_computation.28 | convolution fusion | flops 271319040 | bytes 3944452 | tf_op jit(solution)/shard_map/dot_general | solution.py:111
  68.1 2.0 %copy.24 = bf16[2,512,256]{1,2,0:T(8,128)(2,1)} copy(bf16[2,512,256]{2,1,0:T(8,128)(2,1)} %bitcast.60) | data formatting | bytes 1048576 | tf_op jit(solution)/shard_map/reshape | solution.py:117
  70.2 4.4 %convolution_convert_fusion = bf16[512,2048]{1,0:T(8,128)(2,1)} fusion(bf16[512,512]{0,1:T(8,128)(2,1)} %bitcast.61, bf16[512,2048]{1,0:T(8,128)(2,1)} %param.26), kind=kOutput, calls=%fused_computation.17 | convolution fusion | flops 1074790400 | bytes 4718592 | tf_op jit(solution)/shard_map/dot_general | solution.py:123
  74.6 0.0 reduce-scatter.2.cloned.1.call-update
  74.6 0.6 copy-done.19
  75.2 0.8 scatter_custom_fusion
  76.1 0.0 all-to-all-done
  76.1 2.8 %gather_fusion.1 = bf16[64,32,256]{2,1,0:T(8,128)(2,1)} fusion(bf16[64,32,256]{2,1,0:T(8,128)(2,1)} %all-to-all-done, s32[1024]{0:T(1024)S(1)} %pad_clamp_fusion), kind=kCustom, calls=%fused_computation.1 | custom fusion | bytes 2097408 | tf_op jit(solution)/shard_map/jit(_take)/gather | solution.py:160
  78.9 2.4 %broadcast_select_fusion.1 = bf16[64,32,256]{2,1,0:T(8,128)(2,1)} fusion(bf16[64,32,256]{2,1,0:T(8,128)(2,1)} %gather_fusion.1, pred[64]{0:T(512)(128)(4,1)S(1)} %compare_and_fusion), kind=kLoop, calls=%fused_computation.44 | loop fusion | flops 524288 | bytes 2097216 | tf_op jit(solution)/shard_map/jit(_take)/select_n | solution.py:160
  81.3 10.6 %all-to-all-start.1 = ((bf16[64,32,256]{2,1,0:T(8,128)(2,1)}), bf16[64,32,256]{2,1,0:T(8,128)(2,1)}, u32[]{:S(2)}, u32[]{:S(2)}) async-start(bf16[64,32,256]{2,1,0:T(8,128)(2,1)} %broadcast_select_fusion.1), calls=%async_computation.2 | async-start | bytes 2097152 | tf_op jit(solution)/shard_map/all_to_all | solution.py:161
  91.9 2.8 %multiply_reduce_fusion.1 = (f32[128]{0:T(128)S(1)}, f32[128,2048]{1,0:T(8,128)}) fusion(bf16[64,2048]{1,0:T(8,128)(2,1)S(1)} %copy-done.9, bf16[2048,64]{0,1:T(8,128)(2,1)} %param.28, bf16[512,2048]{1,0:T(8,128)(2,1)} %copy-done.3, s32[]{:T(128)S(6)} %select_n.77), kind=kOutput, calls=%fused_computation.38 | convolution fusion | flops 67641216 | bytes 2097668 | tf_op jit(solution)/shard_map/dot_general | solution.py:135
  94.8 47.7 %all-to-all-done.1 = bf16[64,32,256]{2,1,0:T(8,128)(2,1)} async-done(((bf16[64,32,256]{2,1,0:T(8,128)(2,1)}), bf16[64,32,256]{2,1,0:T(8,128)(2,1)}, u32[]{:S(2)}, u32[]{:S(2)}) %all-to-all-start.1) | async-done | bytes 1048608 | tf_op jit(solution)/shard_map/all_to_all | solution.py:161
  142.4 1.2 fusion.17
  143.7 0.0 copy-start.14
  143.7 4.3 %multiply_reduce_fusion = (f32[128]{0:T(128)S(1)}, f32[128,2048]{1,0:T(8,128)}) fusion(bf16[256,2048]{1,0:T(8,128)(2,1)} %param.32, bf16[2048,256]{1,0:T(8,128)(2,1)} %param.31, bf16[128,256]{1,0:T(8,128)(2,1)S(1)} %copy-done.10, bf16[128,2048]{1,0:T(8,128)(2,1)} %reduce-scatter.2.cloned.1.call-done, f32[128,2048]{1,0:T(8,128)} %get-tuple-element.20, ...), kind=kOutput, calls=%fused_computation.37 | convolution fusion | flops 272465792 | bytes 5850628 | tf_op jit(solution)/shard_map/dot_general | solution.py:147
  148.0 3.4 %add_convert_fusion = bf16[128,2048]{1,0:T(8,128)(2,1)} fusion(f32[128,2048]{1,0:T(8,128)} %get-tuple-element.22, f32[2048]{0:T(1024)S(1)} %copy-done.14, f32[128]{0:T(128)S(1)} %add_rsqrt_fusion.3, f32[2048]{0:T(1024)S(1)} %copy-done.11, f32[128,2048]{1,0:T(8,128)} %get-tuple-element.20, f32[128]{0:T(128)S(1)} %add_rsqrt_fusion.4, ...), kind=kLoop, calls=%fused_computation.36 | loop fusion | flops 3932160 | bytes 4220420 | tf_op jit(solution)/shard_map/convert_element_type | solution.py:148
  151.4 2.3 %copy.29 = bf16[1,1,2048,256]{3,2,1,0:T(8,128)(2,1)} copy(bf16[1,1,2048,256]{3,2,1,0:T(8,128)(2,1)} %bitcast.18) | data formatting | bytes 2097152
  (40 shorter events, 0.2 us)
Async XLA Ops:
  7.2 10.0 %copy-start = (bf16[12,4,128,256]{3,2,1,0:T(8,128)(2,1)S(1)}, bf16[12,4,128,256]{3,2,1,0:T(8,128)(2,1)}, u32[]{:S(2)}) copy-start(bf16[12,4,128,256]{3,2,1,0:T(8,128)(2,1)} %param.34) | copy-start | bytes 9437188
  7.2 3.1 %copy-start.13 = (f32[2048]{0:T(1024)S(1)}, f32[2048]{0:T(1024)}, u32[]{:S(2)}) copy-start(f32[2048]{0:T(1024)} %param.21) | copy-start | bytes 24580
  7.2 50.6 %all-gather.3.cloned.1.call-start = ((), (), s32[]{:S(2)}) async-start(), calls=%async_computation.4 | async-start | bytes 1310720 | tf_op jit(solution)/shard_map/all_gather | solution.py:92
  7.3 3.1 %copy-start.2 = (bf16[512,2048]{1,0:T(8,128)(2,1)S(1)}, bf16[512,2048]{1,0:T(8,128)(2,1)}, u32[]{:S(2)}) copy-start(bf16[512,2048]{1,0:T(8,128)(2,1)} %param.19) | copy-start | bytes 6291460
  10.3 1.9 %copy-start.17 = (bf16[2048,256]{1,0:T(8,128)(2,1)S(1)}, bf16[2048,256]{1,0:T(8,128)(2,1)}, u32[]{:S(2)}) copy-start(bf16[2048,256]{1,0:T(8,128)(2,1)} %param.23) | copy-start | bytes 3145732
  10.9 1.4 copy-start.3
  12.3 1.5 copy-start.15
  13.8 3.3 %copy-start.18 = (s32[1,12]{1,0:T(1,128)S(1)}, s32[1,12]{1,0:T(1,128)}, u32[]{:S(2)}) copy-start(s32[1,12]{1,0:T(1,128)} %param.35) | copy-start | bytes 148
  13.8 2.5 %copy-start.6 = (f32[512,256]{1,0:T(8,128)S(1)}, f32[512,256]{1,0:T(8,128)}, u32[]{:S(2)}) copy-start(f32[512,256]{1,0:T(8,128)} %get-tuple-element.16) | copy-start | bytes 1572868
  26.5 1.3 copy-start.5
  30.7 45.4 %all-to-all-start = ((bf16[64,32,256]{2,1,0:T(8,128)(2,1)}), bf16[64,32,256]{2,1,0:T(8,128)(2,1)}, u32[]{:S(2)}, u32[]{:S(2)}) async-start(bf16[64,32,256]{2,1,0:T(8,128)(2,1)} %bitcast.52), calls=%async_computation.1 | async-start | bytes 2097152 | tf_op jit(solution)/shard_map/all_to_all | solution.py:150
  43.5 99.0 %reduce-scatter.2.cloned.1.call-start = ((), (), s32[]{:S(2)}) async-start(), calls=%async_computation.3 | async-start | bytes 2621440 | tf_op jit(solution)/shard_map/reduce_scatter | solution.py:122
  48.2 3.6 %copy-start.16 = (f32[256]{0:T(256)S(1)}, f32[256]{0:T(256)}, u32[]{:S(2)}) copy-start(f32[256]{0:T(256)} %param.24) | copy-start | bytes 3076
  51.8 2.4 %copy-start.4 = (bf16[12,1,128,256]{3,2,1,0:T(8,128)(2,1)S(1)}, bf16[12,1,128,256]{3,2,1,0:T(8,128)(2,1)}, u32[]{:S(2)}) copy-start(bf16[12,1,128,256]{3,2,1,0:T(8,128)(2,1)} %get-tuple-element.4) | copy-start | bytes 2359300
  53.4 0.7 copy-start.7
  57.8 5.7 %copy-start.8 = (bf16[12,1,128,256]{3,2,1,0:T(8,128)(2,1)S(1)}, bf16[12,1,128,256]{3,2,1,0:T(8,128)(2,1)}, u32[]{:S(2)}) copy-start(bf16[12,1,128,256]{3,2,1,0:T(8,128)(2,1)} %get-tuple-element.3) | copy-start | bytes 2359300
  59.4 4.6 %copy-start.1 = (f32[1024,1536]{1,0:T(8,128)S(1)}, f32[1024,1536]{1,0:T(8,128)}, u32[]{:S(2)}) copy-start(f32[1024,1536]{1,0:T(8,128)} %get-tuple-element.14) | copy-start | bytes 18874372
  74.6 0.7 copy-start.19
  78.9 13.0 %copy-start.9 = (bf16[64,2048]{1,0:T(8,128)(2,1)S(1)}, bf16[64,2048]{1,0:T(8,128)(2,1)}, u32[]{:S(2)}) copy-start(bf16[64,2048]{1,0:T(8,128)(2,1)} %param.29) | copy-start | bytes 786436
  81.3 62.4 %copy-start.10 = (bf16[128,256]{1,0:T(8,128)(2,1)S(1)}, bf16[128,256]{1,0:T(8,128)(2,1)}, u32[]{:S(2)}) copy-start(bf16[128,256]{1,0:T(8,128)(2,1)} %param.20) | copy-start | bytes 196612
  81.3 62.4 %copy-start.11 = (f32[2048]{0:T(1024)S(1)}, f32[2048]{0:T(1024)}, u32[]{:S(2)}) copy-start(f32[2048]{0:T(1024)} %param.30) | copy-start | bytes 24580
  81.3 62.4 %copy-start.12 = (f32[2048]{0:T(1024)S(1)}, f32[2048]{0:T(1024)}, u32[]{:S(2)}) copy-start(f32[2048]{0:T(1024)} %param.27) | copy-start | bytes 24580
  81.3 61.1 %all-to-all-start.1 = ((bf16[64,32,256]{2,1,0:T(8,128)(2,1)}), bf16[64,32,256]{2,1,0:T(8,128)(2,1)}, u32[]{:S(2)}, u32[]{:S(2)}) async-start(bf16[64,32,256]{2,1,0:T(8,128)(2,1)} %broadcast_select_fusion.1), calls=%async_computation.2 | async-start | bytes 2097152 | tf_op jit(solution)/shard_map/all_to_all | solution.py:161
  143.7 4.3 %copy-start.14 = (f32[2048]{0:T(1024)S(1)}, f32[2048]{0:T(1024)}, u32[]{:S(2)}) copy-start(f32[2048]{0:T(1024)} %param.33) | copy-start | bytes 24580
Sparse Core Ops, SparseCore 0:
  17.2 35.9 all-gather.2
  74.7 62.4 reduce-scatter.1
where the time goes:
time: 161 us; the launch traced here: 160 us
  waiting for transfers between devices  47.7 us (30%)
  matrix products  26.4 us (16%)
  other arithmetic  24.6 us (15%)
  starting transfers between devices  23.7 us (15%)
  local copies, waits for them, and re-layouts  22.9 us (14%)
  between operations  15.2 us (9%)
    all_to_all x1, waiting for transfers between devices, on_device(): lax.all_to_all(arranged, 'blk', split_axis=0, concat_axis=0, tiled=True)  47.7 us
    all_to_all x1, starting transfers between devices, on_device(): lax.all_to_all(full_seq.reshape(blocks, block_span, head_dim), 'blk', spl...  12.8 us
    all_to_all x1, starting transfers between devices, on_device(): lax.all_to_all(arranged, 'blk', split_axis=0, concat_axis=0, tiled=True)  10.6 us
    unnamed x43, local copies, waits for them, and re-layouts  5.51 us
    dot_general x2, matrix products, scores_of(): lax.dot_general(rows, keys, (((1,), (1,)), ((), ())), preferred_element_t...  5.25 us
    reduce_sum x2, other arithmetic, on_device(): row_total = jnp.sum(old_exp, axis=1) + jnp.sum(new_exp, axis=1)  4.57 us
    dot_general x1, matrix products, on_device(): jnp.dot(normed, w_query, preferred_element_type=jnp.float32)  4.51 us
    dot_general x1, matrix products, on_device(): jnp.dot(attn, w_out, preferred_element_type=jnp.float32)  4.38 us
  transfers between devices with their start and end apart: 4, of which 1 were waited for; matrix products, arithmetic and copies ran while one was open for 32% of the time, Pallas kernels for 0%

commit v1 on v0

v1 whole, which is shorter than its diff:
```python
import functools

import jax
import jax.numpy as jnp
from jax import lax
from jax.experimental import pallas as pl
from jax.experimental.pallas import tpu as pltpu
from jax.sharding import PartitionSpec as P

QH = 8
KVH = 2
eps = 1e-06
rope_base = 1000000.0
F32 = jnp.float32
BF16 = jnp.bfloat16
ANY = pl.ANY
AXES = ("blk", "head")


def rms_scale(values):
    return values * lax.rsqrt(jnp.mean(values * values, axis=-1, keepdims=True) + eps)


def turn(values, cosine, sine):
    half = values.shape[-1] // 2
    low, high = values[:, :half], values[:, half:]
    return jnp.concatenate([low * cosine - high * sine, high * cosine + low * sine], axis=-1)


def dot(a, b):
    return jnp.dot(a, b, preferred_element_type=F32)


def dot_t(a, b):
    return lax.dot_general(a, b, (((1,), (1,)), ((), ())), preferred_element_type=F32)


def prep_kernel(
    meta, hidden, in_gain, w_kv, k_gain, cosine, sine, pool,
    normed, fresh, seq, fresh_all, old, sem, *, n_pages, page, rows, kv_heads,
):
    step = pl.program_id(0)
    head = meta[n_pages + 1]
    length = meta[n_pages]

    def page_copy(p):
        return pltpu.make_async_copy(
            pool.at[meta[p], head], old.at[pl.ds(p * page, page)], sem.at[p]
        )

    @pl.when(step == 0)
    def _():
        for p in range(n_pages):
            page_copy(p).start()

    tile = hidden.shape[0]
    values = (rms_scale(hidden[...].astype(F32)) * in_gain[...]).astype(BF16)
    normed[...] = values
    own = rms_scale(dot(values, w_kv[...]))
    key = turn(own * k_gain[...], cosine[...], sine[...])
    slot = jnp.where(head < kv_heads, key, own).astype(BF16)
    fresh[...] = slot
    fresh_all[pl.ds(pl.multiple_of(step * tile, tile), tile), :] = slot

    @pl.when(step == pl.num_programs(0) - 1)
    def _():
        total = seq.shape[0]
        span = rows + page
        prefix = n_pages * page
        for p in range(n_pages):
            page_copy(p).wait()
        for p in range(n_pages):
            at = p * page + lax.broadcasted_iota(jnp.int32, (page, 1), 0)
            part = old[p * page : (p + 1) * page, :].astype(F32)
            seq[p * page : (p + 1) * page, :] = jnp.where(at < length, part, 0.0).astype(BF16)
        seq[prefix:total, :] = jnp.zeros((total - prefix, seq.shape[1]), BF16)
        base = jnp.minimum(length // page * page, total - span)
        base = pl.multiple_of(base, page)
        row = base + lax.broadcasted_iota(jnp.int32, (span, 1), 0)
        col = lax.broadcasted_iota(jnp.int32, (span, rows), 1)
        pick = jnp.where(row - length == col, 1.0, 0.0).astype(BF16)
        placed = dot(pick, fresh_all[...])
        window = seq[pl.ds(base, span), :].astype(F32)
        seq[pl.ds(base, span), :] = jnp.where(row < length, window, placed).astype(BF16)


def query_kernel(normed, w_q, q_gain, cosine, sine, queries):
    heads, _, dim = queries.shape
    raw = dot(normed[...], w_q[...])
    for h in range(heads):
        part = rms_scale(raw[:, h * dim : (h + 1) * dim]) * q_gain[...]
        queries[h] = turn(part, cosine[...], sine[...]).astype(BF16)


def attend_kernel(
    meta, queries, w_out, pool, fresh, via_chip, via_core, via_both,
    send, mine, keys, vals, sem, *, n_pages, page, kv_heads, group,
):
    step = pl.program_id(0)
    head = meta[n_pages + 1]
    length = meta[n_pages]
    heads, tile, dim = queries.shape
    kv_of = head * heads // group
    prefix = n_pages * page
    rows = fresh.shape[0]

    @pl.when(step == 0)
    def _():
        copies = []
        for p in range(n_pages):
            for i, buf, slot in ((0, keys, kv_of), (1, vals, kv_of + kv_heads)):
                copies.append(
                    pltpu.make_async_copy(
                        pool.at[meta[p], slot], buf.at[pl.ds(p * page, page)], sem.at[i, p]
                    )
                )
        for copy in copies:
            copy.start()
        sources = (
            (fresh, via_chip),
            (via_core, via_both),
            (via_both, via_core),
            (via_chip, fresh),
        )
        for h, (key_src, val_src) in enumerate(sources):

            @pl.when(head == h)
            def _():
                new_key = pltpu.make_async_copy(
                    key_src, keys.at[pl.ds(prefix, rows)], sem.at[0, n_pages]
                )
                new_val = pltpu.make_async_copy(
                    val_src, vals.at[pl.ds(prefix, rows)], sem.at[1, n_pages]
                )
                new_key.start()
                new_val.start()
                new_key.wait()
                new_val.wait()

        for copy in copies:
            copy.wait()

    quarter = tile_of(step, head)
    flat = queries[...].reshape(heads * tile, dim)
    scores = dot_t(flat, keys[...])
    col = lax.broadcasted_iota(jnp.int32, (1, prefix + rows), 1)
    row = lax.broadcasted_iota(jnp.int32, (heads * tile, 1), 0)
    token = quarter * tile + jnp.where(row >= tile, row - tile, row)
    lowest = jnp.where(col < prefix, jnp.where(col < length, -1, rows), col - prefix)
    scores = jnp.where(lowest <= token, scores, -jnp.inf)
    top = jnp.max(scores, axis=1, keepdims=True)
    expo = jnp.exp(scores - top)
    total = jnp.sum(expo, axis=1, keepdims=True)
    attn = (dot(expo.astype(BF16), vals[...]) / total).astype(BF16)
    part = dot(attn[:tile], w_out[:dim, :])
    for h in range(1, heads):
        part = part + dot(attn[h * tile : (h + 1) * tile], w_out[h * dim : (h + 1) * dim, :])
    part = part.astype(BF16)

    @pl.when(step < 2)
    def _():
        send[0] = part

    @pl.when(step >= 2)
    def _():
        mine[0] = part


def tile_of(step, head):
    core = head % 2
    chip = head // 2
    to_core = jnp.where(step < 2, 1 - core, core)
    to_chip = jnp.where(step % 2 == 0, 1 - chip, chip)
    return to_chip * 2 + to_core


def post_kernel(
    meta, hidden, normed, mine, partner, far, plane, post_gain, left, right, laurel_gain,
    gate, proj, pl_gain, mixed,
):
    total = mine[0].astype(F32) + partner[0].astype(F32) + far[...].astype(F32)
    low = dot_t(normed[...], left[...]).astype(BF16)
    laurel = normed[...].astype(F32) + rms_scale(dot(low, right[...])) * laurel_gain[...]
    state = (hidden[...].astype(F32) + rms_scale(total) * post_gain[...] + laurel) * 2.0 ** (-0.5)
    gated = jax.nn.gelu(dot(state.astype(BF16), gate[...]), approximate=True)
    gated = (gated * plane[...].astype(F32)).astype(BF16)
    mixed[...] = (state + rms_scale(dot(gated, proj[...])) * pl_gain[...]).astype(BF16)


def permute_kernel(owner, spread, after, arranged, sem):
    count = spread.shape[0]

    def send(r, carry):
        pltpu.make_async_copy(spread.at[r], arranged.at[owner[r]], sem).start()
        return carry

    lax.fori_loop(0, count, send, 0)
    pltpu.make_async_copy(spread, arranged, sem).wait()


def whole(shape):
    zeros = (0,) * len(shape)
    return pl.BlockSpec(shape, lambda *_: zeros)


def on_device(
    hidden_in, layer_input, in_gain, w_query, w_keyval, q_gain, k_gain, w_out, post_gain,
    laurel_left, laurel_right, laurel_gain, w_plgate, w_plproj, pl_gain, kv_pool, page_table,
    prefix_len, decode_owner,
):
    rows, width = hidden_in.shape
    dim = kv_pool.shape[3]
    page = kv_pool.shape[2]
    n_pages = page_table.shape[1]
    kv_heads = kv_pool.shape[1] // 2
    heads = w_query.shape[1] // dim
    prefix = n_pages * page
    total_len = prefix + rows
    blocks = lax.axis_size("blk")
    group = QH // KVH
    n_head = lax.axis_size("head")
    quarter = rows // n_head
    head = lax.axis_index("head").astype(jnp.int32)
    meta = jnp.concatenate([page_table[0], prefix_len, head[None]])

    half = dim // 2
    frequency = rope_base ** (-jnp.arange(half, dtype=F32) / half)
    positions = prefix_len[0] + jnp.arange(rows, dtype=jnp.int32)
    angles = positions.astype(F32)[:, None] * frequency[None, :]
    cosine, sine = jnp.cos(angles), jnp.sin(angles)

    in_gain, q_gain, k_gain = in_gain[None], q_gain[None], k_gain[None]
    post_gain, laurel_gain, pl_gain = post_gain[None], laurel_gain[None], pl_gain[None]

    tile = quarter
    steps = rows // tile
    normed, fresh, full_seq = pl.pallas_call(
        functools.partial(
            prep_kernel, n_pages=n_pages, page=page, rows=rows, kv_heads=kv_heads
        ),
        grid_spec=pltpu.PrefetchScalarGridSpec(
            num_scalar_prefetch=1,
            grid=(steps,),
            in_specs=[
                pl.BlockSpec((tile, width), lambda i, m: (i, 0)),
                whole((1, width)),
                whole((width, dim)),
                whole((1, dim)),
                pl.BlockSpec((tile, half), lambda i, m: (i, 0)),
                pl.BlockSpec((tile, half), lambda i, m: (i, 0)),
                pl.BlockSpec(memory_space=ANY),
            ],
            out_specs=[
                pl.BlockSpec((tile, width), lambda i, m: (i, 0)),
                pl.BlockSpec((tile, dim), lambda i, m: (i, 0)),
                whole((total_len, dim)),
            ],
            scratch_shapes=[
                pltpu.VMEM((rows, dim), BF16),
                pltpu.VMEM((prefix, dim), BF16),
                pltpu.SemaphoreType.DMA((n_pages,)),
            ],
        ),
        out_shape=[
            jax.ShapeDtypeStruct((rows, width), BF16),
            jax.ShapeDtypeStruct((rows, dim), BF16),
            jax.ShapeDtypeStruct((total_len, dim), BF16),
        ],
        name="prep",
    )(meta, hidden_in, in_gain, w_keyval, k_gain, cosine, sine, kv_pool)

    def pairs(moves):
        return [(b * n_head + s, b * n_head + t) for b in range(blocks) for s, t in moves]

    via_chip = lax.ppermute(fresh, AXES, pairs(((1, 3), (2, 0))))
    via_core = lax.ppermute(fresh, AXES, pairs(((0, 1), (3, 2))))
    via_both = lax.ppermute(via_chip, AXES, pairs(((0, 1), (3, 2))))
    spread = lax.all_to_all(
        full_seq.reshape(blocks, total_len // blocks, dim), "blk", 0, 0, tiled=True
    )

    queries = pl.pallas_call(
        query_kernel,
        grid=(steps,),
        in_specs=[
            pl.BlockSpec((tile, width), lambda i: (i, 0)),
            whole(w_query.shape),
            whole((1, dim)),
            pl.BlockSpec((tile, half), lambda i: (i, 0)),
            pl.BlockSpec((tile, half), lambda i: (i, 0)),
        ],
        out_specs=pl.BlockSpec((heads, tile, dim), lambda i: (0, i, 0)),
        out_shape=jax.ShapeDtypeStruct((heads, rows, dim), BF16),
        name="query",
    )(normed, w_query, q_gain, cosine, sine)

    send, mine = pl.pallas_call(
        functools.partial(
            attend_kernel, n_pages=n_pages, page=page, kv_heads=kv_heads, group=group
        ),
        grid_spec=pltpu.PrefetchScalarGridSpec(
            num_scalar_prefetch=1,
            grid=(n_head,),
            in_specs=[
                pl.BlockSpec(
                    (heads, quarter, dim), lambda i, m: (0, tile_of(i, m[n_pages + 1]), 0)
                ),
                whole(w_out.shape),
            ]
            + [pl.BlockSpec(memory_space=ANY)] * 5,
            out_specs=[
                pl.BlockSpec((1, quarter, width), lambda i, m: (jnp.minimum(i, 1), 0, 0)),
                pl.BlockSpec((1, quarter, width), lambda i, m: (jnp.maximum(i - 2, 0), 0, 0)),
            ],
            scratch_shapes=[
                pltpu.VMEM((total_len, dim), BF16),
                pltpu.VMEM((total_len, dim), BF16),
                pltpu.SemaphoreType.DMA((2, n_pages + 1)),
            ],
        ),
        out_shape=[jax.ShapeDtypeStruct((2, quarter, width), BF16)] * 2,
        name="attend",
    )(meta, queries, w_out, kv_pool, fresh, via_chip, via_core, via_both)

    core_pairs = pairs(((0, 1), (1, 0), (2, 3), (3, 2)))
    chip_pairs = pairs(((0, 2), (1, 3), (2, 0), (3, 1)))
    partner = lax.ppermute(send, AXES, core_pairs)
    pair_sum = (mine[0].astype(F32) + partner[0].astype(F32)).astype(BF16)
    far = lax.ppermute(pair_sum, AXES, chip_pairs)

    mixed = pl.pallas_call(
        post_kernel,
        grid_spec=pltpu.PrefetchScalarGridSpec(
            num_scalar_prefetch=1,
            grid=(1,),
            in_specs=[
                pl.BlockSpec((quarter, width), lambda i, m: (m[n_pages + 1], 0)),
                pl.BlockSpec((quarter, width), lambda i, m: (m[n_pages + 1], 0)),
                pl.BlockSpec((1, quarter, width), lambda i, m: (1, 0, 0)),
                pl.BlockSpec((1, quarter, width), lambda i, m: (1, 0, 0)),
                whole((quarter, width)),
                whole(layer_input.shape),
                whole((1, width)),
                whole(laurel_left.shape[::-1]),
                whole(laurel_right.shape),
                whole((1, width)),
                whole(w_plgate.shape),
                whole(w_plproj.shape),
                whole((1, width)),
            ],
            out_specs=whole((quarter, width)),
        ),
        out_shape=jax.ShapeDtypeStruct((quarter, width), BF16),
        name="post",
    )(
        meta, hidden_in, normed, mine, partner, far, layer_input, post_gain, laurel_left.T,
        laurel_right, laurel_gain, w_plgate, w_plproj, pl_gain,
    )

    arranged = pl.pallas_call(
        permute_kernel,
        grid_spec=pltpu.PrefetchScalarGridSpec(
            num_scalar_prefetch=1,
            grid=(1,),
            in_specs=[pl.BlockSpec(memory_space=ANY)] * 2,
            out_specs=pl.BlockSpec(memory_space=ANY),
            scratch_shapes=[pltpu.SemaphoreType.DMA],
        ),
        out_shape=jax.ShapeDtypeStruct(spread.shape, spread.dtype),
        name="permute",
    )(decode_owner, spread, pair_sum)
    owned = lax.all_to_all(arranged, "blk", 0, 0, tiled=True)
    return mixed, owned.reshape(1, 1, total_len, dim)


def solution(mesh):
    in_specs = (
        P("blk", None),
        P(("blk", "head"), None),
        P(),
        P(None, "head"),
        P(None, "head"),
        P(),
        P(),
        P("head", None),
        P(),
        P(),
        P(),
        P(),
        P(),
        P(),
        P(),
        P("blk", None, None, None),
        P("blk", None),
        P("blk"),
        P(),
    )
    out_specs = (P(("blk", "head"), None), P("head", "blk", None, None))
    return jax.shard_map(
        on_device, mesh=mesh, in_specs=in_specs, out_specs=out_specs, check_vma=False
    )
```

time: 161 us -> 176 us (1.093)
  Pallas kernels: 0 us -> 65.8 us
  matrix products: 26.4 us -> 0 us
  local copies, waits for them, and re-layouts: 22.9 us -> 3.44 us
  other arithmetic: 24.6 us -> 5.45 us
  starting transfers between devices: 23.7 us -> 37.9 us
  waiting for transfers between devices: 47.7 us -> 61.7 us
  between operations: 15.2 us -> 1.42 us
    pallas_call x0 -> x5, Pallas kernels: none -> 65.8 us  [the longest x1 33.5 us: on_device(): pl.pallas_call(permute_kernel, grid_spec=pltpu.PrefetchScalarGridSpec(num...]
    ppermute x0 -> x5, waiting for transfers between devices: none -> 58.2 us  [the longest x1 39.6 us: on_device(): far = lax.ppermute(pair_sum, AXES, chip_pairs)]
    all_to_all x2, waiting for transfers between devices: 47.7 us -> 3.51 us  [the longest x1 3.5 us: on_device(): owned = lax.all_to_all(arranged, 'blk', 0, 0, tiled=True)]
    dot_general x9 -> x0, matrix products: 26.4 us -> none  [the longest x2 5.25 us: scores_of(): lax.dot_general(rows, keys, (((1,), (1,)), ((), ())), preferred_element_t...]
    ppermute x0 -> x5, starting transfers between devices: none -> 15 us  [the longest x1 6.13 us: on_device(): via_chip = lax.ppermute(fresh, AXES, pairs(((1, 3), (2, 0))))]
    reduce_sum x4 -> x0, other arithmetic: 8.02 us -> none  [the longest x2 4.57 us: on_device(): row_total = jnp.sum(old_exp, axis=1) + jnp.sum(new_exp, axis=1)]
    select_n x6 -> x0, other arithmetic: 6.6 us -> none  [the longest x2 3.91 us: on_device(): my_pages = jnp.take(kv_pool, page_table[0], axis=0)]
    gather x2 -> x0, local copies, waits for them, and re-layouts: 5.31 us -> none  [the longest x1 2.81 us: on_device(): arranged = jnp.take(spread, inverse, axis=0)]
  transfers between devices with their start and end apart: 4 -> 7, of which waited for: 1 -> 5; matrix products, arithmetic and copies ran while one was open for 32% -> 1% of each run, Pallas kernels for 0% -> 14%
where the time goes in v1:
time: 176 us
  Pallas kernels  65.8 us (37%)
  waiting for transfers between devices  61.7 us (35%)
  starting transfers between devices  37.9 us (22%)
  other arithmetic  5.45 us (3%)
  local copies, waits for them, and re-layouts  3.44 us (2%)
    ppermute x1, waiting for transfers between devices, on_device(): far = lax.ppermute(pair_sum, AXES, chip_pairs)  39.6 us
    pallas_call x1, Pallas kernels, on_device(): pl.pallas_call(permute_kernel, grid_spec=pltpu.PrefetchScalarGridSpec(num...  33.5 us
    ppermute x1, waiting for transfers between devices, on_device(): via_chip = lax.ppermute(fresh, AXES, pairs(((1, 3), (2, 0))))  15.2 us
    pallas_call x1, Pallas kernels, on_device(): pl.pallas_call(functools.partial(attend_kernel, n_pages=n_pages, page=pag...  13.8 us
    all_to_all x1, starting transfers between devices, on_device(): lax.all_to_all(full_seq.reshape(blocks, total_len // blocks, dim), 'blk',...  12.7 us
    all_to_all x1, starting transfers between devices, on_device(): owned = lax.all_to_all(arranged, 'blk', 0, 0, tiled=True)  10.2 us
    pallas_call x1, Pallas kernels, on_device(): pl.pallas_call(functools.partial(prep_kernel, n_pages=n_pages, page=page,...  6.98 us
    ppermute x1, starting transfers between devices, on_device(): via_chip = lax.ppermute(fresh, AXES, pairs(((1, 3), (2, 0))))  6.13 us
  transfers between devices with their start and end apart: 7, of which 5 were waited for; matrix products, arithmetic and copies ran while one was open for 1% of the time, Pallas kernels for 14%

profile of v1, /device:TPU:1, one launch (start us, length us, event | category | flops | bytes accessed | tf_op | source)
XLA Modules:
  0.0 175.8 jit_solution(8258479990193964915)
XLA Ops:
  1.3 1.3 pad_add_fusion.meta
  2.6 1.8 %multiply_sine_fusion = (f32[512,128]{1,0:T(8,128)}, f32[512,128]{1,0:T(8,128)}) fusion(f32[128]{0:T(128)S(1)} %multiply_power_fusion, f32[512]{0:T(512)S(1)} %add_convert_fusion.1), kind=kLoop, calls=%fused_computation.2 | loop fusion | flops 65536 | bytes 526848 | tf_op jit(solution)/shard_map/sin | solution.py:230
  4.4 7.0 %prep.1 = (bf16[512,2048]{1,0:T(8,128)(2,1)}, bf16[512,256]{1,0:T(8,128)(2,1)}, bf16[2048,256]{1,0:T(8,128)(2,1)}) custom-call(s32[14]{0:T(128)} %pad_add_fusion.meta, bf16[512,2048]{1,0:T(8,128)(2,1)} %hidden.3, f32[1,2048]{1,0:T(1,128)} %bitcast.18, bf16[2048,256]{1,0:T(8,128)(2,1)} %w_kv.1, f32[1,256]{1,0:T(1,128)} %bitcast.22, ...), custom_call_target="tpu_custom_call" | custom-call | tf_op jit(solution)/shard_map/prep/pallas_call | solution.py:237
  11.4 0.0 copy-start.4
  11.4 12.7 %all-to-all-start = ((bf16[64,32,256]{2,1,0:T(8,128)(2,1)}), bf16[64,32,256]{2,1,0:T(8,128)(2,1)S(1)}, u32[]{:S(2)}, u32[]{:S(2)}) async-start(bf16[64,32,256]{2,1,0:T(8,128)(2,1)} %bitcast.16), calls=%async_computation | async-start | bytes 2097152 | tf_op jit(solution)/shard_map/all_to_all | solution.py:278
  24.1 0.0 copy-done.4
  24.1 6.1 %collective-permute-start = (bf16[512,256]{1,0:T(8,128)(2,1)S(1)}, bf16[512,256]{1,0:T(8,128)(2,1)S(1)}, u32[]{:S(2)}, u32[]{:S(2)}) collective-permute-start(bf16[512,256]{1,0:T(8,128)(2,1)S(1)} %copy-done.4), channel_id=1, source_target_pairs={{1,3},{2,0},{5,7},{6,4},{9,11},{10,8},{13,15},{14,12},{17,19},{18,... | collective-permute-start | bytes 786440 | tf_op jit(solution)/shard_map/ppermute | solution.py:275
  30.3 1.3 collective-permute-start.1
  31.6 15.2 %collective-permute-done.via_chip = bf16[512,256]{1,0:T(8,128)(2,1)S(1)} collective-permute-done((bf16[512,256]{1,0:T(8,128)(2,1)S(1)}, bf16[512,256]{1,0:T(8,128)(2,1)S(1)}, u32[]{:S(2)}, u32[]{:S(2)}) %collective-permute-start) | collective-permute-done | bytes 262176 | tf_op jit(solution)/shard_map/ppermute | solution.py:275
  46.8 0.0 copy-start.5
  46.8 1.3 collective-permute-start.2
  48.1 5.4 %query.1.queries = bf16[2,512,256]{2,1,0:T(8,128)(2,1)} custom-call(bf16[512,2048]{1,0:T(8,128)(2,1)} %get-tuple-element.7.normed, bf16[2048,512]{1,0:T(8,128)(2,1)} %w_q.1, f32[1,256]{1,0:T(1,128)} %bitcast.23, f32[512,128]{1,0:T(8,128)} %get-tuple-element.13.cosine, f32[512,128]{1,0:T(8,128)} %get-tuple-element.12.sine), custom_call_target="tpu_custom_call" | custom-call | tf_op jit(solution)/shard_map/query/pallas_call | solution.py:282
  53.5 0.0 copy-done.5
  53.5 0.0 collective-permute-done.1.via_core
  53.5 0.0 copy-start.6
  53.6 0.9 collective-permute-done.2.via_both
  54.4 0.0 copy-done.6
  54.4 0.0 copy-start.7
  54.5 0.7 copy-done.7
  55.1 13.8 %attend.1 = (bf16[2,128,2048]{2,1,0:T(8,128)(2,1)}, bf16[2,128,2048]{2,1,0:T(8,128)(2,1)}) custom-call(s32[14]{0:T(128)} %pad_add_fusion.meta, bf16[2,512,256]{2,1,0:T(8,128)(2,1)} %query.1.queries, bf16[512,2048]{1,0:T(8,128)(2,1)} %w_out.1, bf16[12,4,128,256]{3,2,1,0:T(8,128)(2,1)} %pool.3, bf16[512,256]{1,0:T(8,128)(2,1)} %get-tuple-element.8.fresh, ...), custom_call_target="tpu_custom_call" | custom-call | tf_op jit(solution)/shard_map/attend/pallas_call | solution.py:297
  69.0 5.2 %collective-permute-start.3 = (bf16[2,128,2048]{2,1,0:T(8,128)(2,1)}, bf16[2,128,2048]{2,1,0:T(8,128)(2,1)S(1)}, u32[]{:S(2)}, u32[]{:S(2)}) collective-permute-start(bf16[2,128,2048]{2,1,0:T(8,128)(2,1)} %get-tuple-element.10), channel_id=1, source_target_pairs={{0,1},{1,0},{2,3},{3,2},{4,5},{5,4},{6,7},{7,6},{8,9},{9,8},{10,11... | collective-permute-start | bytes 3145736 | tf_op jit(solution)/shard_map/ppermute | solution.py:327
  74.2 2.5 %collective-permute-done.3.partner = bf16[2,128,2048]{2,1,0:T(8,128)(2,1)S(1)} collective-permute-done((bf16[2,128,2048]{2,1,0:T(8,128)(2,1)}, bf16[2,128,2048]{2,1,0:T(8,128)(2,1)S(1)}, u32[]{:S(2)}, u32[]{:S(2)}) %collective-permute-start.3) | collective-permute-done | bytes 1048608 | tf_op jit(solution)/shard_map/ppermute | solution.py:327
  76.7 0.0 copy-start.1
  76.7 2.3 %fusion.after = bf16[128,2048]{1,0:T(8,128)(2,1)} fusion(bf16[2,128,2048]{2,1,0:T(8,128)(2,1)S(1)} %collective-permute-done.3.partner, bf16[2,128,2048]{2,1,0:T(8,128)(2,1)} %get-tuple-element.9.mine), kind=kLoop, calls=%fused_computation.1 | loop fusion | flops 1048576 | bytes 1572864 | tf_op jit(solution)/shard_map/convert_element_type | solution.py:328
  79.1 0.0 copy-start.2
  79.1 0.0 all-to-all-done.spread
  79.1 0.0 copy-start
  79.1 1.0 copy-done
  80.0 33.5 %permute.1 = bf16[64,32,256]{2,1,0:T(8,128)(2,1)} custom-call(s32[64]{0:T(128)} %owner.1, bf16[64,32,256]{2,1,0:T(8,128)(2,1)} %copy-done, bf16[128,2048]{1,0:T(8,128)(2,1)} %fusion.after), custom_call_target="tpu_custom_call" | custom-call | tf_op jit(solution)/shard_map/permute/pallas_call | solution.py:360
  113.6 0.0 copy-done.1
  113.6 10.2 %all-to-all-start.1 = ((bf16[64,32,256]{2,1,0:T(8,128)(2,1)}), bf16[64,32,256]{2,1,0:T(8,128)(2,1)S(1)}, u32[]{:S(2)}, u32[]{:S(2)}) async-start(bf16[64,32,256]{2,1,0:T(8,128)(2,1)} %permute.1), calls=%async_computation.1 | async-start | bytes 2097152 | tf_op jit(solution)/shard_map/all_to_all | solution.py:372
  123.8 0.0 copy-done.2
  123.8 1.1 collective-permute-start.4
  124.9 39.6 %collective-permute-done.4.far = bf16[128,2048]{1,0:T(8,128)(2,1)S(1)} collective-permute-done((bf16[128,2048]{1,0:T(8,128)(2,1)S(1)}, bf16[128,2048]{1,0:T(8,128)(2,1)S(1)}, u32[]{:S(2)}, u32[]{:S(2)}) %collective-permute-start.4) | collective-permute-done | bytes 524320 | tf_op jit(solution)/shard_map/ppermute | solution.py:329
  164.5 0.0 copy-start.3
  164.5 0.8 copy-done.3
  165.3 6.0 %post.1 = bf16[128,2048]{1,0:T(8,128)(2,1)} custom-call(s32[14]{0:T(128)} %pad_add_fusion.meta, bf16[512,2048]{1,0:T(8,128)(2,1)} %hidden.3, bf16[512,2048]{1,0:T(8,128)(2,1)} %get-tuple-element.7.normed, bf16[2,128,2048]{2,1,0:T(8,128)(2,1)} %get-tuple-element.9.mine, bf16[2,128,2048]{2,1,0:T(8,128)(2,1)} %copy-done.1, bf16[128,2048]{1,0:T(8,128)(2,1)} %copy-done.3, ...), custom_call_target="tpu_custom_call" | custom-call | tf_op jit(solution)/shard_map/post/pallas_call | solution.py:331
  171.3 3.5 %all-to-all-done.1 = bf16[64,32,256]{2,1,0:T(8,128)(2,1)S(1)} async-done(((bf16[64,32,256]{2,1,0:T(8,128)(2,1)}), bf16[64,32,256]{2,1,0:T(8,128)(2,1)S(1)}, u32[]{:S(2)}, u32[]{:S(2)}) %all-to-all-start.1) | async-done | bytes 1048608 | tf_op jit(solution)/shard_map/all_to_all | solution.py:372
  174.8 1.0 copy.23
  (2 shorter events, 0.0 us)
Async XLA Ops:
  11.4 12.7 %copy-start.4 = (bf16[512,256]{1,0:T(8,128)(2,1)S(1)}, bf16[512,256]{1,0:T(8,128)(2,1)}, u32[]{:S(2)}) copy-start(bf16[512,256]{1,0:T(8,128)(2,1)} %get-tuple-element.8.fresh) | copy-start | bytes 786436
  11.4 67.6 %all-to-all-start = ((bf16[64,32,256]{2,1,0:T(8,128)(2,1)}), bf16[64,32,256]{2,1,0:T(8,128)(2,1)S(1)}, u32[]{:S(2)}, u32[]{:S(2)}) async-start(bf16[64,32,256]{2,1,0:T(8,128)(2,1)} %bitcast.16), calls=%async_computation | async-start | bytes 2097152 | tf_op jit(solution)/shard_map/all_to_all | solution.py:278
  24.1 22.7 %collective-permute-start = (bf16[512,256]{1,0:T(8,128)(2,1)S(1)}, bf16[512,256]{1,0:T(8,128)(2,1)S(1)}, u32[]{:S(2)}, u32[]{:S(2)}) collective-permute-start(bf16[512,256]{1,0:T(8,128)(2,1)S(1)} %copy-done.4), channel_id=1, source_target_pairs={{1,3},{2,0},{5,7},{6,4},{9,11},{10,8},{13,15},{14,12},{17,19},{18,... | collective-permute-start | bytes 786440 | tf_op jit(solution)/shard_map/ppermute | solution.py:275
  30.3 23.3 %collective-permute-start.1 = (bf16[512,256]{1,0:T(8,128)(2,1)S(1)}, bf16[512,256]{1,0:T(8,128)(2,1)S(1)}, u32[]{:S(2)}, u32[]{:S(2)}) collective-permute-start(bf16[512,256]{1,0:T(8,128)(2,1)S(1)} %copy-done.4), channel_id=1, source_target_pairs={{0,1},{3,2},{4,5},{7,6},{8,9},{11,10},{12,13},{15,14},{16,17},{19,... | collective-permute-start | bytes 786440 | tf_op jit(solution)/shard_map/ppermute | solution.py:276
  46.8 6.7 %copy-start.5 = (bf16[512,256]{1,0:T(8,128)(2,1)}, bf16[512,256]{1,0:T(8,128)(2,1)S(1)}, u32[]{:S(2)}) copy-start(bf16[512,256]{1,0:T(8,128)(2,1)S(1)} %collective-permute-done.via_chip) | copy-start | bytes 786436
  46.8 7.6 %collective-permute-start.2 = (bf16[512,256]{1,0:T(8,128)(2,1)S(1)}, bf16[512,256]{1,0:T(8,128)(2,1)S(1)}, u32[]{:S(2)}, u32[]{:S(2)}) collective-permute-start(bf16[512,256]{1,0:T(8,128)(2,1)S(1)} %collective-permute-done.via_chip), channel_id=1, source_target_pairs={{0,1},{3,2},{4,5},{7,6},{8,9},{11,10},{12,13},{15,14},{16,17},{19,... | collective-permute-start | bytes 786440 | tf_op jit(solution)/shard_map/ppermute | solution.py:277
  53.5 0.9 copy-start.6
  54.4 0.7 copy-start.7
  69.0 7.7 %collective-permute-start.3 = (bf16[2,128,2048]{2,1,0:T(8,128)(2,1)}, bf16[2,128,2048]{2,1,0:T(8,128)(2,1)S(1)}, u32[]{:S(2)}, u32[]{:S(2)}) collective-permute-start(bf16[2,128,2048]{2,1,0:T(8,128)(2,1)} %get-tuple-element.10), channel_id=1, source_target_pairs={{0,1},{1,0},{2,3},{3,2},{4,5},{5,4},{6,7},{7,6},{8,9},{9,8},{10,11... | collective-permute-start | bytes 3145736 | tf_op jit(solution)/shard_map/ppermute | solution.py:327
  76.7 36.8 %copy-start.1 = (bf16[2,128,2048]{2,1,0:T(8,128)(2,1)}, bf16[2,128,2048]{2,1,0:T(8,128)(2,1)S(1)}, u32[]{:S(2)}) copy-start(bf16[2,128,2048]{2,1,0:T(8,128)(2,1)S(1)} %collective-permute-done.3.partner) | copy-start | bytes 3145732
  79.1 44.8 %copy-start.2 = (bf16[128,2048]{1,0:T(8,128)(2,1)S(1)}, bf16[128,2048]{1,0:T(8,128)(2,1)}, u32[]{:S(2)}) copy-start(bf16[128,2048]{1,0:T(8,128)(2,1)} %fusion.after) | copy-start | bytes 1572868
  79.1 1.0 copy-start
  113.6 61.2 %all-to-all-start.1 = ((bf16[64,32,256]{2,1,0:T(8,128)(2,1)}), bf16[64,32,256]{2,1,0:T(8,128)(2,1)S(1)}, u32[]{:S(2)}, u32[]{:S(2)}) async-start(bf16[64,32,256]{2,1,0:T(8,128)(2,1)} %permute.1), calls=%async_computation.1 | async-start | bytes 2097152 | tf_op jit(solution)/shard_map/all_to_all | solution.py:372
  123.8 40.6 %collective-permute-start.4 = (bf16[128,2048]{1,0:T(8,128)(2,1)S(1)}, bf16[128,2048]{1,0:T(8,128)(2,1)S(1)}, u32[]{:S(2)}, u32[]{:S(2)}) collective-permute-start(bf16[128,2048]{1,0:T(8,128)(2,1)S(1)} %copy-done.2), channel_id=1, source_target_pairs={{0,2},{1,3},{2,0},{3,1},{4,6},{5,7},{6,4},{7,5},{8,10},{9,11},{10,... | collective-permute-start | bytes 1572872 | tf_op jit(solution)/shard_map/ppermute | solution.py:329
  164.5 0.8 copy-start.3

commit v2 on v1

v2 whole, which is shorter than its diff:
```python
import functools

import jax
import jax.numpy as jnp
from jax import lax
from jax.experimental import pallas as pl
from jax.experimental.pallas import tpu as pltpu
from jax.sharding import PartitionSpec as P

QH = 8
KVH = 2
eps = 1e-06
rope_base = 1000000.0
F32 = jnp.float32
BF16 = jnp.bfloat16
ANY = pl.ANY
AXES = ("blk", "head")


def rms_scale(values):
    return values * lax.rsqrt(jnp.mean(values * values, axis=-1, keepdims=True) + eps)


def turn(values, cosine, sine):
    half = values.shape[-1] // 2
    low, high = values[:, :half], values[:, half:]
    return jnp.concatenate([low * cosine - high * sine, high * cosine + low * sine], axis=-1)


def dot(a, b):
    return jnp.dot(a, b, preferred_element_type=F32)


def dot_t(a, b):
    return lax.dot_general(a, b, (((1,), (1,)), ((), ())), preferred_element_type=F32)


def prep_kernel(
    table, prefix_len, head_at, hidden, in_gain, w_kv, k_gain, frequency, pool,
    normed, fresh, seq, cosine, sine, fresh_all, old, sem, *, n_pages, page, rows, kv_heads,
):
    step = pl.program_id(0)
    steps = pl.num_programs(0)
    head = head_at[0]
    length = prefix_len[0]
    tile = hidden.shape[0]
    total = seq.shape[0]
    prefix = n_pages * page

    def page_copy(p):
        return pltpu.make_async_copy(
            pool.at[table[p], head], old.at[pl.ds(p * page, page)], sem.at[p]
        )

    @pl.when(step == 0)
    def _():
        for p in range(n_pages):
            page_copy(p).start()

    values = (rms_scale(hidden[...].astype(F32)) * in_gain[...]).astype(BF16)
    normed[...] = values
    own = rms_scale(dot(values, w_kv[...]))
    position = length + step * tile + lax.broadcasted_iota(jnp.int32, (tile, 1), 0)
    angles = position.astype(F32) * frequency[...]
    cos, sin = jnp.cos(angles), jnp.sin(angles)
    cosine[...] = cos
    sine[...] = sin
    key = turn(own * k_gain[...], cos, sin)
    slot = jnp.where(head < kv_heads, key, own).astype(BF16)
    fresh[...] = slot
    fresh_all[pl.ds(pl.multiple_of(step * tile, tile), tile), :] = slot

    @pl.when(step == 0)
    def _():
        for p in range(n_pages):
            page_copy(p).wait()
        for p in range(n_pages):
            at = p * page + lax.broadcasted_iota(jnp.int32, (page, 1), 0)
            part = old[p * page : (p + 1) * page, :].astype(F32)
            seq[p * page : (p + 1) * page, :] = jnp.where(at < length, part, 0.0).astype(BF16)
        seq[prefix:total, :] = jnp.zeros((total - prefix, seq.shape[1]), BF16)

    @pl.when(step == steps - 1)
    def _():
        span = rows + page
        base = jnp.minimum(length // page * page, total - span)
        base = pl.multiple_of(base, page)
        row = base + lax.broadcasted_iota(jnp.int32, (span, 1), 0)
        col = lax.broadcasted_iota(jnp.int32, (span, rows), 1)
        pick = jnp.where(row - length == col, 1.0, 0.0).astype(BF16)
        placed = dot(pick, fresh_all[...])
        window = seq[pl.ds(base, span), :].astype(F32)
        seq[pl.ds(base, span), :] = jnp.where(row < length, window, placed).astype(BF16)


def query_kernel(normed, w_q, q_gain, cosine, sine, queries):
    part = rms_scale(dot(normed[...], w_q[...])) * q_gain[...]
    queries[0] = turn(part, cosine[...], sine[...]).astype(BF16)


def attend_kernel(
    table, prefix_len, head_at, near_q, far_q, w_out, pool, fresh, via_chip, via_core, via_both,
    send, mine, keys, vals, sem, *, n_pages, page, kv_heads, group,
):
    step = pl.program_id(0)
    head = head_at[0]
    length = prefix_len[0]
    heads, tile, _ = near_q.shape
    kv_of = head * heads // group
    prefix = n_pages * page
    rows = fresh.shape[0]

    @pl.when(step == 0)
    def _():
        copies = []
        for p in range(n_pages):
            for i, buf, slot in ((0, keys, kv_of), (1, vals, kv_of + kv_heads)):
                copies.append(
                    pltpu.make_async_copy(
                        pool.at[table[p], slot], buf.at[pl.ds(p * page, page)], sem.at[i, p]
                    )
                )
        for copy in copies:
            copy.start()
        sources = (
            (fresh, via_chip),
            (via_core, via_both),
            (via_both, via_core),
            (via_chip, fresh),
        )
        for h, (key_src, val_src) in enumerate(sources):

            @pl.when(head == h)
            def _():
                new_key = pltpu.make_async_copy(
                    key_src, keys.at[pl.ds(prefix, rows)], sem.at[0, n_pages]
                )
                new_val = pltpu.make_async_copy(
                    val_src, vals.at[pl.ds(prefix, rows)], sem.at[1, n_pages]
                )
                new_key.start()
                new_val.start()
                new_key.wait()
                new_val.wait()

        for copy in copies:
            copy.wait()

    col = lax.broadcasted_iota(jnp.int32, (1, prefix + rows), 1)
    lowest = jnp.where(col < prefix, jnp.where(col < length, -1, rows), col - prefix)
    row = lax.broadcasted_iota(jnp.int32, (tile, 1), 0)
    attns = [[], []]
    for h in range(heads):
        both = jnp.concatenate([far_q[h], near_q[h]], axis=0)
        token = jnp.concatenate(
            [quarter_of(step, i, head) * tile + row for i in range(2)], axis=0
        )
        scores = jnp.where(lowest <= token, dot_t(both, keys[...]), -jnp.inf)
        top = jnp.max(scores, axis=1, keepdims=True)
        expo = jnp.exp(scores - top)
        total = jnp.sum(expo, axis=1, keepdims=True)
        attns[h] = (dot(expo.astype(BF16), vals[...]) / total).astype(BF16)
    part = dot(jnp.concatenate(attns, axis=1), w_out[...]).astype(BF16)

    @pl.when(step == 0)
    def _():
        send[0] = part[:tile]
        send[1] = part[tile:]

    @pl.when(step == 1)
    def _():
        mine[0] = part[:tile]
        mine[1] = part[tile:]


def quarter_of(step, own_chip, head):
    core = head % 2
    chip = head // 2
    to_core = jnp.where(step == 0, 1 - core, core)
    to_chip = chip if own_chip else 1 - chip
    return to_chip * 2 + to_core


def post_kernel(
    head_at, hidden, normed, mine, partner, far, plane, post_gain, left, right, laurel_gain,
    gate, proj, pl_gain, mixed,
):
    total = mine[0].astype(F32) + partner[0].astype(F32) + far[...].astype(F32)
    low = dot_t(normed[...], left[...]).astype(BF16)
    laurel = normed[...].astype(F32) + rms_scale(dot(low, right[...])) * laurel_gain[...]
    state = (hidden[...].astype(F32) + rms_scale(total) * post_gain[...] + laurel) * 2.0 ** (-0.5)
    gated = jax.nn.gelu(dot(state.astype(BF16), gate[...]), approximate=True)
    gated = (gated * plane[...].astype(F32)).astype(BF16)
    mixed[...] = (state + rms_scale(dot(gated, proj[...])) * pl_gain[...]).astype(BF16)


def permute_kernel(owner, spread, after, arranged):
    def place(r, carry):
        arranged[owner[r]] = spread[r]
        return carry

    lax.fori_loop(0, spread.shape[0], place, 0, unroll=8)


def whole(shape):
    zeros = (0,) * len(shape)
    return pl.BlockSpec(shape, lambda *_: zeros)


def on_device(
    hidden_in, layer_input, in_gain, w_query, w_keyval, q_gain, k_gain, w_out, post_gain,
    laurel_left, laurel_right, laurel_gain, w_plgate, w_plproj, pl_gain, kv_pool, page_table,
    prefix_len, decode_owner,
):
    rows, width = hidden_in.shape
    dim = kv_pool.shape[3]
    page = kv_pool.shape[2]
    n_pages = page_table.shape[1]
    kv_heads = kv_pool.shape[1] // 2
    heads = w_query.shape[1] // dim
    prefix = n_pages * page
    total_len = prefix + rows
    blocks = lax.axis_size("blk")
    group = QH // KVH
    n_head = lax.axis_size("head")
    quarter = rows // n_head
    head = lax.axis_index("head").astype(jnp.int32)
    half = dim // 2
    frequency = (rope_base ** (-jnp.arange(half, dtype=F32) / half))[None]
    scalars = (page_table[0], prefix_len, head[None])

    in_gain, q_gain, k_gain = in_gain[None], q_gain[None], k_gain[None]
    post_gain, laurel_gain, pl_gain = post_gain[None], laurel_gain[None], pl_gain[None]

    tile = rows // 2
    normed, fresh, full_seq, cosine, sine = pl.pallas_call(
        functools.partial(
            prep_kernel, n_pages=n_pages, page=page, rows=rows, kv_heads=kv_heads
        ),
        grid_spec=pltpu.PrefetchScalarGridSpec(
            num_scalar_prefetch=3,
            grid=(rows // tile,),
            in_specs=[
                pl.BlockSpec((tile, width), lambda i, *_: (i, 0)),
                whole((1, width)),
                whole((width, dim)),
                whole((1, dim)),
                whole((1, half)),
                pl.BlockSpec(memory_space=ANY),
            ],
            out_specs=[
                pl.BlockSpec((tile, width), lambda i, *_: (i, 0)),
                pl.BlockSpec((tile, dim), lambda i, *_: (i, 0)),
                whole((total_len, dim)),
                pl.BlockSpec((tile, half), lambda i, *_: (i, 0)),
                pl.BlockSpec((tile, half), lambda i, *_: (i, 0)),
            ],
            scratch_shapes=[
                pltpu.VMEM((rows, dim), BF16),
                pltpu.VMEM((prefix, dim), BF16),
                pltpu.SemaphoreType.DMA((n_pages,)),
            ],
        ),
        out_shape=[
            jax.ShapeDtypeStruct((rows, width), BF16),
            jax.ShapeDtypeStruct((rows, dim), BF16),
            jax.ShapeDtypeStruct((total_len, dim), BF16),
            jax.ShapeDtypeStruct((rows, half), F32),
            jax.ShapeDtypeStruct((rows, half), F32),
        ],
        name="prep",
    )(*scalars, hidden_in, in_gain, w_keyval, k_gain, frequency, kv_pool)

    def pairs(moves):
        return [(b * n_head + s, b * n_head + t) for b in range(blocks) for s, t in moves]

    via_chip = lax.ppermute(fresh, AXES, pairs(((1, 3), (2, 0))))
    via_core = lax.ppermute(fresh, AXES, pairs(((0, 1), (3, 2))))
    via_both = lax.ppermute(via_chip, AXES, pairs(((0, 1), (3, 2))))
    spread = lax.all_to_all(
        full_seq.reshape(blocks, total_len // blocks, dim), "blk", 0, 0, tiled=True
    )

    queries = pl.pallas_call(
        query_kernel,
        grid=(heads,),
        in_specs=[
            whole((rows, width)),
            pl.BlockSpec((width, dim), lambda i: (0, i)),
            whole((1, dim)),
            whole((rows, half)),
            whole((rows, half)),
        ],
        out_specs=pl.BlockSpec((1, rows, dim), lambda i: (i, 0, 0)),
        out_shape=jax.ShapeDtypeStruct((heads, rows, dim), BF16),
        name="query",
    )(normed, w_query, q_gain, cosine, sine)

    send, mine = pl.pallas_call(
        functools.partial(
            attend_kernel, n_pages=n_pages, page=page, kv_heads=kv_heads, group=group
        ),
        grid_spec=pltpu.PrefetchScalarGridSpec(
            num_scalar_prefetch=3,
            grid=(2,),
            in_specs=[
                pl.BlockSpec(
                    (heads, quarter, dim), lambda i, t, n, h: (0, quarter_of(i, 1, h[0]), 0)
                ),
                pl.BlockSpec(
                    (heads, quarter, dim), lambda i, t, n, h: (0, quarter_of(i, 0, h[0]), 0)
                ),
                whole(w_out.shape),
            ]
            + [pl.BlockSpec(memory_space=ANY)] * 5,
            out_specs=[whole((2, quarter, width))] * 2,
            scratch_shapes=[
                pltpu.VMEM((total_len, dim), BF16),
                pltpu.VMEM((total_len, dim), BF16),
                pltpu.SemaphoreType.DMA((2, n_pages + 1)),
            ],
        ),
        out_shape=[jax.ShapeDtypeStruct((2, quarter, width), BF16)] * 2,
        name="attend",
    )(*scalars, queries, queries, w_out, kv_pool, fresh, via_chip, via_core, via_both)

    core_pairs = pairs(((0, 1), (1, 0), (2, 3), (3, 2)))
    chip_pairs = pairs(((0, 2), (1, 3), (2, 0), (3, 1)))
    partner = lax.ppermute(send, AXES, core_pairs)
    pair_sum = (mine[0].astype(F32) + partner[0].astype(F32)).astype(BF16)
    far = lax.ppermute(pair_sum, AXES, chip_pairs)

    mixed = pl.pallas_call(
        post_kernel,
        grid_spec=pltpu.PrefetchScalarGridSpec(
            num_scalar_prefetch=1,
            grid=(1,),
            in_specs=[
                pl.BlockSpec((quarter, width), lambda i, h: (h[0], 0)),
                pl.BlockSpec((quarter, width), lambda i, h: (h[0], 0)),
                pl.BlockSpec((1, quarter, width), lambda i, h: (1, 0, 0)),
                pl.BlockSpec((1, quarter, width), lambda i, h: (1, 0, 0)),
                whole((quarter, width)),
                whole(layer_input.shape),
                whole((1, width)),
                whole(laurel_left.shape[::-1]),
                whole(laurel_right.shape),
                whole((1, width)),
                whole(w_plgate.shape),
                whole(w_plproj.shape),
                whole((1, width)),
            ],
            out_specs=whole((quarter, width)),
        ),
        out_shape=jax.ShapeDtypeStruct((quarter, width), BF16),
        name="post",
    )(
        scalars[2], hidden_in, normed, mine, partner, far, layer_input, post_gain, laurel_left.T,
        laurel_right, laurel_gain, w_plgate, w_plproj, pl_gain,
    )

    arranged = pl.pallas_call(
        permute_kernel,
        grid_spec=pltpu.PrefetchScalarGridSpec(
            num_scalar_prefetch=1,
            grid=(1,),
            in_specs=[whole(spread.shape), pl.BlockSpec(memory_space=ANY)],
            out_specs=whole(spread.shape),
        ),
        out_shape=jax.ShapeDtypeStruct(spread.shape, spread.dtype),
        name="permute",
    )(decode_owner, spread, pair_sum)
    owned = lax.all_to_all(arranged, "blk", 0, 0, tiled=True)
    return mixed, owned.reshape(1, 1, total_len, dim)


def solution(mesh):
    in_specs = (
        P("blk", None),
        P(("blk", "head"), None),
        P(),
        P(None, "head"),
        P(None, "head"),
        P(),
        P(),
        P("head", None),
        P(),
        P(),
        P(),
        P(),
        P(),
        P(),
        P(),
        P("blk", None, None, None),
        P("blk", None),
        P("blk"),
        P(),
    )
    out_specs = (P(("blk", "head"), None), P("head", "blk", None, None))
    return jax.shard_map(
        on_device, mesh=mesh, in_specs=in_specs, out_specs=out_specs, check_vma=False
    )
```

time: 176 us -> 141 us (0.80)
  Pallas kernels: 65.8 us -> 32.1 us
  other arithmetic: 5.45 us -> 2.84 us
    pallas_call x1, Pallas kernels: 33.5 us -> 2.98 us  [on_device(): pl.pallas_call(permute_kernel, grid_spec=pltpu.PrefetchScalarGridSpec(num...]
    pallas_call x1, Pallas kernels: 13.8 us -> 12 us  [on_device(): pl.pallas_call(functools.partial(attend_kernel, n_pages=n_pages, page=pag...]
    sin x1 -> x0, other arithmetic: 1.8 us -> none  [on_device(): cosine, sine = (jnp.cos(angles), jnp.sin(angles))]
  transfers between devices with their start and end apart: 7 -> 7, of which waited for: 5 -> 5; matrix products, arithmetic and copies ran while one was open for 1% -> 2% of each run, Pallas kernels for 14% -> 16%
where the time goes in v2:
time: 141 us; the launch traced here: 140 us
  waiting for transfers between devices  63.4 us (45%)
  starting transfers between devices  36.9 us (26%)
  Pallas kernels  32.1 us (23%)
  local copies, waits for them, and re-layouts  3.46 us (2%)
  other arithmetic  2.84 us (2%)
    ppermute x1, waiting for transfers between devices, on_device(): far = lax.ppermute(pair_sum, AXES, chip_pairs)  39.6 us
    ppermute x1, waiting for transfers between devices, on_device(): via_chip = lax.ppermute(fresh, AXES, pairs(((1, 3), (2, 0))))  15.2 us
    all_to_all x1, starting transfers between devices, on_device(): lax.all_to_all(full_seq.reshape(blocks, total_len // blocks, dim), 'blk',...  12.7 us
    pallas_call x1, Pallas kernels, on_device(): pl.pallas_call(functools.partial(attend_kernel, n_pages=n_pages, page=pag...  12 us
    all_to_all x1, starting transfers between devices, on_device(): owned = lax.all_to_all(arranged, 'blk', 0, 0, tiled=True)  10.2 us
    pallas_call x1, Pallas kernels, on_device(): pl.pallas_call(functools.partial(prep_kernel, n_pages=n_pages, page=page,...  7.4 us
    ppermute x1, starting transfers between devices, on_device(): via_chip = lax.ppermute(fresh, AXES, pairs(((1, 3), (2, 0))))  6.13 us
    pallas_call x1, Pallas kernels, on_device(): pl.pallas_call(post_kernel, grid_spec=pltpu.PrefetchScalarGridSpec(num_sc...  5.37 us
  transfers between devices with their start and end apart: 7, of which 5 were waited for; matrix products, arithmetic and copies ran while one was open for 2% of the time, Pallas kernels for 16%

profile of v2, /device:TPU:1, one launch (start us, length us, event | category | flops | bytes accessed | tf_op | source)
XLA Modules:
  0.0 140.1 jit_solution(7249873879459295630)
XLA Ops:
  0.6 0.5 multiply_power_fusion.frequency
  1.8 7.4 %prep.1 = (bf16[512,2048]{1,0:T(8,128)(2,1)}, bf16[512,256]{1,0:T(8,128)(2,1)}, bf16[2048,256]{1,0:T(8,128)(2,1)}, f32[512,128]{1,0:T(8,128)}, f32[512,128]{1,0:T(8,128)}) custom-call(s32[12]{0:T(128)} %bitcast.20, s32[1]{0:T(128)S(6)} %copy.22.prefix_len, s32[1]{0:T(128)} %bitcast.head_at, bf16[512,2048]{1,0:T(8,128)(2,1)} %hidden.3, f32[1,2048]{1,0:T(1,128)} %bitcast.16, ...), custom_call_target="tpu_custom_call" | custom-call | tf_op jit(solution)/shard_map/prep/pallas_call | solution.py:236
  9.2 0.0 copy-start.4
  9.2 12.7 %all-to-all-start = ((bf16[64,32,256]{2,1,0:T(8,128)(2,1)}), bf16[64,32,256]{2,1,0:T(8,128)(2,1)S(1)}, u32[]{:S(2)}, u32[]{:S(2)}) async-start(bf16[64,32,256]{2,1,0:T(8,128)(2,1)} %bitcast.14), calls=%async_computation | async-start | bytes 2097152 | tf_op jit(solution)/shard_map/all_to_all | solution.py:280
  21.9 0.0 copy-done.4
  21.9 6.1 %collective-permute-start = (bf16[512,256]{1,0:T(8,128)(2,1)S(1)}, bf16[512,256]{1,0:T(8,128)(2,1)S(1)}, u32[]{:S(2)}, u32[]{:S(2)}) collective-permute-start(bf16[512,256]{1,0:T(8,128)(2,1)S(1)} %copy-done.4), channel_id=1, source_target_pairs={{1,3},{2,0},{5,7},{6,4},{9,11},{10,8},{13,15},{14,12},{17,19},{18,... | collective-permute-start | bytes 786440 | tf_op jit(solution)/shard_map/ppermute | solution.py:277
  28.1 1.3 collective-permute-start.1
  29.4 15.2 %collective-permute-done.via_chip = bf16[512,256]{1,0:T(8,128)(2,1)S(1)} collective-permute-done((bf16[512,256]{1,0:T(8,128)(2,1)S(1)}, bf16[512,256]{1,0:T(8,128)(2,1)S(1)}, u32[]{:S(2)}, u32[]{:S(2)}) %collective-permute-start) | collective-permute-done | bytes 262176 | tf_op jit(solution)/shard_map/ppermute | solution.py:277
  44.6 0.0 copy-start.5
  44.6 1.3 collective-permute-start.2
  45.9 4.4 %query.1.near_q.far_q = bf16[2,512,256]{2,1,0:T(8,128)(2,1)} custom-call(bf16[512,2048]{1,0:T(8,128)(2,1)} %get-tuple-element.9.normed, bf16[2048,512]{1,0:T(8,128)(2,1)} %w_q.1, f32[1,256]{1,0:T(1,128)} %bitcast.23, f32[512,128]{1,0:T(8,128)} %get-tuple-element.10.cosine, f32[512,128]{1,0:T(8,128)} %get-tuple-element.11.sine), custom_call_target="tpu_custom_call" | custom-call | tf_op jit(solution)/shard_map/query/pallas_call | solution.py:284
  50.3 0.0 copy-done.5
  50.3 0.0 collective-permute-done.1.via_core
  50.3 0.0 copy-start.6
  50.3 1.9 %collective-permute-done.2.via_both = bf16[512,256]{1,0:T(8,128)(2,1)S(1)} collective-permute-done((bf16[512,256]{1,0:T(8,128)(2,1)S(1)}, bf16[512,256]{1,0:T(8,128)(2,1)S(1)}, u32[]{:S(2)}, u32[]{:S(2)}) %collective-permute-start.2) | collective-permute-done | bytes 262176 | tf_op jit(solution)/shard_map/ppermute | solution.py:279
  52.2 0.0 copy-done.6
  52.3 0.0 copy-start.7
  52.3 0.7 copy-done.7
  53.0 12.0 %attend.1 = (bf16[2,128,2048]{2,1,0:T(8,128)(2,1)}, bf16[2,128,2048]{2,1,0:T(8,128)(2,1)}) custom-call(s32[12]{0:T(128)} %bitcast.21, s32[1]{0:T(128)S(6)} %copy.22.prefix_len, s32[1]{0:T(128)} %bitcast.head_at, bf16[2,512,256]{2,1,0:T(8,128)(2,1)} %query.1.near_q.far_q, bf16[2,512,256]{2,1,0:T(8,128)(2,1)} %query.1.near_q.far_q, bf16[512,2048]{1,0:T(8,128)(2,1)} %w_out.1, ...), custom_call_target="tpu_custom_call" | custom-call | tf_op jit(solution)/shard_map/attend/pallas_call | solution.py:299
  64.9 4.2 %collective-permute-start.3 = (bf16[2,128,2048]{2,1,0:T(8,128)(2,1)}, bf16[2,128,2048]{2,1,0:T(8,128)(2,1)S(1)}, u32[]{:S(2)}, u32[]{:S(2)}) collective-permute-start(bf16[2,128,2048]{2,1,0:T(8,128)(2,1)} %get-tuple-element.14), channel_id=1, source_target_pairs={{0,1},{1,0},{2,3},{3,2},{4,5},{5,4},{6,7},{7,6},{8,9},{9,8},{10,11... | collective-permute-start | bytes 3145736 | tf_op jit(solution)/shard_map/ppermute | solution.py:329
  69.1 2.5 %collective-permute-done.3.partner = bf16[2,128,2048]{2,1,0:T(8,128)(2,1)S(1)} collective-permute-done((bf16[2,128,2048]{2,1,0:T(8,128)(2,1)}, bf16[2,128,2048]{2,1,0:T(8,128)(2,1)S(1)}, u32[]{:S(2)}, u32[]{:S(2)}) %collective-permute-start.3) | collective-permute-done | bytes 1048608 | tf_op jit(solution)/shard_map/ppermute | solution.py:329
  71.6 0.0 copy-start.1
  71.6 2.3 %fusion.after = bf16[128,2048]{1,0:T(8,128)(2,1)} fusion(bf16[2,128,2048]{2,1,0:T(8,128)(2,1)S(1)} %collective-permute-done.3.partner, bf16[2,128,2048]{2,1,0:T(8,128)(2,1)} %get-tuple-element.13.mine), kind=kLoop, calls=%fused_computation.1 | loop fusion | flops 1048576 | bytes 1572864 | tf_op jit(solution)/shard_map/convert_element_type | solution.py:330
  74.0 0.0 copy-start.2
  74.0 0.0 all-to-all-done.spread
  74.0 0.0 copy-start
  74.0 1.0 copy-done
  74.9 3.0 %permute.1 = bf16[64,32,256]{2,1,0:T(8,128)(2,1)} custom-call(s32[64]{0:T(128)} %owner.1, bf16[64,32,256]{2,1,0:T(8,128)(2,1)} %copy-done, bf16[128,2048]{1,0:T(8,128)(2,1)} %fusion.after), custom_call_target="tpu_custom_call" | custom-call | tf_op jit(solution)/shard_map/permute/pallas_call | solution.py:362
  77.9 0.0 copy-done.1
  77.9 10.2 %all-to-all-start.1 = ((bf16[64,32,256]{2,1,0:T(8,128)(2,1)}), bf16[64,32,256]{2,1,0:T(8,128)(2,1)S(1)}, u32[]{:S(2)}, u32[]{:S(2)}) async-start(bf16[64,32,256]{2,1,0:T(8,128)(2,1)} %permute.1), calls=%async_computation.1 | async-start | bytes 2097152 | tf_op jit(solution)/shard_map/all_to_all | solution.py:373
  88.1 0.0 copy-done.2
  88.1 1.0 collective-permute-start.4
  89.2 39.6 %collective-permute-done.4.far = bf16[128,2048]{1,0:T(8,128)(2,1)S(1)} collective-permute-done((bf16[128,2048]{1,0:T(8,128)(2,1)S(1)}, bf16[128,2048]{1,0:T(8,128)(2,1)S(1)}, u32[]{:S(2)}, u32[]{:S(2)}) %collective-permute-start.4) | collective-permute-done | bytes 524320 | tf_op jit(solution)/shard_map/ppermute | solution.py:331
  128.8 0.0 copy-start.3
  128.8 0.8 copy-done.3
  129.6 5.4 %post.1 = bf16[128,2048]{1,0:T(8,128)(2,1)} custom-call(s32[1]{0:T(128)} %bitcast.head_at, bf16[512,2048]{1,0:T(8,128)(2,1)} %hidden.3, bf16[512,2048]{1,0:T(8,128)(2,1)} %get-tuple-element.9.normed, bf16[2,128,2048]{2,1,0:T(8,128)(2,1)} %get-tuple-element.13.mine, bf16[2,128,2048]{2,1,0:T(8,128)(2,1)} %copy-done.1, bf16[128,2048]{1,0:T(8,128)(2,1)} %copy-done.3, ...), custom_call_target="tpu_custom_call" | custom-call | tf_op jit(solution)/shard_map/post/pallas_call | solution.py:333
  134.9 4.2 %all-to-all-done.1 = bf16[64,32,256]{2,1,0:T(8,128)(2,1)S(1)} async-done(((bf16[64,32,256]{2,1,0:T(8,128)(2,1)}), bf16[64,32,256]{2,1,0:T(8,128)(2,1)S(1)}, u32[]{:S(2)}, u32[]{:S(2)}) %all-to-all-start.1) | async-done | bytes 1048608 | tf_op jit(solution)/shard_map/all_to_all | solution.py:373
  139.1 1.0 copy.23
Async XLA Ops:
  9.2 12.7 %copy-start.4 = (bf16[512,256]{1,0:T(8,128)(2,1)S(1)}, bf16[512,256]{1,0:T(8,128)(2,1)}, u32[]{:S(2)}) copy-start(bf16[512,256]{1,0:T(8,128)(2,1)} %get-tuple-element.12.fresh) | copy-start | bytes 786436
  9.2 64.7 %all-to-all-start = ((bf16[64,32,256]{2,1,0:T(8,128)(2,1)}), bf16[64,32,256]{2,1,0:T(8,128)(2,1)S(1)}, u32[]{:S(2)}, u32[]{:S(2)}) async-start(bf16[64,32,256]{2,1,0:T(8,128)(2,1)} %bitcast.14), calls=%async_computation | async-start | bytes 2097152 | tf_op jit(solution)/shard_map/all_to_all | solution.py:280
  21.9 22.7 %collective-permute-start = (bf16[512,256]{1,0:T(8,128)(2,1)S(1)}, bf16[512,256]{1,0:T(8,128)(2,1)S(1)}, u32[]{:S(2)}, u32[]{:S(2)}) collective-permute-start(bf16[512,256]{1,0:T(8,128)(2,1)S(1)} %copy-done.4), channel_id=1, source_target_pairs={{1,3},{2,0},{5,7},{6,4},{9,11},{10,8},{13,15},{14,12},{17,19},{18,... | collective-permute-start | bytes 786440 | tf_op jit(solution)/shard_map/ppermute | solution.py:277
  28.1 22.3 %collective-permute-start.1 = (bf16[512,256]{1,0:T(8,128)(2,1)S(1)}, bf16[512,256]{1,0:T(8,128)(2,1)S(1)}, u32[]{:S(2)}, u32[]{:S(2)}) collective-permute-start(bf16[512,256]{1,0:T(8,128)(2,1)S(1)} %copy-done.4), channel_id=1, source_target_pairs={{0,1},{3,2},{4,5},{7,6},{8,9},{11,10},{12,13},{15,14},{16,17},{19,... | collective-permute-start | bytes 786440 | tf_op jit(solution)/shard_map/ppermute | solution.py:278
  44.6 5.7 %copy-start.5 = (bf16[512,256]{1,0:T(8,128)(2,1)}, bf16[512,256]{1,0:T(8,128)(2,1)S(1)}, u32[]{:S(2)}) copy-start(bf16[512,256]{1,0:T(8,128)(2,1)S(1)} %collective-permute-done.via_chip) | copy-start | bytes 786436
  44.6 7.6 %collective-permute-start.2 = (bf16[512,256]{1,0:T(8,128)(2,1)S(1)}, bf16[512,256]{1,0:T(8,128)(2,1)S(1)}, u32[]{:S(2)}, u32[]{:S(2)}) collective-permute-start(bf16[512,256]{1,0:T(8,128)(2,1)S(1)} %collective-permute-done.via_chip), channel_id=1, source_target_pairs={{0,1},{3,2},{4,5},{7,6},{8,9},{11,10},{12,13},{15,14},{16,17},{19,... | collective-permute-start | bytes 786440 | tf_op jit(solution)/shard_map/ppermute | solution.py:279
  50.3 1.9 %copy-start.6 = (bf16[512,256]{1,0:T(8,128)(2,1)}, bf16[512,256]{1,0:T(8,128)(2,1)S(1)}, u32[]{:S(2)}) copy-start(bf16[512,256]{1,0:T(8,128)(2,1)S(1)} %collective-permute-done.1.via_core) | copy-start | bytes 786436
  52.3 0.7 copy-start.7
  64.9 6.7 %collective-permute-start.3 = (bf16[2,128,2048]{2,1,0:T(8,128)(2,1)}, bf16[2,128,2048]{2,1,0:T(8,128)(2,1)S(1)}, u32[]{:S(2)}, u32[]{:S(2)}) collective-permute-start(bf16[2,128,2048]{2,1,0:T(8,128)(2,1)} %get-tuple-element.14), channel_id=1, source_target_pairs={{0,1},{1,0},{2,3},{3,2},{4,5},{5,4},{6,7},{7,6},{8,9},{9,8},{10,11... | collective-permute-start | bytes 3145736 | tf_op jit(solution)/shard_map/ppermute | solution.py:329
  71.6 6.3 %copy-start.1 = (bf16[2,128,2048]{2,1,0:T(8,128)(2,1)}, bf16[2,128,2048]{2,1,0:T(8,128)(2,1)S(1)}, u32[]{:S(2)}) copy-start(bf16[2,128,2048]{2,1,0:T(8,128)(2,1)S(1)} %collective-permute-done.3.partner) | copy-start | bytes 3145732
  74.0 14.2 %copy-start.2 = (bf16[128,2048]{1,0:T(8,128)(2,1)S(1)}, bf16[128,2048]{1,0:T(8,128)(2,1)}, u32[]{:S(2)}) copy-start(bf16[128,2048]{1,0:T(8,128)(2,1)} %fusion.after) | copy-start | bytes 1572868
  74.0 1.0 copy-start
  77.9 61.2 %all-to-all-start.1 = ((bf16[64,32,256]{2,1,0:T(8,128)(2,1)}), bf16[64,32,256]{2,1,0:T(8,128)(2,1)S(1)}, u32[]{:S(2)}, u32[]{:S(2)}) async-start(bf16[64,32,256]{2,1,0:T(8,128)(2,1)} %permute.1), calls=%async_computation.1 | async-start | bytes 2097152 | tf_op jit(solution)/shard_map/all_to_all | solution.py:373
  88.1 40.6 %collective-permute-start.4 = (bf16[128,2048]{1,0:T(8,128)(2,1)S(1)}, bf16[128,2048]{1,0:T(8,128)(2,1)S(1)}, u32[]{:S(2)}, u32[]{:S(2)}) collective-permute-start(bf16[128,2048]{1,0:T(8,128)(2,1)S(1)} %copy-done.2), channel_id=1, source_target_pairs={{0,2},{1,3},{2,0},{3,1},{4,6},{5,7},{6,4},{7,5},{8,10},{9,11},{10,... | collective-permute-start | bytes 1572872 | tf_op jit(solution)/shard_map/ppermute | solution.py:331
  128.8 0.8 copy-start.3

commit v3 on v2

--- a/solution.py
+++ b/solution.py
@@ -99,61 +99,58 @@
 
 
 def attend_kernel(
-    table, prefix_len, head_at, near_q, far_q, w_out, pool, fresh, via_chip, via_core, via_both,
-    send, mine, keys, vals, sem, *, n_pages, page, kv_heads, group,
+    table, prefix_len, head_at, send_q, mine_q, w_out, pool, fresh, via_chip, via_core, via_both,
+    send, mine, keys, vals, sem, *, own_chip, n_pages, page, kv_heads, group,
 ):
-    step = pl.program_id(0)
     head = head_at[0]
     length = prefix_len[0]
-    heads, tile, _ = near_q.shape
+    heads, tile, _ = send_q.shape
     kv_of = head * heads // group
     prefix = n_pages * page
     rows = fresh.shape[0]
 
-    @pl.when(step == 0)
-    def _():
-        copies = []
+    copies = []
+    for i, buf, slot in ((0, keys, kv_of), (1, vals, kv_of + kv_heads)):
         for p in range(n_pages):
-            for i, buf, slot in ((0, keys, kv_of), (1, vals, kv_of + kv_heads)):
-                copies.append(
-                    pltpu.make_async_copy(
-                        pool.at[table[p], slot], buf.at[pl.ds(p * page, page)], sem.at[i, p]
-                    )
+            copies.append(
+                pltpu.make_async_copy(
+                    pool.at[table[p], slot], buf.at[pl.ds(p * page, page)], sem.at[i, p]
                 )
-        for copy in copies:
-            copy.start()
-        sources = (
-            (fresh, via_chip),
-            (via_core, via_both),
-            (via_both, via_core),
-            (via_chip, fresh),
-        )
-        for h, (key_src, val_src) in enumerate(sources):
-
-            @pl.when(head == h)
-            def _():
-                new_key = pltpu.make_async_copy(
-                    key_src, keys.at[pl.ds(prefix, rows)], sem.at[0, n_pages]
-                )
-                new_val = pltpu.make_async_copy(
-                    val_src, vals.at[pl.ds(prefix, rows)], sem.at[1, n_pages]
-                )
-                new_key.start()
-                new_val.start()
-                new_key.wait()
-                new_val.wait()
-
-        for copy in copies:
-            copy.wait()
+            )
+    for copy in copies:
+        copy.start()
+    sources = (
+        (fresh, via_chip),
+        (via_core, via_both),
+        (via_both, via_core),
+        (via_chip, fresh),
+    )
+    for h, (key_src, val_src) in enumerate(sources):
+
+        @pl.when(head == h)
+        def _():
+            new_key = pltpu.make_async_copy(
+                key_src, keys.at[pl.ds(prefix, rows)], sem.at[0, n_pages]
+            )
+            new_val = pltpu.make_async_copy(
+                val_src, vals.at[pl.ds(prefix, rows)], sem.at[1, n_pages]
+            )
+            new_key.start()
+            new_val.start()
+            new_key.wait()
+            new_val.wait()
+
+    for copy in copies:
+        copy.wait()
 
     col = lax.broadcasted_iota(jnp.int32, (1, prefix + rows), 1)
     lowest = jnp.where(col < prefix, jnp.where(col < length, -1, rows), col - prefix)
     row = lax.broadcasted_iota(jnp.int32, (tile, 1), 0)
     attns = [[], []]
     for h in range(heads):
-        both = jnp.concatenate([far_q[h], near_q[h]], axis=0)
+        both = jnp.concatenate([send_q[h], mine_q[h]], axis=0)
         token = jnp.concatenate(
-            [quarter_of(step, i, head) * tile + row for i in range(2)], axis=0
+            [quarter_of(own_chip, i, head) * tile + row for i in range(2)], axis=0
         )
         scores = jnp.where(lowest <= token, dot_t(both, keys[...]), -jnp.inf)
         top = jnp.max(scores, axis=1, keepdims=True)
@@ -162,30 +159,21 @@
         attns[h] = (dot(expo.astype(BF16), vals[...]) / total).astype(BF16)
     part = dot(jnp.concatenate(attns, axis=1), w_out[...]).astype(BF16)
 
-    @pl.when(step == 0)
-    def _():
-        send[0] = part[:tile]
-        send[1] = part[tile:]
-
-    @pl.when(step == 1)
-    def _():
-        mine[0] = part[:tile]
-        mine[1] = part[tile:]
-
-
-def quarter_of(step, own_chip, head):
-    core = head % 2
-    chip = head // 2
-    to_core = jnp.where(step == 0, 1 - core, core)
-    to_chip = chip if own_chip else 1 - chip
-    return to_chip * 2 + to_core
+    send[...] = part[:tile]
+    mine[...] = part[tile:]
+
+
+def quarter_of(own_chip, own_core, head):
+    core = head % 2 if own_core else 1 - head % 2
+    chip = head // 2 if own_chip else 1 - head // 2
+    return chip * 2 + core
 
 
 def post_kernel(
     head_at, hidden, normed, mine, partner, far, plane, post_gain, left, right, laurel_gain,
     gate, proj, pl_gain, mixed,
 ):
-    total = mine[0].astype(F32) + partner[0].astype(F32) + far[...].astype(F32)
+    total = mine[...].astype(F32) + partner[...].astype(F32) + far[...].astype(F32)
     low = dot_t(normed[...], left[...]).astype(BF16)
     laurel = normed[...].astype(F32) + rms_scale(dot(low, right[...])) * laurel_gain[...]
     state = (hidden[...].astype(F32) + rms_scale(total) * post_gain[...] + laurel) * 2.0 ** (-0.5)
@@ -296,39 +284,42 @@
         name="query",
     )(normed, w_query, q_gain, cosine, sine)
 
-    send, mine = pl.pallas_call(
-        functools.partial(
-            attend_kernel, n_pages=n_pages, page=page, kv_heads=kv_heads, group=group
-        ),
-        grid_spec=pltpu.PrefetchScalarGridSpec(
-            num_scalar_prefetch=3,
-            grid=(2,),
-            in_specs=[
-                pl.BlockSpec(
-                    (heads, quarter, dim), lambda i, t, n, h: (0, quarter_of(i, 1, h[0]), 0)
-                ),
-                pl.BlockSpec(
-                    (heads, quarter, dim), lambda i, t, n, h: (0, quarter_of(i, 0, h[0]), 0)
-                ),
-                whole(w_out.shape),
-            ]
-            + [pl.BlockSpec(memory_space=ANY)] * 5,
-            out_specs=[whole((2, quarter, width))] * 2,
-            scratch_shapes=[
-                pltpu.VMEM((total_len, dim), BF16),
-                pltpu.VMEM((total_len, dim), BF16),
-                pltpu.SemaphoreType.DMA((2, n_pages + 1)),
-            ],
-        ),
-        out_shape=[jax.ShapeDtypeStruct((2, quarter, width), BF16)] * 2,
-        name="attend",
-    )(*scalars, queries, queries, w_out, kv_pool, fresh, via_chip, via_core, via_both)
+    def attend(own_chip):
+        def query_spec(own_core):
+            return pl.BlockSpec(
+                (heads, quarter, dim),
+                lambda i, t, n, h: (0, quarter_of(own_chip, own_core, h[0]), 0),
+            )
+
+        return pl.pallas_call(
+            functools.partial(
+                attend_kernel, own_chip=own_chip, n_pages=n_pages, page=page,
+                kv_heads=kv_heads, group=group,
+            ),
+            grid_spec=pltpu.PrefetchScalarGridSpec(
+                num_scalar_prefetch=3,
+                grid=(1,),
+                in_specs=[query_spec(False), query_spec(True), whole(w_out.shape)]
+                + [pl.BlockSpec(memory_space=ANY)] * 5,
+                out_specs=[whole((quarter, width))] * 2,
+                scratch_shapes=[
+                    pltpu.VMEM((total_len, dim), BF16),
+                    pltpu.VMEM((total_len, dim), BF16),
+                    pltpu.SemaphoreType.DMA((2, n_pages + 1)),
+                ],
+            ),
+            out_shape=[jax.ShapeDtypeStruct((quarter, width), BF16)] * 2,
+            name="attend_own" if own_chip else "attend_other",
+        )(*scalars, queries, queries, w_out, kv_pool, fresh, via_chip, via_core, via_both)
 
     core_pairs = pairs(((0, 1), (1, 0), (2, 3), (3, 2)))
     chip_pairs = pairs(((0, 2), (1, 3), (2, 0), (3, 1)))
+    send, mine = attend(False)
     partner = lax.ppermute(send, AXES, core_pairs)
-    pair_sum = (mine[0].astype(F32) + partner[0].astype(F32)).astype(BF16)
+    pair_sum = (mine.astype(F32) + partner.astype(F32)).astype(BF16)
     far = lax.ppermute(pair_sum, AXES, chip_pairs)
+    send, mine = attend(True)
+    partner = lax.ppermute(send, AXES, core_pairs)
 
     mixed = pl.pallas_call(
         post_kernel,
@@ -338,8 +329,8 @@
             in_specs=[
                 pl.BlockSpec((quarter, width), lambda i, h: (h[0], 0)),
                 pl.BlockSpec((quarter, width), lambda i, h: (h[0], 0)),
-                pl.BlockSpec((1, quarter, width), lambda i, h: (1, 0, 0)),
-                pl.BlockSpec((1, quarter, width), lambda i, h: (1, 0, 0)),
+                whole((quarter, width)),
+                whole((quarter, width)),
                 whole((quarter, width)),
                 whole(layer_input.shape),
                 whole((1, width)),
@@ -369,7 +360,7 @@
         ),
         out_shape=jax.ShapeDtypeStruct(spread.shape, spread.dtype),
         name="permute",
-    )(decode_owner, spread, pair_sum)
+    )(decode_owner, spread, mine)
     owned = lax.all_to_all(arranged, "blk", 0, 0, tiled=True)
     return mixed, owned.reshape(1, 1, total_len, dim)
 

time: 141 us -> 128 us (0.908)
  the two profiles are of different devices: /device:TPU:1 before, /device:TPU:32 now
where the time goes in v3:
time: 128 us
  waiting for transfers between devices  43.4 us (34%)
  starting transfers between devices  40 us (31%)
  Pallas kernels  36.9 us (29%)
  local copies, waits for them, and re-layouts  4.13 us (3%)
  other arithmetic  1.69 us (1%)
  between operations  1.44 us (1%)
    ppermute x1, waiting for transfers between devices, on_device(): far = lax.ppermute(pair_sum, AXES, chip_pairs)  30.1 us
    all_to_all x1, starting transfers between devices, on_device(): owned = lax.all_to_all(arranged, 'blk', 0, 0, tiled=True)  18.5 us
    pallas_call x2, Pallas kernels, attend(): pl.pallas_call(functools.partial(attend_kernel, own_chip=own_chip, n_page...  16.7 us
    all_to_all x1, starting transfers between devices, on_device(): lax.all_to_all(full_seq.reshape(blocks, total_len // blocks, dim), 'blk',...  11.8 us
    ppermute x1, waiting for transfers between devices, on_device(): via_chip = lax.ppermute(fresh, AXES, pairs(((1, 3), (2, 0))))  11.7 us
    pallas_call x1, Pallas kernels, on_device(): pl.pallas_call(functools.partial(prep_kernel, n_pages=n_pages, page=page,...  7.39 us
    ppermute x1, starting transfers between devices, on_device(): via_core = lax.ppermute(fresh, AXES, pairs(((0, 1), (3, 2))))  6.03 us
    pallas_call x1, Pallas kernels, on_device(): pl.pallas_call(post_kernel, grid_spec=pltpu.PrefetchScalarGridSpec(num_sc...  5.36 us
  transfers between devices with their start and end apart: 8, of which 3 were waited for; matrix products, arithmetic and copies ran while one was open for 1% of the time, Pallas kernels for 21%

profile of v3, /device:TPU:32, one launch (start us, length us, event | category | flops | bytes accessed | tf_op | source)
XLA Modules:
  0.0 127.6 jit_solution(7023254768302432720)
XLA Ops:
  0.6 0.5 multiply_power_fusion.frequency
  1.8 7.4 %prep.1 = (bf16[512,2048]{1,0:T(8,128)(2,1)}, bf16[512,256]{1,0:T(8,128)(2,1)}, bf16[2048,256]{1,0:T(8,128)(2,1)}, f32[512,128]{1,0:T(8,128)}, f32[512,128]{1,0:T(8,128)}) custom-call(s32[12]{0:T(128)} %bitcast.18, s32[1]{0:T(128)S(6)} %copy.22.prefix_len, s32[1]{0:T(128)} %bitcast.head_at, bf16[512,2048]{1,0:T(8,128)(2,1)} %hidden.3, f32[1,2048]{1,0:T(1,128)} %bitcast.14, ...), custom_call_target="tpu_custom_call" | custom-call | tf_op jit(solution)/shard_map/prep/pallas_call | solution.py:224
  9.2 0.0 copy-start.1
  9.2 11.8 %all-to-all-start = ((bf16[64,32,256]{2,1,0:T(8,128)(2,1)}), bf16[64,32,256]{2,1,0:T(8,128)(2,1)S(1)}, u32[]{:S(2)}, u32[]{:S(2)}) async-start(bf16[64,32,256]{2,1,0:T(8,128)(2,1)} %bitcast.12), calls=%async_computation | async-start | bytes 2097152 | tf_op jit(solution)/shard_map/all_to_all | solution.py:268
  21.0 0.0 copy-done.1
  21.0 1.3 %collective-permute-start = (bf16[512,256]{1,0:T(8,128)(2,1)S(1)}, bf16[512,256]{1,0:T(8,128)(2,1)S(1)}, u32[]{:S(2)}, u32[]{:S(2)}) collective-permute-start(bf16[512,256]{1,0:T(8,128)(2,1)S(1)} %copy-done.1), channel_id=1, source_target_pairs={{1,3},{2,0},{5,7},{6,4},{9,11},{10,8},{13,15},{14,12},{17,19},{18,... | collective-permute-start | bytes 786440 | tf_op jit(solution)/shard_map/ppermute | solution.py:265
  22.3 6.0 %collective-permute-start.1 = (bf16[512,256]{1,0:T(8,128)(2,1)S(1)}, bf16[512,256]{1,0:T(8,128)(2,1)S(1)}, u32[]{:S(2)}, u32[]{:S(2)}) collective-permute-start(bf16[512,256]{1,0:T(8,128)(2,1)S(1)} %copy-done.1), channel_id=1, source_target_pairs={{0,1},{3,2},{4,5},{7,6},{8,9},{11,10},{12,13},{15,14},{16,17},{19,... | collective-permute-start | bytes 786440 | tf_op jit(solution)/shard_map/ppermute | solution.py:266
  28.4 11.7 %collective-permute-done.via_chip = bf16[512,256]{1,0:T(8,128)(2,1)S(1)} collective-permute-done((bf16[512,256]{1,0:T(8,128)(2,1)S(1)}, bf16[512,256]{1,0:T(8,128)(2,1)S(1)}, u32[]{:S(2)}, u32[]{:S(2)}) %collective-permute-start) | collective-permute-done | bytes 262176 | tf_op jit(solution)/shard_map/ppermute | solution.py:265
  40.1 0.0 copy-start.2
  40.1 1.3 %collective-permute-start.2 = (bf16[512,256]{1,0:T(8,128)(2,1)S(1)}, bf16[512,256]{1,0:T(8,128)(2,1)S(1)}, u32[]{:S(2)}, u32[]{:S(2)}) collective-permute-start(bf16[512,256]{1,0:T(8,128)(2,1)S(1)} %collective-permute-done.via_chip), channel_id=1, source_target_pairs={{0,1},{3,2},{4,5},{7,6},{8,9},{11,10},{12,13},{15,14},{16,17},{19,... | collective-permute-start | bytes 786440 | tf_op jit(solution)/shard_map/ppermute | solution.py:267
  41.4 4.4 %query.1.send_q.mine_q = bf16[2,512,256]{2,1,0:T(8,128)(2,1)} custom-call(bf16[512,2048]{1,0:T(8,128)(2,1)} %get-tuple-element.11.normed, bf16[2048,512]{1,0:T(8,128)(2,1)} %w_q.1, f32[1,256]{1,0:T(1,128)} %bitcast.22, f32[512,128]{1,0:T(8,128)} %get-tuple-element.12.cosine, f32[512,128]{1,0:T(8,128)} %get-tuple-element.13.sine), custom_call_target="tpu_custom_call" | custom-call | tf_op jit(solution)/shard_map/query/pallas_call | solution.py:272
  45.8 0.0 copy-done.2
  45.8 0.0 collective-permute-done.1.via_core
  45.8 0.0 copy-start.3
  45.8 0.0 collective-permute-done.2.via_both
  45.9 0.7 copy-done.3
  46.5 0.0 copy-start.4
  46.5 0.7 copy-done.4
  47.2 8.3 %attend_own.1 = (bf16[128,2048]{1,0:T(8,128)(2,1)}, bf16[128,2048]{1,0:T(8,128)(2,1)}) custom-call(s32[12]{0:T(128)} %bitcast.19, s32[1]{0:T(128)S(6)} %copy.22.prefix_len, s32[1]{0:T(128)} %bitcast.head_at, bf16[2,512,256]{2,1,0:T(8,128)(2,1)} %query.1.send_q.mine_q, bf16[2,512,256]{2,1,0:T(8,128)(2,1)} %query.1.send_q.mine_q, bf16[512,2048]{1,0:T(8,128)(2,1)} %w_out.3, ...), custom_call_target="tpu_custom_call" | custom-call | tf_op jit(solution)/shard_map/attend_own/pallas_call | solution.py:294
  55.5 0.0 all-to-all-done.spread
  55.6 0.0 copy-start
  55.6 1.0 copy-done
  56.5 3.0 %permute.1 = bf16[64,32,256]{2,1,0:T(8,128)(2,1)} custom-call(s32[64]{0:T(128)} %owner.1, bf16[64,32,256]{2,1,0:T(8,128)(2,1)} %copy-done, bf16[128,2048]{1,0:T(8,128)(2,1)} %get-tuple-element.15.mine.after), custom_call_target="tpu_custom_call" | custom-call | tf_op jit(solution)/shard_map/permute/pallas_call | solution.py:353
  59.5 18.5 %all-to-all-start.1 = ((bf16[64,32,256]{2,1,0:T(8,128)(2,1)}), bf16[64,32,256]{2,1,0:T(8,128)(2,1)S(1)}, u32[]{:S(2)}, u32[]{:S(2)}) async-start(bf16[64,32,256]{2,1,0:T(8,128)(2,1)} %permute.1), calls=%async_computation.1 | async-start | bytes 2097152 | tf_op jit(solution)/shard_map/all_to_all | solution.py:364
  78.0 0.0 copy-start.7
  78.0 8.4 %attend_other.1 = (bf16[128,2048]{1,0:T(8,128)(2,1)}, bf16[128,2048]{1,0:T(8,128)(2,1)}) custom-call(s32[12]{0:T(128)} %bitcast.20, s32[1]{0:T(128)S(6)} %copy.22.prefix_len, s32[1]{0:T(128)} %bitcast.head_at, bf16[2,512,256]{2,1,0:T(8,128)(2,1)} %query.1.send_q.mine_q, bf16[2,512,256]{2,1,0:T(8,128)(2,1)} %query.1.send_q.mine_q, bf16[512,2048]{1,0:T(8,128)(2,1)} %w_out.3, ...), custom_call_target="tpu_custom_call" | custom-call | tf_op jit(solution)/shard_map/attend_other/pallas_call | solution.py:294
  86.4 0.1 collective-permute-start.4
  86.5 0.0 copy-done.7
  86.5 0.5 collective-permute-start.3
  87.0 1.6 %collective-permute-done.4 = bf16[128,2048]{1,0:T(8,128)(2,1)S(1)} collective-permute-done((bf16[128,2048]{1,0:T(8,128)(2,1)}, bf16[128,2048]{1,0:T(8,128)(2,1)S(1)}, u32[]{:S(2)}, u32[]{:S(2)}) %collective-permute-start.4) | collective-permute-done | bytes 524320 | tf_op jit(solution)/shard_map/ppermute | solution.py:318
  88.6 1.2 add_convert_fusion
  89.8 0.5 collective-permute-start.5
  90.4 0.0 collective-permute-done.3.partner
  90.4 0.0 copy-start.5
  90.4 30.1 %collective-permute-done.5.far = bf16[128,2048]{1,0:T(8,128)(2,1)S(1)} collective-permute-done((bf16[128,2048]{1,0:T(8,128)(2,1)S(1)}, bf16[128,2048]{1,0:T(8,128)(2,1)S(1)}, u32[]{:S(2)}, u32[]{:S(2)}) %collective-permute-start.5) | collective-permute-done | bytes 524320 | tf_op jit(solution)/shard_map/ppermute | solution.py:320
  120.4 0.0 copy-start.6
  120.4 0.0 copy-done.5
  120.4 0.8 copy-done.6
  121.2 5.4 %post.1 = bf16[128,2048]{1,0:T(8,128)(2,1)} custom-call(s32[1]{0:T(128)} %bitcast.head_at, bf16[512,2048]{1,0:T(8,128)(2,1)} %hidden.3, bf16[512,2048]{1,0:T(8,128)(2,1)} %get-tuple-element.11.normed, bf16[128,2048]{1,0:T(8,128)(2,1)} %get-tuple-element.15.mine.after, bf16[128,2048]{1,0:T(8,128)(2,1)} %copy-done.5, bf16[128,2048]{1,0:T(8,128)(2,1)} %copy-done.6, ...), custom_call_target="tpu_custom_call" | custom-call | tf_op jit(solution)/shard_map/post/pallas_call | solution.py:324
  126.6 0.0 all-to-all-done.1
  126.6 1.0 copy.23
Async XLA Ops:
  9.2 11.8 %copy-start.1 = (bf16[512,256]{1,0:T(8,128)(2,1)S(1)}, bf16[512,256]{1,0:T(8,128)(2,1)}, u32[]{:S(2)}) copy-start(bf16[512,256]{1,0:T(8,128)(2,1)} %get-tuple-element.14.fresh) | copy-start | bytes 786436
  9.2 46.3 %all-to-all-start = ((bf16[64,32,256]{2,1,0:T(8,128)(2,1)}), bf16[64,32,256]{2,1,0:T(8,128)(2,1)S(1)}, u32[]{:S(2)}, u32[]{:S(2)}) async-start(bf16[64,32,256]{2,1,0:T(8,128)(2,1)} %bitcast.12), calls=%async_computation | async-start | bytes 2097152 | tf_op jit(solution)/shard_map/all_to_all | solution.py:268
  21.0 19.1 %collective-permute-start = (bf16[512,256]{1,0:T(8,128)(2,1)S(1)}, bf16[512,256]{1,0:T(8,128)(2,1)S(1)}, u32[]{:S(2)}, u32[]{:S(2)}) collective-permute-start(bf16[512,256]{1,0:T(8,128)(2,1)S(1)} %copy-done.1), channel_id=1, source_target_pairs={{1,3},{2,0},{5,7},{6,4},{9,11},{10,8},{13,15},{14,12},{17,19},{18,... | collective-permute-start | bytes 786440 | tf_op jit(solution)/shard_map/ppermute | solution.py:265
  22.3 23.5 %collective-permute-start.1 = (bf16[512,256]{1,0:T(8,128)(2,1)S(1)}, bf16[512,256]{1,0:T(8,128)(2,1)S(1)}, u32[]{:S(2)}, u32[]{:S(2)}) collective-permute-start(bf16[512,256]{1,0:T(8,128)(2,1)S(1)} %copy-done.1), channel_id=1, source_target_pairs={{0,1},{3,2},{4,5},{7,6},{8,9},{11,10},{12,13},{15,14},{16,17},{19,... | collective-permute-start | bytes 786440 | tf_op jit(solution)/shard_map/ppermute | solution.py:266
  40.1 5.7 %copy-start.2 = (bf16[512,256]{1,0:T(8,128)(2,1)}, bf16[512,256]{1,0:T(8,128)(2,1)S(1)}, u32[]{:S(2)}) copy-start(bf16[512,256]{1,0:T(8,128)(2,1)S(1)} %collective-permute-done.via_chip) | copy-start | bytes 786436
  40.1 5.7 %collective-permute-start.2 = (bf16[512,256]{1,0:T(8,128)(2,1)S(1)}, bf16[512,256]{1,0:T(8,128)(2,1)S(1)}, u32[]{:S(2)}, u32[]{:S(2)}) collective-permute-start(bf16[512,256]{1,0:T(8,128)(2,1)S(1)} %collective-permute-done.via_chip), channel_id=1, source_target_pairs={{0,1},{3,2},{4,5},{7,6},{8,9},{11,10},{12,13},{15,14},{16,17},{19,... | collective-permute-start | bytes 786440 | tf_op jit(solution)/shard_map/ppermute | solution.py:267
  45.8 0.7 copy-start.3
  46.5 0.7 copy-start.4
  55.6 1.0 copy-start
  59.5 67.1 %all-to-all-start.1 = ((bf16[64,32,256]{2,1,0:T(8,128)(2,1)}), bf16[64,32,256]{2,1,0:T(8,128)(2,1)S(1)}, u32[]{:S(2)}, u32[]{:S(2)}) async-start(bf16[64,32,256]{2,1,0:T(8,128)(2,1)} %permute.1), calls=%async_computation.1 | async-start | bytes 2097152 | tf_op jit(solution)/shard_map/all_to_all | solution.py:364
  78.0 8.5 %copy-start.7 = (bf16[128,2048]{1,0:T(8,128)(2,1)S(1)}, bf16[128,2048]{1,0:T(8,128)(2,1)}, u32[]{:S(2)}) copy-start(bf16[128,2048]{1,0:T(8,128)(2,1)} %get-tuple-element.16) | copy-start | bytes 1572868
  86.4 2.2 %collective-permute-start.4 = (bf16[128,2048]{1,0:T(8,128)(2,1)}, bf16[128,2048]{1,0:T(8,128)(2,1)S(1)}, u32[]{:S(2)}, u32[]{:S(2)}) collective-permute-start(bf16[128,2048]{1,0:T(8,128)(2,1)} %get-tuple-element.18), channel_id=1, source_target_pairs={{0,1},{1,0},{2,3},{3,2},{4,5},{5,4},{6,7},{7,6},{8,9},{9,8},{10,11... | collective-permute-start | bytes 1572872 | tf_op jit(solution)/shard_map/ppermute | solution.py:318
  86.5 3.8 %collective-permute-start.3 = (bf16[128,2048]{1,0:T(8,128)(2,1)S(1)}, bf16[128,2048]{1,0:T(8,128)(2,1)S(1)}, u32[]{:S(2)}, u32[]{:S(2)}) collective-permute-start(bf16[128,2048]{1,0:T(8,128)(2,1)S(1)} %copy-done.7), channel_id=1, source_target_pairs={{0,1},{1,0},{2,3},{3,2},{4,5},{5,4},{6,7},{7,6},{8,9},{9,8},{10,11... | collective-permute-start | bytes 1572872 | tf_op jit(solution)/shard_map/ppermute | solution.py:322
  89.8 30.6 %collective-permute-start.5 = (bf16[128,2048]{1,0:T(8,128)(2,1)S(1)}, bf16[128,2048]{1,0:T(8,128)(2,1)S(1)}, u32[]{:S(2)}, u32[]{:S(2)}) collective-permute-start(bf16[128,2048]{1,0:T(8,128)(2,1)S(1)} %add_convert_fusion), channel_id=1, source_target_pairs={{0,2},{1,3},{2,0},{3,1},{4,6},{5,7},{6,4},{7,5},{8,10},{9,11},{10,... | collective-permute-start | bytes 1572872 | tf_op jit(solution)/shard_map/ppermute | solution.py:320
  90.4 30.1 %copy-start.5 = (bf16[128,2048]{1,0:T(8,128)(2,1)}, bf16[128,2048]{1,0:T(8,128)(2,1)S(1)}, u32[]{:S(2)}) copy-start(bf16[128,2048]{1,0:T(8,128)(2,1)S(1)} %collective-permute-done.3.partner) | copy-start | bytes 1572868
  120.4 0.8 copy-start.6

commit v4 on v3

--- a/solution.py
+++ b/solution.py
@@ -37,7 +37,7 @@
 
 def prep_kernel(
     table, prefix_len, head_at, hidden, in_gain, w_kv, k_gain, frequency, pool,
-    normed, fresh, seq, cosine, sine, fresh_all, old, sem, *, n_pages, page, rows, kv_heads,
+    normed, fresh, seq, cosine, sine, fresh_all, sem, *, n_pages, page, rows, kv_heads,
 ):
     step = pl.program_id(0)
     steps = pl.num_programs(0)
@@ -49,7 +49,7 @@
 
     def page_copy(p):
         return pltpu.make_async_copy(
-            pool.at[table[p], head], old.at[pl.ds(p * page, page)], sem.at[p]
+            pool.at[table[p], head], seq.at[pl.ds(p * page, page)], sem.at[p]
         )
 
     @pl.when(step == 0)
@@ -60,9 +60,15 @@
     values = (rms_scale(hidden[...].astype(F32)) * in_gain[...]).astype(BF16)
     normed[...] = values
     own = rms_scale(dot(values, w_kv[...]))
-    position = length + step * tile + lax.broadcasted_iota(jnp.int32, (tile, 1), 0)
-    angles = position.astype(F32) * frequency[...]
-    cos, sin = jnp.cos(angles), jnp.sin(angles)
+    fine = 16
+    at = lax.broadcasted_iota(jnp.int32, (tile // fine, 1), 0)
+    coarse_angle = (length + step * tile + at * fine).astype(F32) * frequency[...]
+    at = lax.broadcasted_iota(jnp.int32, (fine, 1), 0)
+    fine_angle = at.astype(F32) * frequency[...]
+    cos_a, sin_a = jnp.cos(coarse_angle)[:, None], jnp.sin(coarse_angle)[:, None]
+    cos_b, sin_b = jnp.cos(fine_angle)[None], jnp.sin(fine_angle)[None]
+    cos = (cos_a * cos_b - sin_a * sin_b).reshape(tile, -1)
+    sin = (sin_a * cos_b + cos_a * sin_b).reshape(tile, -1)
     cosine[...] = cos
     sine[...] = sin
     key = turn(own * k_gain[...], cos, sin)
@@ -75,9 +81,11 @@
         for p in range(n_pages):
             page_copy(p).wait()
         for p in range(n_pages):
-            at = p * page + lax.broadcasted_iota(jnp.int32, (page, 1), 0)
-            part = old[p * page : (p + 1) * page, :].astype(F32)
-            seq[p * page : (p + 1) * page, :] = jnp.where(at < length, part, 0.0).astype(BF16)
+
+            @pl.when(length <= p * page)
+            def _():
+                seq[p * page : (p + 1) * page, :] = jnp.zeros((page, seq.shape[1]), BF16)
+
         seq[prefix:total, :] = jnp.zeros((total - prefix, seq.shape[1]), BF16)
 
     @pl.when(step == steps - 1)
@@ -245,7 +253,6 @@
             ],
             scratch_shapes=[
                 pltpu.VMEM((rows, dim), BF16),
-                pltpu.VMEM((prefix, dim), BF16),
                 pltpu.SemaphoreType.DMA((n_pages,)),
             ],
         ),
@@ -360,7 +367,7 @@
         ),
         out_shape=jax.ShapeDtypeStruct(spread.shape, spread.dtype),
         name="permute",
-    )(decode_owner, spread, mine)
+    )(decode_owner, spread, pair_sum)
     owned = lax.all_to_all(arranged, "blk", 0, 0, tiled=True)
     return mixed, owned.reshape(1, 1, total_len, dim)
 

time: 128 us -> 136 us (1.062)
  the two profiles are of different devices: /device:TPU:32 before, /device:TPU:1 now
where the time goes in v4:
time: 136 us; the launch traced here: 135 us
  waiting for transfers between devices  53.8 us (40%)
  starting transfers between devices  37.4 us (28%)
  Pallas kernels  36.4 us (27%)
  local copies, waits for them, and re-layouts  3.44 us (3%)
  other arithmetic  2.48 us (2%)
  between operations  1.4 us (1%)
    ppermute x1, waiting for transfers between devices, on_device(): far = lax.ppermute(pair_sum, AXES, chip_pairs)  29.8 us
    pallas_call x2, Pallas kernels, attend(): pl.pallas_call(functools.partial(attend_kernel, own_chip=own_chip, n_page...  16.7 us
    ppermute x1, waiting for transfers between devices, on_device(): via_chip = lax.ppermute(fresh, AXES, pairs(((1, 3), (2, 0))))  15.2 us
    all_to_all x1, starting transfers between devices, on_device(): lax.all_to_all(full_seq.reshape(blocks, total_len // blocks, dim), 'blk',...  12.7 us
    all_to_all x1, starting transfers between devices, on_device(): owned = lax.all_to_all(arranged, 'blk', 0, 0, tiled=True)  10.2 us
    pallas_call x1, Pallas kernels, on_device(): pl.pallas_call(functools.partial(prep_kernel, n_pages=n_pages, page=page,...  6.94 us
    ppermute x1, starting transfers between devices, on_device(): via_chip = lax.ppermute(fresh, AXES, pairs(((1, 3), (2, 0))))  6.13 us
    pallas_call x1, Pallas kernels, on_device(): pl.pallas_call(post_kernel, grid_spec=pltpu.PrefetchScalarGridSpec(num_sc...  5.36 us
  transfers between devices with their start and end apart: 8, of which 6 were waited for; matrix products, arithmetic and copies ran while one was open for 1% of the time, Pallas kernels for 20%

profile of v4, /device:TPU:1, one launch (start us, length us, event | category | flops | bytes accessed | tf_op | source)
XLA Modules:
  0.0 134.8 jit_solution(10439811127599847804)
XLA Ops:
  0.6 0.5 multiply_power_fusion.frequency
  1.8 6.9 %prep.1 = (bf16[512,2048]{1,0:T(8,128)(2,1)}, bf16[512,256]{1,0:T(8,128)(2,1)}, bf16[2048,256]{1,0:T(8,128)(2,1)}, f32[512,128]{1,0:T(8,128)}, f32[512,128]{1,0:T(8,128)}) custom-call(s32[12]{0:T(128)} %bitcast.18, s32[1]{0:T(128)S(6)} %copy.22.prefix_len, s32[1]{0:T(128)} %bitcast.head_at, bf16[512,2048]{1,0:T(8,128)(2,1)} %hidden.3, f32[1,2048]{1,0:T(1,128)} %bitcast.14, ...), custom_call_target="tpu_custom_call" | custom-call | tf_op jit(solution)/shard_map/prep/pallas_call | solution.py:232
  8.8 0.0 copy-start.2
  8.8 12.7 %all-to-all-start = ((bf16[64,32,256]{2,1,0:T(8,128)(2,1)}), bf16[64,32,256]{2,1,0:T(8,128)(2,1)S(1)}, u32[]{:S(2)}, u32[]{:S(2)}) async-start(bf16[64,32,256]{2,1,0:T(8,128)(2,1)} %bitcast.12), calls=%async_computation | async-start | bytes 2097152 | tf_op jit(solution)/shard_map/all_to_all | solution.py:275
  21.5 0.0 copy-done.2
  21.5 6.1 %collective-permute-start = (bf16[512,256]{1,0:T(8,128)(2,1)S(1)}, bf16[512,256]{1,0:T(8,128)(2,1)S(1)}, u32[]{:S(2)}, u32[]{:S(2)}) collective-permute-start(bf16[512,256]{1,0:T(8,128)(2,1)S(1)} %copy-done.2), channel_id=1, source_target_pairs={{1,3},{2,0},{5,7},{6,4},{9,11},{10,8},{13,15},{14,12},{17,19},{18,... | collective-permute-start | bytes 786440 | tf_op jit(solution)/shard_map/ppermute | solution.py:272
  27.6 1.3 collective-permute-start.1
  28.9 15.2 %collective-permute-done.via_chip = bf16[512,256]{1,0:T(8,128)(2,1)S(1)} collective-permute-done((bf16[512,256]{1,0:T(8,128)(2,1)S(1)}, bf16[512,256]{1,0:T(8,128)(2,1)S(1)}, u32[]{:S(2)}, u32[]{:S(2)}) %collective-permute-start) | collective-permute-done | bytes 262176 | tf_op jit(solution)/shard_map/ppermute | solution.py:272
  44.2 0.0 copy-start.3
  44.2 1.3 collective-permute-start.2
  45.5 4.4 %query.1.send_q.mine_q = bf16[2,512,256]{2,1,0:T(8,128)(2,1)} custom-call(bf16[512,2048]{1,0:T(8,128)(2,1)} %get-tuple-element.11.normed, bf16[2048,512]{1,0:T(8,128)(2,1)} %w_q.1, f32[1,256]{1,0:T(1,128)} %bitcast.22, f32[512,128]{1,0:T(8,128)} %get-tuple-element.12.cosine, f32[512,128]{1,0:T(8,128)} %get-tuple-element.13.sine), custom_call_target="tpu_custom_call" | custom-call | tf_op jit(solution)/shard_map/query/pallas_call | solution.py:279
  49.9 0.0 copy-done.3
  49.9 0.0 collective-permute-done.1.via_core
  49.9 0.0 copy-start.4
  49.9 1.9 %collective-permute-done.2.via_both = bf16[512,256]{1,0:T(8,128)(2,1)S(1)} collective-permute-done((bf16[512,256]{1,0:T(8,128)(2,1)S(1)}, bf16[512,256]{1,0:T(8,128)(2,1)S(1)}, u32[]{:S(2)}, u32[]{:S(2)}) %collective-permute-start.2) | collective-permute-done | bytes 262176 | tf_op jit(solution)/shard_map/ppermute | solution.py:274
  51.8 0.0 copy-done.4
  51.8 0.0 copy-start.5
  51.8 0.7 copy-done.5
  52.5 8.3 %attend_other.1 = (bf16[128,2048]{1,0:T(8,128)(2,1)}, bf16[128,2048]{1,0:T(8,128)(2,1)}) custom-call(s32[12]{0:T(128)} %bitcast.19, s32[1]{0:T(128)S(6)} %copy.22.prefix_len, s32[1]{0:T(128)} %bitcast.head_at, bf16[2,512,256]{2,1,0:T(8,128)(2,1)} %query.1.send_q.mine_q, bf16[2,512,256]{2,1,0:T(8,128)(2,1)} %query.1.send_q.mine_q, bf16[512,2048]{1,0:T(8,128)(2,1)} %w_out.3, ...), custom_call_target="tpu_custom_call" | custom-call | tf_op jit(solution)/shard_map/attend_other/pallas_call | solution.py:301
  60.8 4.2 %collective-permute-start.4 = (bf16[128,2048]{1,0:T(8,128)(2,1)}, bf16[128,2048]{1,0:T(8,128)(2,1)S(1)}, u32[]{:S(2)}, u32[]{:S(2)}) collective-permute-start(bf16[128,2048]{1,0:T(8,128)(2,1)} %get-tuple-element.18), channel_id=1, source_target_pairs={{0,1},{1,0},{2,3},{3,2},{4,5},{5,4},{6,7},{7,6},{8,9},{9,8},{10,11... | collective-permute-start | bytes 1572872 | tf_op jit(solution)/shard_map/ppermute | solution.py:325
  65.0 1.7 %collective-permute-done.4 = bf16[128,2048]{1,0:T(8,128)(2,1)S(1)} collective-permute-done((bf16[128,2048]{1,0:T(8,128)(2,1)}, bf16[128,2048]{1,0:T(8,128)(2,1)S(1)}, u32[]{:S(2)}, u32[]{:S(2)}) %collective-permute-start.4) | collective-permute-done | bytes 524320 | tf_op jit(solution)/shard_map/ppermute | solution.py:325
  66.8 2.0 %add_convert_fusion.after = bf16[128,2048]{1,0:T(8,128)(2,1)} fusion(bf16[128,2048]{1,0:T(8,128)(2,1)S(1)} %collective-permute-done.4, bf16[128,2048]{1,0:T(8,128)(2,1)} %get-tuple-element.17), kind=kLoop, calls=%fused_computation | loop fusion | flops 1048576 | bytes 1572864 | tf_op jit(solution)/shard_map/convert_element_type | solution.py:326
  68.7 0.0 all-to-all-done.spread
  68.7 0.0 copy-start
  68.7 1.0 copy-done
  69.7 3.0 %permute.1 = bf16[64,32,256]{2,1,0:T(8,128)(2,1)} custom-call(s32[64]{0:T(128)} %owner.1, bf16[64,32,256]{2,1,0:T(8,128)(2,1)} %copy-done, bf16[128,2048]{1,0:T(8,128)(2,1)} %add_convert_fusion.after), custom_call_target="tpu_custom_call" | custom-call | tf_op jit(solution)/shard_map/permute/pallas_call | solution.py:360
  72.7 10.2 %all-to-all-start.1 = ((bf16[64,32,256]{2,1,0:T(8,128)(2,1)}), bf16[64,32,256]{2,1,0:T(8,128)(2,1)S(1)}, u32[]{:S(2)}, u32[]{:S(2)}) async-start(bf16[64,32,256]{2,1,0:T(8,128)(2,1)} %permute.1), calls=%async_computation.1 | async-start | bytes 2097152 | tf_op jit(solution)/shard_map/all_to_all | solution.py:371
  82.9 0.0 copy-start.1
  82.9 8.4 %attend_own.1 = (bf16[128,2048]{1,0:T(8,128)(2,1)}, bf16[128,2048]{1,0:T(8,128)(2,1)}) custom-call(s32[12]{0:T(128)} %bitcast.20, s32[1]{0:T(128)S(6)} %copy.22.prefix_len, s32[1]{0:T(128)} %bitcast.head_at, bf16[2,512,256]{2,1,0:T(8,128)(2,1)} %query.1.send_q.mine_q, bf16[2,512,256]{2,1,0:T(8,128)(2,1)} %query.1.send_q.mine_q, bf16[512,2048]{1,0:T(8,128)(2,1)} %w_out.3, ...), custom_call_target="tpu_custom_call" | custom-call | tf_op jit(solution)/shard_map/attend_own/pallas_call | solution.py:301
  91.3 0.7 collective-permute-start.3
  92.1 0.0 copy-done.1
  92.1 0.8 collective-permute-start.5
  92.8 1.0 collective-permute-done.3.partner
  93.8 0.0 copy-start.6
  93.8 29.8 %collective-permute-done.5.far = bf16[128,2048]{1,0:T(8,128)(2,1)S(1)} collective-permute-done((bf16[128,2048]{1,0:T(8,128)(2,1)S(1)}, bf16[128,2048]{1,0:T(8,128)(2,1)S(1)}, u32[]{:S(2)}, u32[]{:S(2)}) %collective-permute-start.5) | collective-permute-done | bytes 524320 | tf_op jit(solution)/shard_map/ppermute | solution.py:327
  123.6 0.0 copy-start.7
  123.6 0.0 copy-done.6
  123.6 0.8 copy-done.7
  124.4 5.4 %post.1 = bf16[128,2048]{1,0:T(8,128)(2,1)} custom-call(s32[1]{0:T(128)} %bitcast.head_at, bf16[512,2048]{1,0:T(8,128)(2,1)} %hidden.3, bf16[512,2048]{1,0:T(8,128)(2,1)} %get-tuple-element.11.normed, bf16[128,2048]{1,0:T(8,128)(2,1)} %get-tuple-element.15.mine, bf16[128,2048]{1,0:T(8,128)(2,1)} %copy-done.6, bf16[128,2048]{1,0:T(8,128)(2,1)} %copy-done.7, ...), custom_call_target="tpu_custom_call" | custom-call | tf_op jit(solution)/shard_map/post/pallas_call | solution.py:331
  129.7 4.2 %all-to-all-done.1 = bf16[64,32,256]{2,1,0:T(8,128)(2,1)S(1)} async-done(((bf16[64,32,256]{2,1,0:T(8,128)(2,1)}), bf16[64,32,256]{2,1,0:T(8,128)(2,1)S(1)}, u32[]{:S(2)}, u32[]{:S(2)}) %all-to-all-start.1) | async-done | bytes 1048608 | tf_op jit(solution)/shard_map/all_to_all | solution.py:371
  133.9 1.0 copy.23
Async XLA Ops:
  8.8 12.7 %copy-start.2 = (bf16[512,256]{1,0:T(8,128)(2,1)S(1)}, bf16[512,256]{1,0:T(8,128)(2,1)}, u32[]{:S(2)}) copy-start(bf16[512,256]{1,0:T(8,128)(2,1)} %get-tuple-element.14.fresh) | copy-start | bytes 786436
  8.8 60.0 %all-to-all-start = ((bf16[64,32,256]{2,1,0:T(8,128)(2,1)}), bf16[64,32,256]{2,1,0:T(8,128)(2,1)S(1)}, u32[]{:S(2)}, u32[]{:S(2)}) async-start(bf16[64,32,256]{2,1,0:T(8,128)(2,1)} %bitcast.12), calls=%async_computation | async-start | bytes 2097152 | tf_op jit(solution)/shard_map/all_to_all | solution.py:275
  21.5 22.7 %collective-permute-start = (bf16[512,256]{1,0:T(8,128)(2,1)S(1)}, bf16[512,256]{1,0:T(8,128)(2,1)S(1)}, u32[]{:S(2)}, u32[]{:S(2)}) collective-permute-start(bf16[512,256]{1,0:T(8,128)(2,1)S(1)} %copy-done.2), channel_id=1, source_target_pairs={{1,3},{2,0},{5,7},{6,4},{9,11},{10,8},{13,15},{14,12},{17,19},{18,... | collective-permute-start | bytes 786440 | tf_op jit(solution)/shard_map/ppermute | solution.py:272
  27.6 22.3 %collective-permute-start.1 = (bf16[512,256]{1,0:T(8,128)(2,1)S(1)}, bf16[512,256]{1,0:T(8,128)(2,1)S(1)}, u32[]{:S(2)}, u32[]{:S(2)}) collective-permute-start(bf16[512,256]{1,0:T(8,128)(2,1)S(1)} %copy-done.2), channel_id=1, source_target_pairs={{0,1},{3,2},{4,5},{7,6},{8,9},{11,10},{12,13},{15,14},{16,17},{19,... | collective-permute-start | bytes 786440 | tf_op jit(solution)/shard_map/ppermute | solution.py:273
  44.2 5.7 %copy-start.3 = (bf16[512,256]{1,0:T(8,128)(2,1)}, bf16[512,256]{1,0:T(8,128)(2,1)S(1)}, u32[]{:S(2)}) copy-start(bf16[512,256]{1,0:T(8,128)(2,1)S(1)} %collective-permute-done.via_chip) | copy-start | bytes 786436
  44.2 7.6 %collective-permute-start.2 = (bf16[512,256]{1,0:T(8,128)(2,1)S(1)}, bf16[512,256]{1,0:T(8,128)(2,1)S(1)}, u32[]{:S(2)}, u32[]{:S(2)}) collective-permute-start(bf16[512,256]{1,0:T(8,128)(2,1)S(1)} %collective-permute-done.via_chip), channel_id=1, source_target_pairs={{0,1},{3,2},{4,5},{7,6},{8,9},{11,10},{12,13},{15,14},{16,17},{19,... | collective-permute-start | bytes 786440 | tf_op jit(solution)/shard_map/ppermute | solution.py:274
  49.9 1.9 %copy-start.4 = (bf16[512,256]{1,0:T(8,128)(2,1)}, bf16[512,256]{1,0:T(8,128)(2,1)S(1)}, u32[]{:S(2)}) copy-start(bf16[512,256]{1,0:T(8,128)(2,1)S(1)} %collective-permute-done.1.via_core) | copy-start | bytes 786436
  51.8 0.7 copy-start.5
  60.8 6.0 %collective-permute-start.4 = (bf16[128,2048]{1,0:T(8,128)(2,1)}, bf16[128,2048]{1,0:T(8,128)(2,1)S(1)}, u32[]{:S(2)}, u32[]{:S(2)}) collective-permute-start(bf16[128,2048]{1,0:T(8,128)(2,1)} %get-tuple-element.18), channel_id=1, source_target_pairs={{0,1},{1,0},{2,3},{3,2},{4,5},{5,4},{6,7},{7,6},{8,9},{9,8},{10,11... | collective-permute-start | bytes 1572872 | tf_op jit(solution)/shard_map/ppermute | solution.py:325
  68.7 1.0 copy-start
  72.7 61.2 %all-to-all-start.1 = ((bf16[64,32,256]{2,1,0:T(8,128)(2,1)}), bf16[64,32,256]{2,1,0:T(8,128)(2,1)S(1)}, u32[]{:S(2)}, u32[]{:S(2)}) async-start(bf16[64,32,256]{2,1,0:T(8,128)(2,1)} %permute.1), calls=%async_computation.1 | async-start | bytes 2097152 | tf_op jit(solution)/shard_map/all_to_all | solution.py:371
  82.9 9.2 %copy-start.1 = (bf16[128,2048]{1,0:T(8,128)(2,1)S(1)}, bf16[128,2048]{1,0:T(8,128)(2,1)}, u32[]{:S(2)}) copy-start(bf16[128,2048]{1,0:T(8,128)(2,1)} %add_convert_fusion.after) | copy-start | bytes 1572868
  91.3 2.5 %collective-permute-start.3 = (bf16[128,2048]{1,0:T(8,128)(2,1)}, bf16[128,2048]{1,0:T(8,128)(2,1)S(1)}, u32[]{:S(2)}, u32[]{:S(2)}) collective-permute-start(bf16[128,2048]{1,0:T(8,128)(2,1)} %get-tuple-element.16), channel_id=1, source_target_pairs={{0,1},{1,0},{2,3},{3,2},{4,5},{5,4},{6,7},{7,6},{8,9},{9,8},{10,11... | collective-permute-start | bytes 1572872 | tf_op jit(solution)/shard_map/ppermute | solution.py:329
  92.1 31.5 %collective-permute-start.5 = (bf16[128,2048]{1,0:T(8,128)(2,1)S(1)}, bf16[128,2048]{1,0:T(8,128)(2,1)S(1)}, u32[]{:S(2)}, u32[]{:S(2)}) collective-permute-start(bf16[128,2048]{1,0:T(8,128)(2,1)S(1)} %copy-done.1), channel_id=1, source_target_pairs={{0,2},{1,3},{2,0},{3,1},{4,6},{5,7},{6,4},{7,5},{8,10},{9,11},{10,... | collective-permute-start | bytes 1572872 | tf_op jit(solution)/shard_map/ppermute | solution.py:327
  93.8 29.8 %copy-start.6 = (bf16[128,2048]{1,0:T(8,128)(2,1)}, bf16[128,2048]{1,0:T(8,128)(2,1)S(1)}, u32[]{:S(2)}) copy-start(bf16[128,2048]{1,0:T(8,128)(2,1)S(1)} %collective-permute-done.3.partner) | copy-start | bytes 1572868
  123.6 0.8 copy-start.7

commit v5 on v4

--- a/solution.py
+++ b/solution.py
@@ -106,9 +106,93 @@
     queries[0] = turn(part, cosine[...], sine[...]).astype(BF16)
 
 
+def old_copies(table, pool, keys, vals, sem, kv_of, kv_heads, n_pages, page):
+    return [
+        pltpu.make_async_copy(
+            pool.at[table[p], slot], buf.at[pl.ds(p * page, page)], sem.at[i, p]
+        )
+        for i, buf, slot in ((0, keys, kv_of), (1, vals, kv_of + kv_heads))
+        for p in range(n_pages)
+    ]
+
+
+def new_copies(head, fresh, via_ring, via_both, keys, vals, key_sem, val_sem):
+    sources = (
+        (fresh, via_ring),
+        (via_ring, via_both),
+        (via_both, via_ring),
+        (via_ring, fresh),
+    )
+    for h, (key_src, val_src) in enumerate(sources):
+
+        @pl.when(head == h)
+        def _():
+            new_key = pltpu.make_async_copy(key_src, keys, key_sem)
+            new_val = pltpu.make_async_copy(val_src, vals, val_sem)
+            new_key.start()
+            new_val.start()
+            new_key.wait()
+            new_val.wait()
+
+
+def attend_old_kernel(
+    table, prefix_len, head_at, send_q, mine_q, pool, acc, stat, keys, vals, sem,
+    *, n_pages, page, kv_heads, group,
+):
+    head = head_at[0]
+    length = prefix_len[0]
+    heads, tile, _ = send_q.shape
+    prefix = n_pages * page
+    kv_of = head * heads // group
+    copies = old_copies(table, pool, keys, vals, sem, kv_of, kv_heads, n_pages, page)
+    for copy in copies:
+        copy.start()
+    for copy in copies:
+        copy.wait()
+    live = lax.broadcasted_iota(jnp.int32, (1, prefix), 1) < length
+    for h in range(heads):
+        both = jnp.concatenate([send_q[h], mine_q[h]], axis=0)
+        scores = jnp.where(live, dot_t(both, keys[...]), -jnp.inf)
+        top = jnp.max(scores, axis=1, keepdims=True)
+        expo = jnp.exp(scores - top)
+        total = jnp.sum(expo, axis=1, keepdims=True)
+        acc[h] = dot(expo.astype(BF16), vals[...])
+        half = stat.shape[2] // 2
+        stat[h, :, :half] = jnp.broadcast_to(top, (2 * tile, half))
+        stat[h, :, half:] = jnp.broadcast_to(total, (2 * tile, half))
+
+
+def attend_new_kernel(
+    head_at, send_q, mine_q, acc, stat, w_out, fresh, via_ring, via_both,
+    send, mine, keys, vals, sem,
+):
+    head = head_at[0]
+    heads, tile, _ = send_q.shape
+    rows = fresh.shape[0]
+    new_copies(head, fresh, via_ring, via_both, keys, vals, sem.at[0], sem.at[1])
+    col = lax.broadcasted_iota(jnp.int32, (1, rows), 1)
+    row = lax.broadcasted_iota(jnp.int32, (tile, 1), 0)
+    token = jnp.concatenate([quarter_of(False, i, head) * tile + row for i in range(2)], axis=0)
+    half = stat.shape[2] // 2
+    attns = []
+    for h in range(heads):
+        both = jnp.concatenate([send_q[h], mine_q[h]], axis=0)
+        scores = jnp.where(col <= token, dot_t(both, keys[...]), -jnp.inf)
+        old_top = stat[h, :, :1]
+        top = jnp.maximum(old_top, jnp.max(scores, axis=1, keepdims=True))
+        expo = jnp.exp(scores - top)
+        fade = jnp.exp(old_top - top)
+        total = stat[h, :, half : half + 1] * fade + jnp.sum(expo, axis=1, keepdims=True)
+        value = acc[h] * fade + dot(expo.astype(BF16), vals[...])
+        attns.append((value / total).astype(BF16))
+    part = dot(jnp.concatenate(attns, axis=1), w_out[...]).astype(BF16)
+    send[...] = part[:tile]
+    mine[...] = part[tile:]
+
+
 def attend_kernel(
-    table, prefix_len, head_at, send_q, mine_q, w_out, pool, fresh, via_chip, via_core, via_both,
-    send, mine, keys, vals, sem, *, own_chip, n_pages, page, kv_heads, group,
+    table, prefix_len, head_at, send_q, mine_q, w_out, pool, fresh, via_ring, via_both,
+    send, mine, keys, vals, sem, *, n_pages, page, kv_heads, group,
 ):
     head = head_at[0]
     length = prefix_len[0]
@@ -117,37 +201,13 @@
     prefix = n_pages * page
     rows = fresh.shape[0]
 
-    copies = []
-    for i, buf, slot in ((0, keys, kv_of), (1, vals, kv_of + kv_heads)):
-        for p in range(n_pages):
-            copies.append(
-                pltpu.make_async_copy(
-                    pool.at[table[p], slot], buf.at[pl.ds(p * page, page)], sem.at[i, p]
-                )
-            )
+    copies = old_copies(table, pool, keys, vals, sem, kv_of, kv_heads, n_pages, page)
     for copy in copies:
         copy.start()
-    sources = (
-        (fresh, via_chip),
-        (via_core, via_both),
-        (via_both, via_core),
-        (via_chip, fresh),
-    )
-    for h, (key_src, val_src) in enumerate(sources):
-
-        @pl.when(head == h)
-        def _():
-            new_key = pltpu.make_async_copy(
-                key_src, keys.at[pl.ds(prefix, rows)], sem.at[0, n_pages]
-            )
-            new_val = pltpu.make_async_copy(
-                val_src, vals.at[pl.ds(prefix, rows)], sem.at[1, n_pages]
-            )
-            new_key.start()
-            new_val.start()
-            new_key.wait()
-            new_val.wait()
-
+    new_copies(
+        head, fresh, via_ring, via_both, keys.at[pl.ds(prefix, rows)],
+        vals.at[pl.ds(prefix, rows)], sem.at[0, n_pages], sem.at[1, n_pages],
+    )
     for copy in copies:
         copy.wait()
 
@@ -158,7 +218,7 @@
     for h in range(heads):
         both = jnp.concatenate([send_q[h], mine_q[h]], axis=0)
         token = jnp.concatenate(
-            [quarter_of(own_chip, i, head) * tile + row for i in range(2)], axis=0
+            [quarter_of(True, i, head) * tile + row for i in range(2)], axis=0
         )
         scores = jnp.where(lowest <= token, dot_t(both, keys[...]), -jnp.inf)
         top = jnp.max(scores, axis=1, keepdims=True)
@@ -269,9 +329,8 @@
     def pairs(moves):
         return [(b * n_head + s, b * n_head + t) for b in range(blocks) for s, t in moves]
 
-    via_chip = lax.ppermute(fresh, AXES, pairs(((1, 3), (2, 0))))
-    via_core = lax.ppermute(fresh, AXES, pairs(((0, 1), (3, 2))))
-    via_both = lax.ppermute(via_chip, AXES, pairs(((0, 1), (3, 2))))
+    via_ring = lax.ppermute(fresh, AXES, pairs(((0, 1), (1, 3), (3, 2), (2, 0))))
+    via_both = lax.ppermute(via_ring, AXES, pairs(((0, 1), (3, 2))))
     spread = lax.all_to_all(
         full_seq.reshape(blocks, total_len // blocks, dim), "blk", 0, 0, tiled=True
     )
@@ -291,41 +350,77 @@
         name="query",
     )(normed, w_query, q_gain, cosine, sine)
 
-    def attend(own_chip):
-        def query_spec(own_core):
-            return pl.BlockSpec(
+    hbm = pl.BlockSpec(memory_space=ANY)
+    parts = [jax.ShapeDtypeStruct((quarter, width), BF16)] * 2
+    sizes = dict(n_pages=n_pages, page=page, kv_heads=kv_heads, group=group)
+    state = (heads, 2 * quarter, dim)
+
+    def query_specs(own_chip):
+        return [
+            pl.BlockSpec(
                 (heads, quarter, dim),
-                lambda i, t, n, h: (0, quarter_of(own_chip, own_core, h[0]), 0),
+                lambda i, *m, core=core: (0, quarter_of(own_chip, core, m[-1][0]), 0),
             )
-
-        return pl.pallas_call(
-            functools.partial(
-                attend_kernel, own_chip=own_chip, n_pages=n_pages, page=page,
-                kv_heads=kv_heads, group=group,
-            ),
-            grid_spec=pltpu.PrefetchScalarGridSpec(
-                num_scalar_prefetch=3,
-                grid=(1,),
-                in_specs=[query_spec(False), query_spec(True), whole(w_out.shape)]
-                + [pl.BlockSpec(memory_space=ANY)] * 5,
-                out_specs=[whole((quarter, width))] * 2,
-                scratch_shapes=[
-                    pltpu.VMEM((total_len, dim), BF16),
-                    pltpu.VMEM((total_len, dim), BF16),
-                    pltpu.SemaphoreType.DMA((2, n_pages + 1)),
-                ],
-            ),
-            out_shape=[jax.ShapeDtypeStruct((quarter, width), BF16)] * 2,
-            name="attend_own" if own_chip else "attend_other",
-        )(*scalars, queries, queries, w_out, kv_pool, fresh, via_chip, via_core, via_both)
+            for core in (False, True)
+        ]
+
+    acc, stat = pl.pallas_call(
+        functools.partial(attend_old_kernel, **sizes),
+        grid_spec=pltpu.PrefetchScalarGridSpec(
+            num_scalar_prefetch=3,
+            grid=(1,),
+            in_specs=query_specs(False) + [hbm],
+            out_specs=[whole(state)] * 2,
+            scratch_shapes=[
+                pltpu.VMEM((prefix, dim), BF16),
+                pltpu.VMEM((prefix, dim), BF16),
+                pltpu.SemaphoreType.DMA((2, n_pages)),
+            ],
+        ),
+        out_shape=[jax.ShapeDtypeStruct(state, F32)] * 2,
+        name="attend_old",
+    )(*scalars, queries, queries, kv_pool)
+
+    send, mine = pl.pallas_call(
+        attend_new_kernel,
+        grid_spec=pltpu.PrefetchScalarGridSpec(
+            num_scalar_prefetch=1,
+            grid=(1,),
+            in_specs=query_specs(False)
+            + [whole(state), whole(state), whole(w_out.shape)]
+            + [hbm] * 3,
+            out_specs=[whole((quarter, width))] * 2,
+            scratch_shapes=[
+                pltpu.VMEM((rows, dim), BF16),
+                pltpu.VMEM((rows, dim), BF16),
+                pltpu.SemaphoreType.DMA((2,)),
+            ],
+        ),
+        out_shape=parts,
+        name="attend_new",
+    )(scalars[2], queries, queries, acc, stat, w_out, fresh, via_ring, via_both)
 
     core_pairs = pairs(((0, 1), (1, 0), (2, 3), (3, 2)))
     chip_pairs = pairs(((0, 2), (1, 3), (2, 0), (3, 1)))
-    send, mine = attend(False)
     partner = lax.ppermute(send, AXES, core_pairs)
     pair_sum = (mine.astype(F32) + partner.astype(F32)).astype(BF16)
     far = lax.ppermute(pair_sum, AXES, chip_pairs)
-    send, mine = attend(True)
+    send, mine = pl.pallas_call(
+        functools.partial(attend_kernel, **sizes),
+        grid_spec=pltpu.PrefetchScalarGridSpec(
+            num_scalar_prefetch=3,
+            grid=(1,),
+            in_specs=query_specs(True) + [whole(w_out.shape)] + [hbm] * 4,
+            out_specs=[whole((quarter, width))] * 2,
+            scratch_shapes=[
+                pltpu.VMEM((total_len, dim), BF16),
+                pltpu.VMEM((total_len, dim), BF16),
+                pltpu.SemaphoreType.DMA((2, n_pages + 1)),
+            ],
+        ),
+        out_shape=parts,
+        name="attend_own",
+    )(*scalars, queries, queries, w_out, kv_pool, fresh, via_ring, via_both)
     partner = lax.ppermute(send, AXES, core_pairs)
 
     mixed = pl.pallas_call(

time: 136 us -> 138 us (1.015)
  Pallas kernels: 36.4 us -> 39.7 us
  starting transfers between devices: 37.4 us -> 35.6 us
    pallas_call x2 -> x3, Pallas kernels: 16.7 us -> 20 us  [the longest x1 8.4 us: on_device(): pl.pallas_call(functools.partial(attend_kernel, **sizes), grid_spec=pltpu...]
    ppermute x3 -> x2, starting transfers between devices: 8.7 us -> 5.58 us  [the longest x1 4.3 us: on_device(): lax.ppermute(fresh, AXES, pairs(((0, 1), (1, 3), (3, 2), (2, 0))))]
    ppermute x2, starting transfers between devices: 4.98 us -> 6.37 us  [on_device(): partner = lax.ppermute(send, AXES, core_pairs)]
    ppermute x3 -> x2, waiting for transfers between devices: 17.2 us -> 18.4 us  [the longest x1 18.4 us: on_device(): lax.ppermute(fresh, AXES, pairs(((0, 1), (1, 3), (3, 2), (2, 0))))]
    unnamed x17 -> x15, local copies, waits for them, and re-layouts: 3.44 us -> 3.45 us
  transfers between devices with their start and end apart: 8 -> 7, of which waited for: 6 -> 5; matrix products, arithmetic and copies ran while one was open for 1% -> 1% of each run, Pallas kernels for 20% -> 22%
where the time goes in v5:
time: 138 us; the launch traced here: 137 us
  waiting for transfers between devices  54.9 us (40%)
  Pallas kernels  39.7 us (29%)
  starting transfers between devices  35.6 us (26%)
  local copies, waits for them, and re-layouts  3.45 us (2%)
  other arithmetic  2.49 us (2%)
  between operations  1.39 us (1%)
    ppermute x1, waiting for transfers between devices, on_device(): far = lax.ppermute(pair_sum, AXES, chip_pairs)  29.5 us
    ppermute x1, waiting for transfers between devices, on_device(): lax.ppermute(fresh, AXES, pairs(((0, 1), (1, 3), (3, 2), (2, 0))))  18.4 us
    all_to_all x1, starting transfers between devices, on_device(): lax.all_to_all(full_seq.reshape(blocks, total_len // blocks, dim), 'blk',...  12.7 us
    all_to_all x1, starting transfers between devices, on_device(): owned = lax.all_to_all(arranged, 'blk', 0, 0, tiled=True)  10.2 us
    pallas_call x1, Pallas kernels, on_device(): pl.pallas_call(functools.partial(attend_kernel, **sizes), grid_spec=pltpu...  8.4 us
    pallas_call x1, Pallas kernels, on_device(): pl.pallas_call(functools.partial(prep_kernel, n_pages=n_pages, page=page,...  6.95 us
    ppermute x2, starting transfers between devices, on_device(): partner = lax.ppermute(send, AXES, core_pairs)  6.37 us
    pallas_call x1, Pallas kernels, on_device(): pl.pallas_call(functools.partial(attend_old_kernel, **sizes), grid_spec=p...  5.84 us
  transfers between devices with their start and end apart: 7, of which 5 were waited for; matrix products, arithmetic and copies ran while one was open for 1% of the time, Pallas kernels for 22%

profile of v5, /device:TPU:1, one launch (start us, length us, event | category | flops | bytes accessed | tf_op | source)
XLA Modules:
  0.0 137.5 jit_solution(14336102359754941003)
XLA Ops:
  0.6 0.5 multiply_power_fusion.frequency
  1.8 7.0 %prep.1 = (bf16[512,2048]{1,0:T(8,128)(2,1)}, bf16[512,256]{1,0:T(8,128)(2,1)}, bf16[2048,256]{1,0:T(8,128)(2,1)}, f32[512,128]{1,0:T(8,128)}, f32[512,128]{1,0:T(8,128)}) custom-call(s32[12]{0:T(128)} %bitcast.18, s32[1]{0:T(128)S(6)} %copy.22.prefix_len, s32[1]{0:T(128)} %bitcast.head_at, bf16[512,2048]{1,0:T(8,128)(2,1)} %hidden.3, f32[1,2048]{1,0:T(1,128)} %bitcast.14, ...), custom_call_target="tpu_custom_call" | custom-call | tf_op jit(solution)/shard_map/prep/pallas_call | solution.py:292
  8.8 0.0 copy-start.2
  8.8 12.7 %all-to-all-start = ((bf16[64,32,256]{2,1,0:T(8,128)(2,1)}), bf16[64,32,256]{2,1,0:T(8,128)(2,1)S(1)}, u32[]{:S(2)}, u32[]{:S(2)}) async-start(bf16[64,32,256]{2,1,0:T(8,128)(2,1)} %bitcast.12), calls=%async_computation | async-start | bytes 2097152 | tf_op jit(solution)/shard_map/all_to_all | solution.py:334
  21.5 0.0 copy-done.2
  21.5 4.3 %collective-permute-start = (bf16[512,256]{1,0:T(8,128)(2,1)S(1)}, bf16[512,256]{1,0:T(8,128)(2,1)S(1)}, u32[]{:S(2)}, u32[]{:S(2)}) collective-permute-start(bf16[512,256]{1,0:T(8,128)(2,1)S(1)} %copy-done.2), channel_id=1, source_target_pairs={{0,1},{1,3},{3,2},{2,0},{4,5},{5,7},{7,6},{6,4},{8,9},{9,11},{11,1... | collective-permute-start | bytes 786440 | tf_op jit(solution)/shard_map/ppermute | solution.py:332
  25.8 18.4 %collective-permute-done.via_ring = bf16[512,256]{1,0:T(8,128)(2,1)S(1)} collective-permute-done((bf16[512,256]{1,0:T(8,128)(2,1)S(1)}, bf16[512,256]{1,0:T(8,128)(2,1)S(1)}, u32[]{:S(2)}, u32[]{:S(2)}) %collective-permute-start) | collective-permute-done | bytes 262176 | tf_op jit(solution)/shard_map/ppermute | solution.py:332
  44.2 0.0 copy-start.3
  44.2 1.3 collective-permute-start.1
  45.5 4.4 %query.1.send_q.mine_q = bf16[2,512,256]{2,1,0:T(8,128)(2,1)} custom-call(bf16[512,2048]{1,0:T(8,128)(2,1)} %get-tuple-element.13.normed, bf16[2048,512]{1,0:T(8,128)(2,1)} %w_q.1, f32[1,256]{1,0:T(1,128)} %bitcast.22, f32[512,128]{1,0:T(8,128)} %get-tuple-element.14.cosine, f32[512,128]{1,0:T(8,128)} %get-tuple-element.15.sine), custom_call_target="tpu_custom_call" | custom-call | tf_op jit(solution)/shard_map/query/pallas_call | solution.py:338
  49.9 0.0 copy-done.3
  49.9 5.8 %attend_old.1 = (f32[2,256,256]{2,1,0:T(8,128)}, f32[2,256,256]{2,1,0:T(8,128)}) custom-call(s32[12]{0:T(128)} %bitcast.19, s32[1]{0:T(128)S(6)} %copy.22.prefix_len, s32[1]{0:T(128)} %bitcast.head_at, bf16[2,512,256]{2,1,0:T(8,128)(2,1)} %query.1.send_q.mine_q, bf16[2,512,256]{2,1,0:T(8,128)(2,1)} %query.1.send_q.mine_q, bf16[12,4,128,256]{3,2,1,0:T(8,128)(2,1)} %pool.5), custom_call_target="tpu_custom_call" | custom-call | tf_op jit(solution)/shard_map/attend_old/pallas_call | solution.py:367
  55.7 0.0 collective-permute-done.1.via_both
  55.7 0.0 copy-start.4
  55.8 0.7 copy-done.4
  56.5 5.7 %attend_new.1 = (bf16[128,2048]{1,0:T(8,128)(2,1)}, bf16[128,2048]{1,0:T(8,128)(2,1)}) custom-call(s32[1]{0:T(128)} %bitcast.head_at, bf16[2,512,256]{2,1,0:T(8,128)(2,1)} %query.1.send_q.mine_q, bf16[2,512,256]{2,1,0:T(8,128)(2,1)} %query.1.send_q.mine_q, f32[2,256,256]{2,1,0:T(8,128)} %get-tuple-element.19.acc, f32[2,256,256]{2,1,0:T(8,128)} %get-tuple-element.20.stat, ...), custom_call_target="tpu_custom_call" | custom-call | tf_op jit(solution)/shard_map/attend_new/pallas_call | solution.py:384
  62.2 5.4 %collective-permute-start.3 = (bf16[128,2048]{1,0:T(8,128)(2,1)}, bf16[128,2048]{1,0:T(8,128)(2,1)S(1)}, u32[]{:S(2)}, u32[]{:S(2)}) collective-permute-start(bf16[128,2048]{1,0:T(8,128)(2,1)} %get-tuple-element.22), channel_id=1, source_target_pairs={{0,1},{1,0},{2,3},{3,2},{4,5},{5,4},{6,7},{7,6},{8,9},{9,8},{10,11... | collective-permute-start | bytes 1572872 | tf_op jit(solution)/shard_map/ppermute | solution.py:405
  67.6 1.7 %collective-permute-done.3 = bf16[128,2048]{1,0:T(8,128)(2,1)S(1)} collective-permute-done((bf16[128,2048]{1,0:T(8,128)(2,1)}, bf16[128,2048]{1,0:T(8,128)(2,1)S(1)}, u32[]{:S(2)}, u32[]{:S(2)}) %collective-permute-start.3) | collective-permute-done | bytes 524320 | tf_op jit(solution)/shard_map/ppermute | solution.py:405
  69.4 2.0 %add_convert_fusion.after = bf16[128,2048]{1,0:T(8,128)(2,1)} fusion(bf16[128,2048]{1,0:T(8,128)(2,1)S(1)} %collective-permute-done.3, bf16[128,2048]{1,0:T(8,128)(2,1)} %get-tuple-element.21), kind=kLoop, calls=%fused_computation | loop fusion | flops 1048576 | bytes 1572864 | tf_op jit(solution)/shard_map/convert_element_type | solution.py:406
  71.4 0.0 all-to-all-done.spread
  71.4 0.0 copy-start
  71.4 1.0 copy-done
  72.3 3.0 %permute.1 = bf16[64,32,256]{2,1,0:T(8,128)(2,1)} custom-call(s32[64]{0:T(128)} %owner.1, bf16[64,32,256]{2,1,0:T(8,128)(2,1)} %copy-done, bf16[128,2048]{1,0:T(8,128)(2,1)} %add_convert_fusion.after), custom_call_target="tpu_custom_call" | custom-call | tf_op jit(solution)/shard_map/permute/pallas_call | solution.py:455
  75.3 10.2 %all-to-all-start.1 = ((bf16[64,32,256]{2,1,0:T(8,128)(2,1)}), bf16[64,32,256]{2,1,0:T(8,128)(2,1)S(1)}, u32[]{:S(2)}, u32[]{:S(2)}) async-start(bf16[64,32,256]{2,1,0:T(8,128)(2,1)} %permute.1), calls=%async_computation.1 | async-start | bytes 2097152 | tf_op jit(solution)/shard_map/all_to_all | solution.py:466
  85.5 0.0 copy-start.1
  85.5 8.4 %attend_own.1 = (bf16[128,2048]{1,0:T(8,128)(2,1)}, bf16[128,2048]{1,0:T(8,128)(2,1)}) custom-call(s32[12]{0:T(128)} %bitcast.20, s32[1]{0:T(128)S(6)} %copy.22.prefix_len, s32[1]{0:T(128)} %bitcast.head_at, bf16[2,512,256]{2,1,0:T(8,128)(2,1)} %query.1.send_q.mine_q, bf16[2,512,256]{2,1,0:T(8,128)(2,1)} %query.1.send_q.mine_q, bf16[512,2048]{1,0:T(8,128)(2,1)} %w_out.3, ...), custom_call_target="tpu_custom_call" | custom-call | tf_op jit(solution)/shard_map/attend_own/pallas_call | solution.py:408
  93.9 0.9 collective-permute-start.2
  94.9 0.0 copy-done.1
  94.9 0.7 collective-permute-start.4
  95.6 1.0 collective-permute-done.2.partner
  96.6 0.0 copy-start.5
  96.6 29.5 %collective-permute-done.4.far = bf16[128,2048]{1,0:T(8,128)(2,1)S(1)} collective-permute-done((bf16[128,2048]{1,0:T(8,128)(2,1)S(1)}, bf16[128,2048]{1,0:T(8,128)(2,1)S(1)}, u32[]{:S(2)}, u32[]{:S(2)}) %collective-permute-start.4) | collective-permute-done | bytes 524320 | tf_op jit(solution)/shard_map/ppermute | solution.py:407
  126.2 0.0 copy-start.6
  126.2 0.0 copy-done.5
  126.2 0.8 copy-done.6
  127.0 5.4 %post.1 = bf16[128,2048]{1,0:T(8,128)(2,1)} custom-call(s32[1]{0:T(128)} %bitcast.head_at, bf16[512,2048]{1,0:T(8,128)(2,1)} %hidden.3, bf16[512,2048]{1,0:T(8,128)(2,1)} %get-tuple-element.13.normed, bf16[128,2048]{1,0:T(8,128)(2,1)} %get-tuple-element.17.mine, bf16[128,2048]{1,0:T(8,128)(2,1)} %copy-done.5, bf16[128,2048]{1,0:T(8,128)(2,1)} %copy-done.6, ...), custom_call_target="tpu_custom_call" | custom-call | tf_op jit(solution)/shard_map/post/pallas_call | solution.py:426
  132.3 4.2 %all-to-all-done.1 = bf16[64,32,256]{2,1,0:T(8,128)(2,1)S(1)} async-done(((bf16[64,32,256]{2,1,0:T(8,128)(2,1)}), bf16[64,32,256]{2,1,0:T(8,128)(2,1)S(1)}, u32[]{:S(2)}, u32[]{:S(2)}) %all-to-all-start.1) | async-done | bytes 1048608 | tf_op jit(solution)/shard_map/all_to_all | solution.py:466
  136.5 1.0 copy.23
Async XLA Ops:
  8.8 12.7 %copy-start.2 = (bf16[512,256]{1,0:T(8,128)(2,1)S(1)}, bf16[512,256]{1,0:T(8,128)(2,1)}, u32[]{:S(2)}) copy-start(bf16[512,256]{1,0:T(8,128)(2,1)} %get-tuple-element.16.fresh) | copy-start | bytes 786436
  8.8 62.6 %all-to-all-start = ((bf16[64,32,256]{2,1,0:T(8,128)(2,1)}), bf16[64,32,256]{2,1,0:T(8,128)(2,1)S(1)}, u32[]{:S(2)}, u32[]{:S(2)}) async-start(bf16[64,32,256]{2,1,0:T(8,128)(2,1)} %bitcast.12), calls=%async_computation | async-start | bytes 2097152 | tf_op jit(solution)/shard_map/all_to_all | solution.py:334
  21.5 22.7 %collective-permute-start = (bf16[512,256]{1,0:T(8,128)(2,1)S(1)}, bf16[512,256]{1,0:T(8,128)(2,1)S(1)}, u32[]{:S(2)}, u32[]{:S(2)}) collective-permute-start(bf16[512,256]{1,0:T(8,128)(2,1)S(1)} %copy-done.2), channel_id=1, source_target_pairs={{0,1},{1,3},{3,2},{2,0},{4,5},{5,7},{7,6},{6,4},{8,9},{9,11},{11,1... | collective-permute-start | bytes 786440 | tf_op jit(solution)/shard_map/ppermute | solution.py:332
  44.2 5.7 %copy-start.3 = (bf16[512,256]{1,0:T(8,128)(2,1)}, bf16[512,256]{1,0:T(8,128)(2,1)S(1)}, u32[]{:S(2)}) copy-start(bf16[512,256]{1,0:T(8,128)(2,1)S(1)} %collective-permute-done.via_ring) | copy-start | bytes 786436
  44.2 11.6 %collective-permute-start.1 = (bf16[512,256]{1,0:T(8,128)(2,1)S(1)}, bf16[512,256]{1,0:T(8,128)(2,1)S(1)}, u32[]{:S(2)}, u32[]{:S(2)}) collective-permute-start(bf16[512,256]{1,0:T(8,128)(2,1)S(1)} %collective-permute-done.via_ring), channel_id=1, source_target_pairs={{0,1},{3,2},{4,5},{7,6},{8,9},{11,10},{12,13},{15,14},{16,17},{19,... | collective-permute-start | bytes 786440 | tf_op jit(solution)/shard_map/ppermute | solution.py:333
  55.7 0.7 copy-start.4
  62.2 7.2 %collective-permute-start.3 = (bf16[128,2048]{1,0:T(8,128)(2,1)}, bf16[128,2048]{1,0:T(8,128)(2,1)S(1)}, u32[]{:S(2)}, u32[]{:S(2)}) collective-permute-start(bf16[128,2048]{1,0:T(8,128)(2,1)} %get-tuple-element.22), channel_id=1, source_target_pairs={{0,1},{1,0},{2,3},{3,2},{4,5},{5,4},{6,7},{7,6},{8,9},{9,8},{10,11... | collective-permute-start | bytes 1572872 | tf_op jit(solution)/shard_map/ppermute | solution.py:405
  71.4 1.0 copy-start
  75.3 61.2 %all-to-all-start.1 = ((bf16[64,32,256]{2,1,0:T(8,128)(2,1)}), bf16[64,32,256]{2,1,0:T(8,128)(2,1)S(1)}, u32[]{:S(2)}, u32[]{:S(2)}) async-start(bf16[64,32,256]{2,1,0:T(8,128)(2,1)} %permute.1), calls=%async_computation.1 | async-start | bytes 2097152 | tf_op jit(solution)/shard_map/all_to_all | solution.py:466
  85.5 9.3 %copy-start.1 = (bf16[128,2048]{1,0:T(8,128)(2,1)S(1)}, bf16[128,2048]{1,0:T(8,128)(2,1)}, u32[]{:S(2)}) copy-start(bf16[128,2048]{1,0:T(8,128)(2,1)} %add_convert_fusion.after) | copy-start | bytes 1572868
  93.9 2.7 %collective-permute-start.2 = (bf16[128,2048]{1,0:T(8,128)(2,1)}, bf16[128,2048]{1,0:T(8,128)(2,1)S(1)}, u32[]{:S(2)}, u32[]{:S(2)}) collective-permute-start(bf16[128,2048]{1,0:T(8,128)(2,1)} %get-tuple-element.18), channel_id=1, source_target_pairs={{0,1},{1,0},{2,3},{3,2},{4,5},{5,4},{6,7},{7,6},{8,9},{9,8},{10,11... | collective-permute-start | bytes 1572872 | tf_op jit(solution)/shard_map/ppermute | solution.py:424
  94.9 31.3 %collective-permute-start.4 = (bf16[128,2048]{1,0:T(8,128)(2,1)S(1)}, bf16[128,2048]{1,0:T(8,128)(2,1)S(1)}, u32[]{:S(2)}, u32[]{:S(2)}) collective-permute-start(bf16[128,2048]{1,0:T(8,128)(2,1)S(1)} %copy-done.1), channel_id=1, source_target_pairs={{0,2},{1,3},{2,0},{3,1},{4,6},{5,7},{6,4},{7,5},{8,10},{9,11},{10,... | collective-permute-start | bytes 1572872 | tf_op jit(solution)/shard_map/ppermute | solution.py:407
  96.6 29.5 %copy-start.5 = (bf16[128,2048]{1,0:T(8,128)(2,1)}, bf16[128,2048]{1,0:T(8,128)(2,1)S(1)}, u32[]{:S(2)}) copy-start(bf16[128,2048]{1,0:T(8,128)(2,1)S(1)} %collective-permute-done.2.partner) | copy-start | bytes 1572868
  126.2 0.8 copy-start.6

commit v6 on v5

--- a/solution.py
+++ b/solution.py
@@ -2,6 +2,7 @@
 
 import jax
 import jax.numpy as jnp
+import numpy as np
 from jax import lax
 from jax.experimental import pallas as pl
 from jax.experimental.pallas import tpu as pltpu
@@ -37,10 +38,9 @@
 
 def prep_kernel(
     table, prefix_len, head_at, hidden, in_gain, w_kv, k_gain, frequency, pool,
-    normed, fresh, seq, cosine, sine, fresh_all, sem, *, n_pages, page, rows, kv_heads,
+    normed, fresh, seq, cosine, sine, sem, *, n_pages, page, kv_heads,
 ):
     step = pl.program_id(0)
-    steps = pl.num_programs(0)
     head = head_at[0]
     length = prefix_len[0]
     tile = hidden.shape[0]
@@ -74,7 +74,6 @@
     key = turn(own * k_gain[...], cos, sin)
     slot = jnp.where(head < kv_heads, key, own).astype(BF16)
     fresh[...] = slot
-    fresh_all[pl.ds(pl.multiple_of(step * tile, tile), tile), :] = slot
 
     @pl.when(step == 0)
     def _():
@@ -88,17 +87,15 @@
 
         seq[prefix:total, :] = jnp.zeros((total - prefix, seq.shape[1]), BF16)
 
-    @pl.when(step == steps - 1)
-    def _():
-        span = rows + page
-        base = jnp.minimum(length // page * page, total - span)
-        base = pl.multiple_of(base, page)
-        row = base + lax.broadcasted_iota(jnp.int32, (span, 1), 0)
-        col = lax.broadcasted_iota(jnp.int32, (span, rows), 1)
-        pick = jnp.where(row - length == col, 1.0, 0.0).astype(BF16)
-        placed = dot(pick, fresh_all[...])
-        window = seq[pl.ds(base, span), :].astype(F32)
-        seq[pl.ds(base, span), :] = jnp.where(row < length, window, placed).astype(BF16)
+    start = length + step * tile
+    span = tile + page
+    base = pl.multiple_of(jnp.minimum(start // page * page, total - span), page)
+    row = base + lax.broadcasted_iota(jnp.int32, (span, 1), 0)
+    col = lax.broadcasted_iota(jnp.int32, (span, tile), 1)
+    pick = jnp.where(row - start == col, 1.0, 0.0).astype(BF16)
+    placed = dot(pick, slot)
+    window = seq[pl.ds(base, span), :].astype(F32)
+    seq[pl.ds(base, span), :] = jnp.where(row < start, window, placed).astype(BF16)
 
 
 def query_kernel(normed, w_q, q_gain, cosine, sine, queries):
@@ -282,7 +279,7 @@
     quarter = rows // n_head
     head = lax.axis_index("head").astype(jnp.int32)
     half = dim // 2
-    frequency = (rope_base ** (-jnp.arange(half, dtype=F32) / half))[None]
+    frequency = jnp.asarray((rope_base ** (-np.arange(half) / half))[None], F32)
     scalars = (page_table[0], prefix_len, head[None])
 
     in_gain, q_gain, k_gain = in_gain[None], q_gain[None], k_gain[None]
@@ -291,7 +288,7 @@
     tile = rows // 2
     normed, fresh, full_seq, cosine, sine = pl.pallas_call(
         functools.partial(
-            prep_kernel, n_pages=n_pages, page=page, rows=rows, kv_heads=kv_heads
+            prep_kernel, n_pages=n_pages, page=page, kv_heads=kv_heads
         ),
         grid_spec=pltpu.PrefetchScalarGridSpec(
             num_scalar_prefetch=3,
@@ -312,7 +309,6 @@
                 pl.BlockSpec((tile, half), lambda i, *_: (i, 0)),
             ],
             scratch_shapes=[
-                pltpu.VMEM((rows, dim), BF16),
                 pltpu.SemaphoreType.DMA((n_pages,)),
             ],
         ),

time: 138 us -> 138 us (level)
  no operation moved by 1% of the time
where the time goes in v6:
time: 138 us; the launch traced here: 137 us
  waiting for transfers between devices  55 us (40%)
  Pallas kernels  39.7 us (29%)
  starting transfers between devices  35.4 us (26%)
  local copies, waits for them, and re-layouts  3.45 us (2%)
  other arithmetic  1.97 us (1%)
  between operations  1.39 us (1%)
    ppermute x1, waiting for transfers between devices, on_device(): far = lax.ppermute(pair_sum, AXES, chip_pairs)  29.8 us
    ppermute x1, waiting for transfers between devices, on_device(): lax.ppermute(fresh, AXES, pairs(((0, 1), (1, 3), (3, 2), (2, 0))))  18.4 us
    all_to_all x1, starting transfers between devices, on_device(): lax.all_to_all(full_seq.reshape(blocks, total_len // blocks, dim), 'blk',...  12.7 us
    all_to_all x1, starting transfers between devices, on_device(): owned = lax.all_to_all(arranged, 'blk', 0, 0, tiled=True)  10.2 us
    pallas_call x1, Pallas kernels, on_device(): pl.pallas_call(functools.partial(attend_kernel, **sizes), grid_spec=pltpu...  8.4 us
    pallas_call x1, Pallas kernels, on_device(): pl.pallas_call(functools.partial(prep_kernel, n_pages=n_pages, page=page,...  6.97 us
    ppermute x2, starting transfers between devices, on_device(): partner = lax.ppermute(send, AXES, core_pairs)  6.19 us
    pallas_call x1, Pallas kernels, on_device(): pl.pallas_call(functools.partial(attend_old_kernel, **sizes), grid_spec=p...  5.84 us
  transfers between devices with their start and end apart: 7, of which 5 were waited for; matrix products, arithmetic and copies ran while one was open for 1% of the time, Pallas kernels for 22%

profile of v6, /device:TPU:1, one launch (start us, length us, event | category | flops | bytes accessed | tf_op | source)
XLA Modules:
  0.0 137.0 jit_solution(4802458511330440901)
XLA Ops:
  1.3 7.0 %prep.1 = (bf16[512,2048]{1,0:T(8,128)(2,1)}, bf16[512,256]{1,0:T(8,128)(2,1)}, bf16[2048,256]{1,0:T(8,128)(2,1)}, f32[512,128]{1,0:T(8,128)}, f32[512,128]{1,0:T(8,128)}) custom-call(s32[12]{0:T(128)} %bitcast.18, s32[1]{0:T(128)S(6)} %copy.23.prefix_len, s32[1]{0:T(128)} %bitcast.head_at, bf16[512,2048]{1,0:T(8,128)(2,1)} %hidden.3, f32[1,2048]{1,0:T(1,128)} %bitcast.14, ...), custom_call_target="tpu_custom_call" | custom-call | tf_op jit(solution)/shard_map/prep/pallas_call | solution.py:289
  8.3 0.0 copy-start.2
  8.3 12.7 %all-to-all-start = ((bf16[64,32,256]{2,1,0:T(8,128)(2,1)}), bf16[64,32,256]{2,1,0:T(8,128)(2,1)S(1)}, u32[]{:S(2)}, u32[]{:S(2)}) async-start(bf16[64,32,256]{2,1,0:T(8,128)(2,1)} %bitcast.12), calls=%async_computation | async-start | bytes 2097152 | tf_op jit(solution)/shard_map/all_to_all | solution.py:330
  21.0 0.0 copy-done.2
  21.0 4.3 %collective-permute-start = (bf16[512,256]{1,0:T(8,128)(2,1)S(1)}, bf16[512,256]{1,0:T(8,128)(2,1)S(1)}, u32[]{:S(2)}, u32[]{:S(2)}) collective-permute-start(bf16[512,256]{1,0:T(8,128)(2,1)S(1)} %copy-done.2), channel_id=1, source_target_pairs={{0,1},{1,3},{3,2},{2,0},{4,5},{5,7},{7,6},{6,4},{8,9},{9,11},{11,1... | collective-permute-start | bytes 786440 | tf_op jit(solution)/shard_map/ppermute | solution.py:328
  25.3 18.4 %collective-permute-done.via_ring = bf16[512,256]{1,0:T(8,128)(2,1)S(1)} collective-permute-done((bf16[512,256]{1,0:T(8,128)(2,1)S(1)}, bf16[512,256]{1,0:T(8,128)(2,1)S(1)}, u32[]{:S(2)}, u32[]{:S(2)}) %collective-permute-start) | collective-permute-done | bytes 262176 | tf_op jit(solution)/shard_map/ppermute | solution.py:328
  43.7 0.0 copy-start.3
  43.7 1.3 collective-permute-start.1
  45.0 4.4 %query.1.send_q.mine_q = bf16[2,512,256]{2,1,0:T(8,128)(2,1)} custom-call(bf16[512,2048]{1,0:T(8,128)(2,1)} %get-tuple-element.13.normed, bf16[2048,512]{1,0:T(8,128)(2,1)} %w_q.1, f32[1,256]{1,0:T(1,128)} %bitcast.22, f32[512,128]{1,0:T(8,128)} %get-tuple-element.14.cosine, f32[512,128]{1,0:T(8,128)} %get-tuple-element.15.sine), custom_call_target="tpu_custom_call" | custom-call | tf_op jit(solution)/shard_map/query/pallas_call | solution.py:334
  49.4 0.0 copy-done.3
  49.4 5.8 %attend_old.1 = (f32[2,256,256]{2,1,0:T(8,128)}, f32[2,256,256]{2,1,0:T(8,128)}) custom-call(s32[12]{0:T(128)} %bitcast.19, s32[1]{0:T(128)S(6)} %copy.23.prefix_len, s32[1]{0:T(128)} %bitcast.head_at, bf16[2,512,256]{2,1,0:T(8,128)(2,1)} %query.1.send_q.mine_q, bf16[2,512,256]{2,1,0:T(8,128)(2,1)} %query.1.send_q.mine_q, bf16[12,4,128,256]{3,2,1,0:T(8,128)(2,1)} %pool.5), custom_call_target="tpu_custom_call" | custom-call | tf_op jit(solution)/shard_map/attend_old/pallas_call | solution.py:363
  55.2 0.0 collective-permute-done.1.via_both
  55.2 0.0 copy-start.4
  55.2 0.7 copy-done.4
  55.9 5.7 %attend_new.1 = (bf16[128,2048]{1,0:T(8,128)(2,1)}, bf16[128,2048]{1,0:T(8,128)(2,1)}) custom-call(s32[1]{0:T(128)} %bitcast.head_at, bf16[2,512,256]{2,1,0:T(8,128)(2,1)} %query.1.send_q.mine_q, bf16[2,512,256]{2,1,0:T(8,128)(2,1)} %query.1.send_q.mine_q, f32[2,256,256]{2,1,0:T(8,128)} %get-tuple-element.19.acc, f32[2,256,256]{2,1,0:T(8,128)} %get-tuple-element.20.stat, ...), custom_call_target="tpu_custom_call" | custom-call | tf_op jit(solution)/shard_map/attend_new/pallas_call | solution.py:380
  61.7 5.4 %collective-permute-start.3 = (bf16[128,2048]{1,0:T(8,128)(2,1)}, bf16[128,2048]{1,0:T(8,128)(2,1)S(1)}, u32[]{:S(2)}, u32[]{:S(2)}) collective-permute-start(bf16[128,2048]{1,0:T(8,128)(2,1)} %get-tuple-element.22), channel_id=1, source_target_pairs={{0,1},{1,0},{2,3},{3,2},{4,5},{5,4},{6,7},{7,6},{8,9},{9,8},{10,11... | collective-permute-start | bytes 1572872 | tf_op jit(solution)/shard_map/ppermute | solution.py:401
  67.1 1.7 %collective-permute-done.3 = bf16[128,2048]{1,0:T(8,128)(2,1)S(1)} collective-permute-done((bf16[128,2048]{1,0:T(8,128)(2,1)}, bf16[128,2048]{1,0:T(8,128)(2,1)S(1)}, u32[]{:S(2)}, u32[]{:S(2)}) %collective-permute-start.3) | collective-permute-done | bytes 524320 | tf_op jit(solution)/shard_map/ppermute | solution.py:401
  68.9 2.0 %add_convert_fusion.after = bf16[128,2048]{1,0:T(8,128)(2,1)} fusion(bf16[128,2048]{1,0:T(8,128)(2,1)S(1)} %collective-permute-done.3, bf16[128,2048]{1,0:T(8,128)(2,1)} %get-tuple-element.21), kind=kLoop, calls=%fused_computation | loop fusion | flops 1048576 | bytes 1572864 | tf_op jit(solution)/shard_map/convert_element_type | solution.py:402
  70.9 0.0 all-to-all-done.spread
  70.9 0.0 copy-start
  70.9 1.0 copy-done
  71.8 3.0 %permute.1 = bf16[64,32,256]{2,1,0:T(8,128)(2,1)} custom-call(s32[64]{0:T(128)} %owner.1, bf16[64,32,256]{2,1,0:T(8,128)(2,1)} %copy-done, bf16[128,2048]{1,0:T(8,128)(2,1)} %add_convert_fusion.after), custom_call_target="tpu_custom_call" | custom-call | tf_op jit(solution)/shard_map/permute/pallas_call | solution.py:451
  74.8 10.2 %all-to-all-start.1 = ((bf16[64,32,256]{2,1,0:T(8,128)(2,1)}), bf16[64,32,256]{2,1,0:T(8,128)(2,1)S(1)}, u32[]{:S(2)}, u32[]{:S(2)}) async-start(bf16[64,32,256]{2,1,0:T(8,128)(2,1)} %permute.1), calls=%async_computation.1 | async-start | bytes 2097152 | tf_op jit(solution)/shard_map/all_to_all | solution.py:462
  85.0 0.0 copy-start.1
  85.0 8.4 %attend_own.1 = (bf16[128,2048]{1,0:T(8,128)(2,1)}, bf16[128,2048]{1,0:T(8,128)(2,1)}) custom-call(s32[12]{0:T(128)} %bitcast.20, s32[1]{0:T(128)S(6)} %copy.23.prefix_len, s32[1]{0:T(128)} %bitcast.head_at, bf16[2,512,256]{2,1,0:T(8,128)(2,1)} %query.1.send_q.mine_q, bf16[2,512,256]{2,1,0:T(8,128)(2,1)} %query.1.send_q.mine_q, bf16[512,2048]{1,0:T(8,128)(2,1)} %w_out.3, ...), custom_call_target="tpu_custom_call" | custom-call | tf_op jit(solution)/shard_map/attend_own/pallas_call | solution.py:404
  93.4 0.7 collective-permute-start.2
  94.2 0.0 copy-done.1
  94.2 0.7 collective-permute-start.4
  94.9 1.0 collective-permute-done.2.partner
  95.9 0.0 copy-start.5
  95.9 29.8 %collective-permute-done.4.far = bf16[128,2048]{1,0:T(8,128)(2,1)S(1)} collective-permute-done((bf16[128,2048]{1,0:T(8,128)(2,1)S(1)}, bf16[128,2048]{1,0:T(8,128)(2,1)S(1)}, u32[]{:S(2)}, u32[]{:S(2)}) %collective-permute-start.4) | collective-permute-done | bytes 524320 | tf_op jit(solution)/shard_map/ppermute | solution.py:403
  125.7 0.0 copy-start.6
  125.7 0.0 copy-done.5
  125.7 0.8 copy-done.6
  126.5 5.4 %post.1 = bf16[128,2048]{1,0:T(8,128)(2,1)} custom-call(s32[1]{0:T(128)} %bitcast.head_at, bf16[512,2048]{1,0:T(8,128)(2,1)} %hidden.3, bf16[512,2048]{1,0:T(8,128)(2,1)} %get-tuple-element.13.normed, bf16[128,2048]{1,0:T(8,128)(2,1)} %get-tuple-element.17.mine, bf16[128,2048]{1,0:T(8,128)(2,1)} %copy-done.5, bf16[128,2048]{1,0:T(8,128)(2,1)} %copy-done.6, ...), custom_call_target="tpu_custom_call" | custom-call | tf_op jit(solution)/shard_map/post/pallas_call | solution.py:422
  131.8 4.1 %all-to-all-done.1 = bf16[64,32,256]{2,1,0:T(8,128)(2,1)S(1)} async-done(((bf16[64,32,256]{2,1,0:T(8,128)(2,1)}), bf16[64,32,256]{2,1,0:T(8,128)(2,1)S(1)}, u32[]{:S(2)}, u32[]{:S(2)}) %all-to-all-start.1) | async-done | bytes 1048608 | tf_op jit(solution)/shard_map/all_to_all | solution.py:462
  136.0 1.0 copy.24
Async XLA Ops:
  8.3 12.7 %copy-start.2 = (bf16[512,256]{1,0:T(8,128)(2,1)S(1)}, bf16[512,256]{1,0:T(8,128)(2,1)}, u32[]{:S(2)}) copy-start(bf16[512,256]{1,0:T(8,128)(2,1)} %get-tuple-element.16.fresh) | copy-start | bytes 786436
  8.3 62.6 %all-to-all-start = ((bf16[64,32,256]{2,1,0:T(8,128)(2,1)}), bf16[64,32,256]{2,1,0:T(8,128)(2,1)S(1)}, u32[]{:S(2)}, u32[]{:S(2)}) async-start(bf16[64,32,256]{2,1,0:T(8,128)(2,1)} %bitcast.12), calls=%async_computation | async-start | bytes 2097152 | tf_op jit(solution)/shard_map/all_to_all | solution.py:330
  21.0 22.7 %collective-permute-start = (bf16[512,256]{1,0:T(8,128)(2,1)S(1)}, bf16[512,256]{1,0:T(8,128)(2,1)S(1)}, u32[]{:S(2)}, u32[]{:S(2)}) collective-permute-start(bf16[512,256]{1,0:T(8,128)(2,1)S(1)} %copy-done.2), channel_id=1, source_target_pairs={{0,1},{1,3},{3,2},{2,0},{4,5},{5,7},{7,6},{6,4},{8,9},{9,11},{11,1... | collective-permute-start | bytes 786440 | tf_op jit(solution)/shard_map/ppermute | solution.py:328
  43.7 5.7 %copy-start.3 = (bf16[512,256]{1,0:T(8,128)(2,1)}, bf16[512,256]{1,0:T(8,128)(2,1)S(1)}, u32[]{:S(2)}) copy-start(bf16[512,256]{1,0:T(8,128)(2,1)S(1)} %collective-permute-done.via_ring) | copy-start | bytes 786436
  43.7 11.6 %collective-permute-start.1 = (bf16[512,256]{1,0:T(8,128)(2,1)S(1)}, bf16[512,256]{1,0:T(8,128)(2,1)S(1)}, u32[]{:S(2)}, u32[]{:S(2)}) collective-permute-start(bf16[512,256]{1,0:T(8,128)(2,1)S(1)} %collective-permute-done.via_ring), channel_id=1, source_target_pairs={{0,1},{3,2},{4,5},{7,6},{8,9},{11,10},{12,13},{15,14},{16,17},{19,... | collective-permute-start | bytes 786440 | tf_op jit(solution)/shard_map/ppermute | solution.py:329
  55.2 0.7 copy-start.4
  61.7 7.2 %collective-permute-start.3 = (bf16[128,2048]{1,0:T(8,128)(2,1)}, bf16[128,2048]{1,0:T(8,128)(2,1)S(1)}, u32[]{:S(2)}, u32[]{:S(2)}) collective-permute-start(bf16[128,2048]{1,0:T(8,128)(2,1)} %get-tuple-element.22), channel_id=1, source_target_pairs={{0,1},{1,0},{2,3},{3,2},{4,5},{5,4},{6,7},{7,6},{8,9},{9,8},{10,11... | collective-permute-start | bytes 1572872 | tf_op jit(solution)/shard_map/ppermute | solution.py:401
  70.9 1.0 copy-start
  74.8 61.2 %all-to-all-start.1 = ((bf16[64,32,256]{2,1,0:T(8,128)(2,1)}), bf16[64,32,256]{2,1,0:T(8,128)(2,1)S(1)}, u32[]{:S(2)}, u32[]{:S(2)}) async-start(bf16[64,32,256]{2,1,0:T(8,128)(2,1)} %permute.1), calls=%async_computation.1 | async-start | bytes 2097152 | tf_op jit(solution)/shard_map/all_to_all | solution.py:462
  85.0 9.2 %copy-start.1 = (bf16[128,2048]{1,0:T(8,128)(2,1)S(1)}, bf16[128,2048]{1,0:T(8,128)(2,1)}, u32[]{:S(2)}) copy-start(bf16[128,2048]{1,0:T(8,128)(2,1)} %add_convert_fusion.after) | copy-start | bytes 1572868
  93.4 2.5 %collective-permute-start.2 = (bf16[128,2048]{1,0:T(8,128)(2,1)}, bf16[128,2048]{1,0:T(8,128)(2,1)S(1)}, u32[]{:S(2)}, u32[]{:S(2)}) collective-permute-start(bf16[128,2048]{1,0:T(8,128)(2,1)} %get-tuple-element.18), channel_id=1, source_target_pairs={{0,1},{1,0},{2,3},{3,2},{4,5},{5,4},{6,7},{7,6},{8,9},{9,8},{10,11... | collective-permute-start | bytes 1572872 | tf_op jit(solution)/shard_map/ppermute | solution.py:420
  94.2 31.5 %collective-permute-start.4 = (bf16[128,2048]{1,0:T(8,128)(2,1)S(1)}, bf16[128,2048]{1,0:T(8,128)(2,1)S(1)}, u32[]{:S(2)}, u32[]{:S(2)}) collective-permute-start(bf16[128,2048]{1,0:T(8,128)(2,1)S(1)} %copy-done.1), channel_id=1, source_target_pairs={{0,2},{1,3},{2,0},{3,1},{4,6},{5,7},{6,4},{7,5},{8,10},{9,11},{10,... | collective-permute-start | bytes 1572872 | tf_op jit(solution)/shard_map/ppermute | solution.py:403
  95.9 29.8 %copy-start.5 = (bf16[128,2048]{1,0:T(8,128)(2,1)}, bf16[128,2048]{1,0:T(8,128)(2,1)S(1)}, u32[]{:S(2)}) copy-start(bf16[128,2048]{1,0:T(8,128)(2,1)S(1)} %collective-permute-done.2.partner) | copy-start | bytes 1572868
  125.7 0.8 copy-start.6

commit v7 on v6

--- a/solution.py
+++ b/solution.py
@@ -38,7 +38,7 @@
 
 def prep_kernel(
     table, prefix_len, head_at, hidden, in_gain, w_kv, k_gain, frequency, pool,
-    normed, fresh, seq, cosine, sine, sem, *, n_pages, page, kv_heads,
+    normed, fresh, seq, cosine, sine, weights, sem, *, n_pages, page, kv_heads,
 ):
     step = pl.program_id(0)
     head = head_at[0]
@@ -52,14 +52,22 @@
             pool.at[table[p], head], seq.at[pl.ds(p * page, page)], sem.at[p]
         )
 
+    fetch = pltpu.make_async_copy(w_kv, weights, sem.at[n_pages])
+
     @pl.when(step == 0)
     def _():
+        fetch.start()
         for p in range(n_pages):
             page_copy(p).start()
 
     values = (rms_scale(hidden[...].astype(F32)) * in_gain[...]).astype(BF16)
     normed[...] = values
-    own = rms_scale(dot(values, w_kv[...]))
+
+    @pl.when(step == 0)
+    def _():
+        fetch.wait()
+
+    own = rms_scale(dot(values, weights[...]))
     fine = 16
     at = lax.broadcasted_iota(jnp.int32, (tile // fine, 1), 0)
     coarse_angle = (length + step * tile + at * fine).astype(F32) * frequency[...]
@@ -144,7 +152,7 @@
     copies = old_copies(table, pool, keys, vals, sem, kv_of, kv_heads, n_pages, page)
     for copy in copies:
         copy.start()
-    for copy in copies:
+    for copy in copies[:n_pages]:
         copy.wait()
     live = lax.broadcasted_iota(jnp.int32, (1, prefix), 1) < length
     for h in range(heads):
@@ -153,6 +161,9 @@
         top = jnp.max(scores, axis=1, keepdims=True)
         expo = jnp.exp(scores - top)
         total = jnp.sum(expo, axis=1, keepdims=True)
+        if h == 0:
+            for copy in copies[n_pages:]:
+                copy.wait()
         acc[h] = dot(expo.astype(BF16), vals[...])
         half = stat.shape[2] // 2
         stat[h, :, :half] = jnp.broadcast_to(top, (2 * tile, half))
@@ -161,12 +172,14 @@
 
 def attend_new_kernel(
     head_at, send_q, mine_q, acc, stat, w_out, fresh, via_ring, via_both,
-    send, mine, keys, vals, sem,
+    send, mine, keys, vals, weights, sem,
 ):
     head = head_at[0]
+    fetch = pltpu.make_async_copy(w_out, weights, sem.at[2])
     heads, tile, _ = send_q.shape
     rows = fresh.shape[0]
     new_copies(head, fresh, via_ring, via_both, keys, vals, sem.at[0], sem.at[1])
+    fetch.start()
     col = lax.broadcasted_iota(jnp.int32, (1, rows), 1)
     row = lax.broadcasted_iota(jnp.int32, (tile, 1), 0)
     token = jnp.concatenate([quarter_of(False, i, head) * tile + row for i in range(2)], axis=0)
@@ -182,7 +195,8 @@
         total = stat[h, :, half : half + 1] * fade + jnp.sum(expo, axis=1, keepdims=True)
         value = acc[h] * fade + dot(expo.astype(BF16), vals[...])
         attns.append((value / total).astype(BF16))
-    part = dot(jnp.concatenate(attns, axis=1), w_out[...]).astype(BF16)
+    fetch.wait()
+    part = dot(jnp.concatenate(attns, axis=1), weights[...]).astype(BF16)
     send[...] = part[:tile]
     mine[...] = part[tile:]
 
@@ -296,7 +310,7 @@
             in_specs=[
                 pl.BlockSpec((tile, width), lambda i, *_: (i, 0)),
                 whole((1, width)),
-                whole((width, dim)),
+                pl.BlockSpec(memory_space=ANY),
                 whole((1, dim)),
                 whole((1, half)),
                 pl.BlockSpec(memory_space=ANY),
@@ -309,7 +323,8 @@
                 pl.BlockSpec((tile, half), lambda i, *_: (i, 0)),
             ],
             scratch_shapes=[
-                pltpu.SemaphoreType.DMA((n_pages,)),
+                pltpu.VMEM((width, dim), BF16),
+                pltpu.SemaphoreType.DMA((n_pages + 1,)),
             ],
         ),
         out_shape=[
@@ -383,13 +398,14 @@
             num_scalar_prefetch=1,
             grid=(1,),
             in_specs=query_specs(False)
-            + [whole(state), whole(state), whole(w_out.shape)]
-            + [hbm] * 3,
+            + [whole(state), whole(state)]
+            + [hbm] * 4,
             out_specs=[whole((quarter, width))] * 2,
             scratch_shapes=[
                 pltpu.VMEM((rows, dim), BF16),
                 pltpu.VMEM((rows, dim), BF16),
-                pltpu.SemaphoreType.DMA((2,)),
+                pltpu.VMEM(w_out.shape, BF16),
+                pltpu.SemaphoreType.DMA((3,)),
             ],
         ),
         out_shape=parts,

time: 138 us -> 138 us (level)
  no operation moved by 1% of the time
where the time goes in v7:
time: 138 us; the launch traced here: 137 us
  waiting for transfers between devices  54.9 us (40%)
  Pallas kernels  39.7 us (29%)
  starting transfers between devices  35.6 us (26%)
  local copies, waits for them, and re-layouts  3.45 us (2%)
  other arithmetic  1.97 us (1%)
  between operations  1.39 us (1%)
    ppermute x1, waiting for transfers between devices, on_device(): far = lax.ppermute(pair_sum, AXES, chip_pairs)  29.8 us
    ppermute x1, waiting for transfers between devices, on_device(): lax.ppermute(fresh, AXES, pairs(((0, 1), (1, 3), (3, 2), (2, 0))))  18.4 us
    all_to_all x1, starting transfers between devices, on_device(): lax.all_to_all(full_seq.reshape(blocks, total_len // blocks, dim), 'blk',...  12.7 us
    all_to_all x1, starting transfers between devices, on_device(): owned = lax.all_to_all(arranged, 'blk', 0, 0, tiled=True)  10.4 us
    pallas_call x1, Pallas kernels, on_device(): pl.pallas_call(functools.partial(attend_kernel, **sizes), grid_spec=pltpu...  8.4 us
    pallas_call x1, Pallas kernels, on_device(): pl.pallas_call(functools.partial(prep_kernel, n_pages=n_pages, page=page,...  6.87 us
    ppermute x2, starting transfers between devices, on_device(): partner = lax.ppermute(send, AXES, core_pairs)  6.18 us
    pallas_call x1, Pallas kernels, on_device(): pl.pallas_call(functools.partial(attend_old_kernel, **sizes), grid_spec=p...  6.03 us
  transfers between devices with their start and end apart: 7, of which 5 were waited for; matrix products, arithmetic and copies ran while one was open for 1% of the time, Pallas kernels for 22%

profile of v7, /device:TPU:1, one launch (start us, length us, event | category | flops | bytes accessed | tf_op | source)
XLA Modules:
  0.0 137.0 jit_solution(6405535673362618441)
XLA Ops:
  1.3 6.9 %prep.1 = (bf16[512,2048]{1,0:T(8,128)(2,1)}, bf16[512,256]{1,0:T(8,128)(2,1)}, bf16[2048,256]{1,0:T(8,128)(2,1)}, f32[512,128]{1,0:T(8,128)}, f32[512,128]{1,0:T(8,128)}) custom-call(s32[12]{0:T(128)} %bitcast.18, s32[1]{0:T(128)S(6)} %copy.23.prefix_len, s32[1]{0:T(128)} %bitcast.head_at, bf16[512,2048]{1,0:T(8,128)(2,1)} %hidden.3, f32[1,2048]{1,0:T(1,128)} %bitcast.14, ...), custom_call_target="tpu_custom_call" | custom-call | tf_op jit(solution)/shard_map/prep/pallas_call | solution.py:303
  8.2 0.0 copy-start.2
  8.2 12.7 %all-to-all-start = ((bf16[64,32,256]{2,1,0:T(8,128)(2,1)}), bf16[64,32,256]{2,1,0:T(8,128)(2,1)S(1)}, u32[]{:S(2)}, u32[]{:S(2)}) async-start(bf16[64,32,256]{2,1,0:T(8,128)(2,1)} %bitcast.12), calls=%async_computation | async-start | bytes 2097152 | tf_op jit(solution)/shard_map/all_to_all | solution.py:345
  20.9 0.0 copy-done.2
  20.9 4.3 %collective-permute-start = (bf16[512,256]{1,0:T(8,128)(2,1)S(1)}, bf16[512,256]{1,0:T(8,128)(2,1)S(1)}, u32[]{:S(2)}, u32[]{:S(2)}) collective-permute-start(bf16[512,256]{1,0:T(8,128)(2,1)S(1)} %copy-done.2), channel_id=1, source_target_pairs={{0,1},{1,3},{3,2},{2,0},{4,5},{5,7},{7,6},{6,4},{8,9},{9,11},{11,1... | collective-permute-start | bytes 786440 | tf_op jit(solution)/shard_map/ppermute | solution.py:343
  25.2 18.4 %collective-permute-done.via_ring = bf16[512,256]{1,0:T(8,128)(2,1)S(1)} collective-permute-done((bf16[512,256]{1,0:T(8,128)(2,1)S(1)}, bf16[512,256]{1,0:T(8,128)(2,1)S(1)}, u32[]{:S(2)}, u32[]{:S(2)}) %collective-permute-start) | collective-permute-done | bytes 262176 | tf_op jit(solution)/shard_map/ppermute | solution.py:343
  43.6 0.0 copy-start.3
  43.6 1.3 collective-permute-start.1
  44.8 4.4 %query.1.send_q.mine_q = bf16[2,512,256]{2,1,0:T(8,128)(2,1)} custom-call(bf16[512,2048]{1,0:T(8,128)(2,1)} %get-tuple-element.13.normed, bf16[2048,512]{1,0:T(8,128)(2,1)} %w_q.1, f32[1,256]{1,0:T(1,128)} %bitcast.22, f32[512,128]{1,0:T(8,128)} %get-tuple-element.14.cosine, f32[512,128]{1,0:T(8,128)} %get-tuple-element.15.sine), custom_call_target="tpu_custom_call" | custom-call | tf_op jit(solution)/shard_map/query/pallas_call | solution.py:349
  49.3 0.0 copy-done.3
  49.3 6.0 %attend_old.1 = (f32[2,256,256]{2,1,0:T(8,128)}, f32[2,256,256]{2,1,0:T(8,128)}) custom-call(s32[12]{0:T(128)} %bitcast.19, s32[1]{0:T(128)S(6)} %copy.23.prefix_len, s32[1]{0:T(128)} %bitcast.head_at, bf16[2,512,256]{2,1,0:T(8,128)(2,1)} %query.1.send_q.mine_q, bf16[2,512,256]{2,1,0:T(8,128)(2,1)} %query.1.send_q.mine_q, bf16[12,4,128,256]{3,2,1,0:T(8,128)(2,1)} %pool.5), custom_call_target="tpu_custom_call" | custom-call | tf_op jit(solution)/shard_map/attend_old/pallas_call | solution.py:378
  55.3 0.0 collective-permute-done.1.via_both
  55.3 0.0 copy-start.4
  55.3 0.7 copy-done.4
  56.0 5.7 %attend_new.1 = (bf16[128,2048]{1,0:T(8,128)(2,1)}, bf16[128,2048]{1,0:T(8,128)(2,1)}) custom-call(s32[1]{0:T(128)} %bitcast.head_at, bf16[2,512,256]{2,1,0:T(8,128)(2,1)} %query.1.send_q.mine_q, bf16[2,512,256]{2,1,0:T(8,128)(2,1)} %query.1.send_q.mine_q, f32[2,256,256]{2,1,0:T(8,128)} %get-tuple-element.19.acc, f32[2,256,256]{2,1,0:T(8,128)} %get-tuple-element.20.stat, ...), custom_call_target="tpu_custom_call" | custom-call | tf_op jit(solution)/shard_map/attend_new/pallas_call | solution.py:395
  61.7 5.4 %collective-permute-start.3 = (bf16[128,2048]{1,0:T(8,128)(2,1)}, bf16[128,2048]{1,0:T(8,128)(2,1)S(1)}, u32[]{:S(2)}, u32[]{:S(2)}) collective-permute-start(bf16[128,2048]{1,0:T(8,128)(2,1)} %get-tuple-element.22), channel_id=1, source_target_pairs={{0,1},{1,0},{2,3},{3,2},{4,5},{5,4},{6,7},{7,6},{8,9},{9,8},{10,11... | collective-permute-start | bytes 1572872 | tf_op jit(solution)/shard_map/ppermute | solution.py:417
  67.1 1.7 %collective-permute-done.3 = bf16[128,2048]{1,0:T(8,128)(2,1)S(1)} collective-permute-done((bf16[128,2048]{1,0:T(8,128)(2,1)}, bf16[128,2048]{1,0:T(8,128)(2,1)S(1)}, u32[]{:S(2)}, u32[]{:S(2)}) %collective-permute-start.3) | collective-permute-done | bytes 524320 | tf_op jit(solution)/shard_map/ppermute | solution.py:417
  68.9 2.0 %add_convert_fusion.after = bf16[128,2048]{1,0:T(8,128)(2,1)} fusion(bf16[128,2048]{1,0:T(8,128)(2,1)S(1)} %collective-permute-done.3, bf16[128,2048]{1,0:T(8,128)(2,1)} %get-tuple-element.21), kind=kLoop, calls=%fused_computation | loop fusion | flops 1048576 | bytes 1572864 | tf_op jit(solution)/shard_map/convert_element_type | solution.py:418
  70.9 0.0 all-to-all-done.spread
  70.9 0.0 copy-start
  70.9 1.0 copy-done
  71.8 3.0 %permute.1 = bf16[64,32,256]{2,1,0:T(8,128)(2,1)} custom-call(s32[64]{0:T(128)} %owner.1, bf16[64,32,256]{2,1,0:T(8,128)(2,1)} %copy-done, bf16[128,2048]{1,0:T(8,128)(2,1)} %add_convert_fusion.after), custom_call_target="tpu_custom_call" | custom-call | tf_op jit(solution)/shard_map/permute/pallas_call | solution.py:467
  74.8 10.4 %all-to-all-start.1 = ((bf16[64,32,256]{2,1,0:T(8,128)(2,1)}), bf16[64,32,256]{2,1,0:T(8,128)(2,1)S(1)}, u32[]{:S(2)}, u32[]{:S(2)}) async-start(bf16[64,32,256]{2,1,0:T(8,128)(2,1)} %permute.1), calls=%async_computation.1 | async-start | bytes 2097152 | tf_op jit(solution)/shard_map/all_to_all | solution.py:478
  85.2 0.0 copy-start.1
  85.2 8.4 %attend_own.1 = (bf16[128,2048]{1,0:T(8,128)(2,1)}, bf16[128,2048]{1,0:T(8,128)(2,1)}) custom-call(s32[12]{0:T(128)} %bitcast.20, s32[1]{0:T(128)S(6)} %copy.23.prefix_len, s32[1]{0:T(128)} %bitcast.head_at, bf16[2,512,256]{2,1,0:T(8,128)(2,1)} %query.1.send_q.mine_q, bf16[2,512,256]{2,1,0:T(8,128)(2,1)} %query.1.send_q.mine_q, bf16[512,2048]{1,0:T(8,128)(2,1)} %w_out.3, ...), custom_call_target="tpu_custom_call" | custom-call | tf_op jit(solution)/shard_map/attend_own/pallas_call | solution.py:420
  93.6 0.7 collective-permute-start.2
  94.4 0.0 copy-done.1
  94.4 0.7 collective-permute-start.4
  95.1 1.0 collective-permute-done.2.partner
  96.1 0.0 copy-start.5
  96.1 29.8 %collective-permute-done.4.far = bf16[128,2048]{1,0:T(8,128)(2,1)S(1)} collective-permute-done((bf16[128,2048]{1,0:T(8,128)(2,1)S(1)}, bf16[128,2048]{1,0:T(8,128)(2,1)S(1)}, u32[]{:S(2)}, u32[]{:S(2)}) %collective-permute-start.4) | collective-permute-done | bytes 524320 | tf_op jit(solution)/shard_map/ppermute | solution.py:419
  125.9 0.0 copy-start.6
  125.9 0.0 copy-done.5
  125.9 0.8 copy-done.6
  126.7 5.4 %post.1 = bf16[128,2048]{1,0:T(8,128)(2,1)} custom-call(s32[1]{0:T(128)} %bitcast.head_at, bf16[512,2048]{1,0:T(8,128)(2,1)} %hidden.3, bf16[512,2048]{1,0:T(8,128)(2,1)} %get-tuple-element.13.normed, bf16[128,2048]{1,0:T(8,128)(2,1)} %get-tuple-element.17.mine, bf16[128,2048]{1,0:T(8,128)(2,1)} %copy-done.5, bf16[128,2048]{1,0:T(8,128)(2,1)} %copy-done.6, ...), custom_call_target="tpu_custom_call" | custom-call | tf_op jit(solution)/shard_map/post/pallas_call | solution.py:438
  132.0 4.0 %all-to-all-done.1 = bf16[64,32,256]{2,1,0:T(8,128)(2,1)S(1)} async-done(((bf16[64,32,256]{2,1,0:T(8,128)(2,1)}), bf16[64,32,256]{2,1,0:T(8,128)(2,1)S(1)}, u32[]{:S(2)}, u32[]{:S(2)}) %all-to-all-start.1) | async-done | bytes 1048608 | tf_op jit(solution)/shard_map/all_to_all | solution.py:478
  136.0 1.0 copy.24
Async XLA Ops:
  8.2 12.7 %copy-start.2 = (bf16[512,256]{1,0:T(8,128)(2,1)S(1)}, bf16[512,256]{1,0:T(8,128)(2,1)}, u32[]{:S(2)}) copy-start(bf16[512,256]{1,0:T(8,128)(2,1)} %get-tuple-element.16.fresh) | copy-start | bytes 786436
  8.2 62.7 %all-to-all-start = ((bf16[64,32,256]{2,1,0:T(8,128)(2,1)}), bf16[64,32,256]{2,1,0:T(8,128)(2,1)S(1)}, u32[]{:S(2)}, u32[]{:S(2)}) async-start(bf16[64,32,256]{2,1,0:T(8,128)(2,1)} %bitcast.12), calls=%async_computation | async-start | bytes 2097152 | tf_op jit(solution)/shard_map/all_to_all | solution.py:345
  20.9 22.7 %collective-permute-start = (bf16[512,256]{1,0:T(8,128)(2,1)S(1)}, bf16[512,256]{1,0:T(8,128)(2,1)S(1)}, u32[]{:S(2)}, u32[]{:S(2)}) collective-permute-start(bf16[512,256]{1,0:T(8,128)(2,1)S(1)} %copy-done.2), channel_id=1, source_target_pairs={{0,1},{1,3},{3,2},{2,0},{4,5},{5,7},{7,6},{6,4},{8,9},{9,11},{11,1... | collective-permute-start | bytes 786440 | tf_op jit(solution)/shard_map/ppermute | solution.py:343
  43.6 5.7 %copy-start.3 = (bf16[512,256]{1,0:T(8,128)(2,1)}, bf16[512,256]{1,0:T(8,128)(2,1)S(1)}, u32[]{:S(2)}) copy-start(bf16[512,256]{1,0:T(8,128)(2,1)S(1)} %collective-permute-done.via_ring) | copy-start | bytes 786436
  43.6 11.7 %collective-permute-start.1 = (bf16[512,256]{1,0:T(8,128)(2,1)S(1)}, bf16[512,256]{1,0:T(8,128)(2,1)S(1)}, u32[]{:S(2)}, u32[]{:S(2)}) collective-permute-start(bf16[512,256]{1,0:T(8,128)(2,1)S(1)} %collective-permute-done.via_ring), channel_id=1, source_target_pairs={{0,1},{3,2},{4,5},{7,6},{8,9},{11,10},{12,13},{15,14},{16,17},{19,... | collective-permute-start | bytes 786440 | tf_op jit(solution)/shard_map/ppermute | solution.py:344
  55.3 0.7 copy-start.4
  61.7 7.2 %collective-permute-start.3 = (bf16[128,2048]{1,0:T(8,128)(2,1)}, bf16[128,2048]{1,0:T(8,128)(2,1)S(1)}, u32[]{:S(2)}, u32[]{:S(2)}) collective-permute-start(bf16[128,2048]{1,0:T(8,128)(2,1)} %get-tuple-element.22), channel_id=1, source_target_pairs={{0,1},{1,0},{2,3},{3,2},{4,5},{5,4},{6,7},{7,6},{8,9},{9,8},{10,11... | collective-permute-start | bytes 1572872 | tf_op jit(solution)/shard_map/ppermute | solution.py:417
  70.9 1.0 copy-start
  74.8 61.2 %all-to-all-start.1 = ((bf16[64,32,256]{2,1,0:T(8,128)(2,1)}), bf16[64,32,256]{2,1,0:T(8,128)(2,1)S(1)}, u32[]{:S(2)}, u32[]{:S(2)}) async-start(bf16[64,32,256]{2,1,0:T(8,128)(2,1)} %permute.1), calls=%async_computation.1 | async-start | bytes 2097152 | tf_op jit(solution)/shard_map/all_to_all | solution.py:478
  85.2 9.2 %copy-start.1 = (bf16[128,2048]{1,0:T(8,128)(2,1)S(1)}, bf16[128,2048]{1,0:T(8,128)(2,1)}, u32[]{:S(2)}) copy-start(bf16[128,2048]{1,0:T(8,128)(2,1)} %add_convert_fusion.after) | copy-start | bytes 1572868
  93.6 2.5 %collective-permute-start.2 = (bf16[128,2048]{1,0:T(8,128)(2,1)}, bf16[128,2048]{1,0:T(8,128)(2,1)S(1)}, u32[]{:S(2)}, u32[]{:S(2)}) collective-permute-start(bf16[128,2048]{1,0:T(8,128)(2,1)} %get-tuple-element.18), channel_id=1, source_target_pairs={{0,1},{1,0},{2,3},{3,2},{4,5},{5,4},{6,7},{7,6},{8,9},{9,8},{10,11... | collective-permute-start | bytes 1572872 | tf_op jit(solution)/shard_map/ppermute | solution.py:436
  94.4 31.5 %collective-permute-start.4 = (bf16[128,2048]{1,0:T(8,128)(2,1)S(1)}, bf16[128,2048]{1,0:T(8,128)(2,1)S(1)}, u32[]{:S(2)}, u32[]{:S(2)}) collective-permute-start(bf16[128,2048]{1,0:T(8,128)(2,1)S(1)} %copy-done.1), channel_id=1, source_target_pairs={{0,2},{1,3},{2,0},{3,1},{4,6},{5,7},{6,4},{7,5},{8,10},{9,11},{10,... | collective-permute-start | bytes 1572872 | tf_op jit(solution)/shard_map/ppermute | solution.py:419
  96.1 29.8 %copy-start.5 = (bf16[128,2048]{1,0:T(8,128)(2,1)}, bf16[128,2048]{1,0:T(8,128)(2,1)S(1)}, u32[]{:S(2)}) copy-start(bf16[128,2048]{1,0:T(8,128)(2,1)S(1)} %collective-permute-done.2.partner) | copy-start | bytes 1572868
  125.9 0.8 copy-start.6
